TPU v7x, 32 devices: a whole 2x2x4 slice. The times are simulated.
32 devices in a mesh: dp: 8 (over z, y), rep: 4 (over x, core).
Axes of the slice: x: 2, y: 2, z: 4, core: 2. Of those that a mesh axis runs over, the one named last changes fastest.
Arguments:
- x_in: bfloat16 [16384, 768], P(('dp', 'rep')), may hold values from -6 to 6
- seq_lens: int32 [32, 3], P(('dp', 'rep')), may hold values from 1 to 384, 512 in all within a row
- routes: int32 [16384, 2], P(('dp', 'rep')), may hold values from 0 to 11, all different within a row; in each aligned block of 512 rows (0 to 511, 512 to 1023, ...) at most 128 rows name the same one
- positions: int32 [4096], P(('dp', 'rep')), may hold values from 0 to 511, as said below
- targets: int32 [4, 8, 128], P('rep'), may hold values from 0 to 65535
- dense_w: float32 [768, 3072], P(None, ('dp', 'rep')), may hold values from -0.3125 to 0.3125
- small_w: float32 [21, 768], P(None, ('dp', 'rep'))
- expert_in: float32 [2, 768, 16384], P(None, 'rep', 'dp'), may hold values from -0.21875 to 0.21875
- expert_out: float32 [16384, 768], P(('dp', 'rep')), may hold values from -0.75 to 0.75
- table: float32 [65536, 768], P(('dp', 'rep')), may hold values from -0.4375 to 0.4375
- dense_m: float32 [768, 3072], P(None, ('dp', 'rep')), may hold values from -0.21875 to 0.21875
- small_m: float32 [21, 768], P(None, ('dp', 'rep')), may hold values from -0.21875 to 0.21875
- expin_m: float32 [2, 768, 16384], P(None, 'rep', 'dp'), may hold values from -0.0546875 to 0.0546875
- expout_m: float32 [16384, 768], P(('dp', 'rep')), may hold values from -0.0068359375 to 0.0068359375
- table_m: float32 [65536, 768], P(('dp', 'rep')), may hold values from -0.00036621094 to 0.00036621094
- dense_v: float32 [768, 3072], P(None, ('dp', 'rep')), may hold values from 0.0013020834 to 0.0052083335
- small_v: float32 [21, 768], P(None, ('dp', 'rep')), may hold values from 0.0013020834 to 0.0052083335
- expin_v: float32 [2, 768, 16384], P(None, 'rep', 'dp'), may hold values from 3.2958986e-05 to 0.00013061524
- expout_v: float32 [16384, 768], P(('dp', 'rep')), may hold values from 3.2552084e-06 to 1.3020834e-05
- table_v: float32 [65536, 768], P(('dp', 'rep')), may hold values from 3.2014214e-09 to 1.2805685e-08
Outputs:
- loss: float32 [], replicated
- lamb_norms: float32 [3, 7], replicated
- dense_m_new: float32 [768, 3072], P(None, ('dp', 'rep'))
- dense_v_new: float32 [768, 3072], P(None, ('dp', 'rep'))
- dense_w_new: float32 [768, 3072], P(None, ('dp', 'rep'))
- dense_w_low: bfloat16 [768, 3072], P(None, ('dp', 'rep'))
- small_m_new: float32 [21, 768], P(None, ('dp', 'rep'))
- small_v_new: float32 [21, 768], P(None, ('dp', 'rep'))
- small_w_new: float32 [21, 768], P(None, ('dp', 'rep'))
- small_w_low: bfloat16 [21, 768], P(None, ('dp', 'rep'))
- expin_m_new: float32 [2, 768, 16384], P(None, 'rep', 'dp')
- expin_v_new: float32 [2, 768, 16384], P(None, 'rep', 'dp')
- expin_w_new: float32 [2, 768, 16384], P(None, 'rep', 'dp')
- expin_w_low: bfloat16 [2, 768, 16384], P(None, 'rep', 'dp')
- expout_m_new: float32 [16384, 768], P(('dp', 'rep'))
- expout_v_new: float32 [16384, 768], P(('dp', 'rep'))
- expout_w_new: float32 [16384, 768], P(('dp', 'rep'))
- expout_w_low: bfloat16 [16384, 768], P(('dp', 'rep'))
- table_m_new: float32 [65536, 768], P(('dp', 'rep'))
- table_v_new: float32 [65536, 768], P(('dp', 'rep'))
- table_w_new: float32 [65536, 768], P(('dp', 'rep'))
- table_w_low: bfloat16 [65536, 768], P(('dp', 'rep'))
Inputs may be any that keep to these rules, and one draw needn't show every extreme that they name: `seq_lens`: each row sums to 512; the longest sequence is exactly 384. `routes`: the two experts of a token differ. No expert is named by more than 128 rows of one device; some device has an expert named by exactly 128 rows. The 128 positions of one device are distinct.
All inputs are finite; a program needn't handle non-finite values.
Results may differ from a plain program's by a relative error of at most 0.018.
Values may be sent and summed in bfloat16 or wider, within the bound.
No kernel may reach another device: no remote copies, remote signals or barrier semaphores. Data moves between devices by JAX's collectives and lax.ppermute only.
A program may use at most 256 MiB of HBM per device.

v0:
```python
import jax
import jax.numpy as jnp
from jax import lax
from jax.sharding import PartitionSpec as P

D = 768
HDIM = 64
EXPERTS = 8
NULLS = 4
STEP = 5
CAP = 96


EPS = 1e-06
HIGH = lax.Precision.HIGHEST
LOWER = jnp.bfloat16
WIDE = jnp.float32


def merged(value, axis, join):
    pieces = jax.tree.map(lambda part: lax.all_gather(part, axis), value)
    head = jax.tree.map(lambda part: part[0], pieces)
    tail = jax.tree.map(lambda part: part[1:], pieces)
    subtotal, _ = lax.scan(lambda subtotal, slab: (join(subtotal, slab), None), head, tail)
    return subtotal


def contract_rows(left, right):
    return lax.dot_general(left, right, (((0,), (0,)), ((), ())), preferred_element_type=WIDE)


def contract_cols(left, right):
    return lax.dot_general(left, right, (((1,), (1,)), ((), ())), preferred_element_type=WIDE)


def rows_high(left, right):
    return lax.dot_general(left, right, (((0,), (0,)), ((), ())), precision=HIGH)


def norm_fwd(hidden, gain):
    scale = lax.rsqrt(jnp.mean(hidden * hidden, -1, keepdims=True) + EPS)
    return (hidden * scale * gain, scale)


def norm_back(hidden, scale, gain, grad_out):
    normed = hidden * scale
    grad_gain = jnp.sum(grad_out * normed, 0)
    inner = grad_out * gain
    grad_in = scale * (inner - normed * jnp.mean(inner * normed, -1, keepdims=True))
    return (grad_in, grad_gain)


def seq_mask(lens, tokens):
    place = jnp.arange(tokens, dtype=jnp.int32)
    ends = jnp.cumsum(lens)
    segment = jnp.sum((place[:, None] >= ends[None, :]).astype(jnp.int32), 1)
    return (segment[:, None] == segment[None, :]) & (place[None, :] <= place[:, None])


def split_heads(qkv, which):
    return qkv[:, which * D : (which + 1) * D].reshape(qkv.shape[0], -1, HDIM)


def head_scores(qkv, mask):
    scores = jnp.einsum(
        "qhd,khd->hqk", split_heads(qkv, 0), split_heads(qkv, 1), preferred_element_type=WIDE
    )
    return jnp.where(mask[None], scores * HDIM ** (-0.5), -1e30)


def merge_rows(first, second):
    top = jnp.maximum(first[0], second[0])
    total = first[1] * jnp.exp(first[0] - top) + second[1] * jnp.exp(second[0] - top)
    return (top, total, first[2] + second[2])


def fan_out(buffer, shards):
    return jnp.broadcast_to(buffer[:, None], (EXPERTS, shards) + buffer.shape[1:]).reshape(
        (EXPERTS * shards,) + buffer.shape[1:]
    )


def fan_in(received, shards):
    return jnp.sum(received.astype(WIDE).reshape((EXPERTS, shards) + received.shape[1:]), 1)


def split_small(small_all):
    return (
        small_all[:3].astype(WIDE),
        small_all[3:5].astype(WIDE),
        small_all[5:17],
        small_all[17:21],
    )


def layer_forward(hidden, lens, routes, dense_all, small_all, w_in, w_out, shards):
    gains, const_vec, router, const_gate = split_small(small_all)
    tokens = hidden.shape[0]
    mask = seq_mask(lens, tokens)
    normed, scale_one = norm_fwd(hidden, gains[0])
    normed_low = normed.astype(LOWER)
    qkv = jnp.dot(normed_low, dense_all[:, : 3 * D], preferred_element_type=WIDE).astype(LOWER)
    scores = head_scores(qkv, mask)
    top = jnp.max(scores, -1, keepdims=True)
    expo = jnp.exp(scores - top)
    total = jnp.sum(expo, -1, keepdims=True)
    probs = (expo / total).astype(LOWER)
    mixed = jnp.einsum("hqk,khd->qhd", probs, split_heads(qkv, 2), preferred_element_type=WIDE)
    mixed = mixed.reshape(tokens, D).astype(LOWER)
    first = hidden + jnp.dot(mixed, dense_all[:, 3 * D :], preferred_element_type=WIDE)
    second, scale_two = norm_fwd(first, gains[1])
    second_low = second.astype(LOWER)
    route_p = jax.nn.softmax(contract_cols(second_low, router), -1)
    used = jnp.sum(
        (routes[:, :, None] == jnp.arange(EXPERTS + NULLS, dtype=jnp.int32)[None, None, :]).astype(
            WIDE
        ),
        1,
    )
    weight = route_p * used
    real = used[:, :EXPERTS]
    rank = jnp.cumsum(real, 0) - real
    slots = (rank.T[:, None, :] == jnp.arange(CAP, dtype=WIDE)[None, :, None]).astype(
        WIDE
    ) * real.T[:, None, :]
    buffer = jnp.einsum(
        "ect,td->ecd", slots.astype(LOWER), second_low, preferred_element_type=WIDE
    ).astype(LOWER)
    received = lax.all_to_all(
        fan_out(buffer, shards), "dp", split_axis=0, concat_axis=0, tiled=True
    )
    rows = received.reshape(-1, D)
    gate_pre = jnp.dot(rows, w_in[0], preferred_element_type=WIDE)
    up_pre = jnp.dot(rows, w_in[1], preferred_element_type=WIDE)
    inner = (jax.nn.silu(gate_pre) * up_pre).astype(LOWER)
    part = jnp.dot(inner, w_out, preferred_element_type=WIDE).astype(LOWER)
    returned = lax.all_to_all(
        part.reshape(EXPERTS * shards, CAP, D), "dp", split_axis=0, concat_axis=0, tiled=True
    )
    outputs = fan_in(returned, shards)
    spread = slots * weight[:, :EXPERTS].T[:, None, :]
    moe = jnp.einsum("ect,ecd->td", spread, outputs, precision=HIGH)
    const_p = jax.nn.softmax(contract_cols(second_low, const_gate).reshape(tokens, 2, 2), -1)
    const_out = const_p[:, :, 0:1] * second[:, None, :] + const_p[:, :, 1:2] * const_vec[None]
    moe = moe + weight[:, EXPERTS + 1 : EXPERTS + 2] * second
    moe = (
        moe
        + weight[:, EXPERTS + 2 : EXPERTS + 3] * const_out[:, 0]
        + weight[:, EXPERTS + 3 :] * const_out[:, 1]
    )
    third = first + moe
    kept = dict(
        mask=mask,
        scale_one=scale_one,
        normed_low=normed_low,
        qkv=qkv,
        lse=top + jnp.log(total),
        mixed=mixed,
        first=first,
        second=second,
        scale_two=scale_two,
        second_low=second_low,
        route_p=route_p,
        used=used,
        weight=weight,
        slots=slots,
        spread=spread,
        rows=rows,
        gate_pre=gate_pre,
        up_pre=up_pre,
        inner=inner,
        outputs=outputs,
        const_p=const_p,
        const_out=const_out,
    )
    return (third, kept)


def head_step(third, positions, targets, table_all, gain, own):
    final, scale_three = norm_fwd(third, gain)
    tokens = third.shape[0]
    count = positions.shape[0]
    pick = (positions[:, None] == jnp.arange(tokens, dtype=jnp.int32)[None, :]).astype(WIDE)
    chosen = jnp.dot(pick, final, precision=HIGH).astype(LOWER)
    gathered = lax.all_gather(chosen, "dp", axis=0, tiled=True)
    logits = contract_cols(gathered, table_all)
    local_rows = table_all.shape[0]
    hit = (
        targets.reshape(-1)[:, None] - own * local_rows
        == jnp.arange(local_rows, dtype=jnp.int32)[None, :]
    )
    top = jnp.max(logits, -1)
    total = jnp.sum(jnp.exp(logits - top[:, None]), -1)
    aimed = jnp.sum(jnp.where(hit, logits, 0.0), -1)
    top, total, aimed = merged((top, total, aimed), "dp", merge_rows)
    lse = top + jnp.log(total)
    loss_part = jnp.sum(lax.dynamic_slice_in_dim(lse - aimed, own * count, count)) / count
    grad_logits = ((jnp.exp(logits - lse[:, None]) - hit.astype(WIDE)) / count).astype(LOWER)
    grad_table = contract_rows(grad_logits, gathered)
    grad_chosen = lax.psum_scatter(
        jnp.dot(grad_logits, table_all, preferred_element_type=WIDE).astype(jnp.bfloat16),
        "dp",
        scatter_dimension=0,
        tiled=True,
    ).astype(jnp.float32)
    grad_final = jnp.dot(pick.T, grad_chosen, precision=HIGH)
    grad_third, grad_gain = norm_back(third, scale_three, gain, grad_final)
    return (loss_part, grad_third, grad_gain, grad_table)


def layer_backward(hidden, grad_third, kept, dense_all, small_all, w_in, w_out, shards):
    gains, const_vec, router, const_gate = split_small(small_all)
    tokens = hidden.shape[0]
    weight = kept["weight"]
    route_p = kept["route_p"]
    second_wide = kept["second_low"].astype(WIDE)
    per_token = jnp.einsum("ect,ecd->etd", kept["slots"], kept["outputs"], precision=HIGH)
    grad_real = jnp.sum(per_token * grad_third[None], -1).T
    grad_copy = jnp.sum(grad_third * kept["second"], -1, keepdims=True)
    grad_const = jnp.sum(grad_third[:, None, :] * kept["const_out"], -1)
    grad_weight = jnp.concatenate(
        [grad_real, jnp.zeros((tokens, 1), WIDE), grad_copy, grad_const], 1
    )
    grad_p = grad_weight * kept["used"]
    grad_logit = route_p * (grad_p - jnp.sum(route_p * grad_p, -1, keepdims=True))
    grad_router = rows_high(grad_logit, second_wide)
    grad_second = jnp.dot(grad_logit, router.astype(WIDE), precision=HIGH)
    const_p = kept["const_p"]
    w_const = weight[:, EXPERTS + 2 :]
    along_vec = jnp.dot(grad_third, const_vec.T, precision=HIGH)
    grad_alpha = w_const[:, :, None] * jnp.stack(
        [jnp.broadcast_to(grad_copy, along_vec.shape), along_vec], -1
    )
    grad_clog = (const_p * (grad_alpha - jnp.sum(const_p * grad_alpha, -1, keepdims=True))).reshape(
        tokens, 4
    )
    grad_cgate = rows_high(grad_clog, second_wide)
    grad_cvec = rows_high(w_const * const_p[:, :, 1], grad_third)
    grad_second = grad_second + jnp.dot(grad_clog, const_gate.astype(WIDE), precision=HIGH)
    carry = weight[:, EXPERTS + 1 : EXPERTS + 2] + jnp.sum(
        w_const * const_p[:, :, 0], -1, keepdims=True
    )
    grad_second = grad_second + carry * grad_third
    grad_out = jnp.einsum("ect,td->ecd", kept["spread"], grad_third, precision=HIGH).astype(LOWER)
    grad_part = lax.all_to_all(
        fan_out(grad_out, shards), "dp", split_axis=0, concat_axis=0, tiled=True
    ).reshape(-1, D)
    gate_pre, up_pre = (kept["gate_pre"], kept["up_pre"])
    grad_inner = contract_cols(grad_part, w_out)
    sig = jax.nn.sigmoid(gate_pre)
    grad_gate = (grad_inner * up_pre * sig * (1.0 + gate_pre * (1.0 - sig))).astype(LOWER)
    grad_up = (grad_inner * gate_pre * sig).astype(LOWER)
    grad_w_out = contract_rows(kept["inner"], grad_part)
    grad_w_in = jnp.stack(
        [contract_rows(kept["rows"], grad_gate), contract_rows(kept["rows"], grad_up)]
    )
    grad_rows = (contract_cols(grad_gate, w_in[0]) + contract_cols(grad_up, w_in[1])).astype(LOWER)
    came_back = lax.all_to_all(
        grad_rows.reshape(EXPERTS * shards, CAP, D), "dp", split_axis=0, concat_axis=0, tiled=True
    )
    grad_second = grad_second + jnp.einsum(
        "ect,ecd->td", kept["slots"], fan_in(came_back, shards), precision=HIGH
    )
    grad_first_norm, grad_gain_two = norm_back(
        kept["first"], kept["scale_two"], gains[1], grad_second
    )
    grad_first = grad_third + grad_first_norm
    grad_attn = grad_first.astype(LOWER)
    grad_wo = contract_rows(kept["mixed"], grad_attn)
    grad_mixed = (
        contract_cols(grad_attn, dense_all[:, 3 * D :]).astype(LOWER).reshape(tokens, -1, HDIM)
    )
    qkv = kept["qkv"]
    probs = jnp.exp(head_scores(qkv, kept["mask"]) - kept["lse"])
    grad_values = jnp.einsum(
        "hqk,qhd->khd", probs.astype(LOWER), grad_mixed, preferred_element_type=WIDE
    )
    grad_probs = jnp.einsum(
        "qhd,khd->hqk", grad_mixed, split_heads(qkv, 2), preferred_element_type=WIDE
    )
    grad_scores = (probs * (grad_probs - jnp.sum(probs * grad_probs, -1, keepdims=True))).astype(
        LOWER
    )
    grad_query = jnp.einsum(
        "hqk,khd->qhd", grad_scores, split_heads(qkv, 1), preferred_element_type=WIDE
    ) * HDIM ** (-0.5)
    grad_keys = jnp.einsum(
        "hqk,qhd->khd", grad_scores, split_heads(qkv, 0), preferred_element_type=WIDE
    ) * HDIM ** (-0.5)
    grad_qkv = jnp.concatenate(
        [
            grad_query.reshape(tokens, D),
            grad_keys.reshape(tokens, D),
            grad_values.reshape(tokens, D),
        ],
        1,
    ).astype(LOWER)
    grad_wqkv = contract_rows(kept["normed_low"], grad_qkv)
    grad_normed = contract_cols(grad_qkv, dense_all[:, : 3 * D])
    unused, grad_gain_one = norm_back(hidden, kept["scale_one"], gains[0], grad_normed)
    dense_grad = jnp.concatenate([grad_wqkv, grad_wo], 1)
    small_parts = (grad_gain_one[None], grad_gain_two[None], grad_cvec, grad_router, grad_cgate)
    return (dense_grad, small_parts, grad_w_in, grad_w_out)


def group_squares(arrays, device):
    dense, small, ein, eout, tab = arrays
    width = dense.shape[1]
    front = (device * width + jnp.arange(width, dtype=jnp.int32) < 3 * D).astype(WIDE)
    dense_sq = jnp.sum(dense * dense, 0)
    return jnp.stack(
        [
            jnp.sum(dense_sq * front),
            jnp.sum(dense_sq * (1.0 - front)),
            jnp.sum(small[:5] * small[:5]),
            jnp.sum(small[5:] * small[5:]),
            jnp.sum(ein * ein),
            jnp.sum(eout * eout),
            jnp.sum(tab * tab),
        ]
    )


def moments(weight, first, second, grad):
    first = 0.5 * first + 0.5 * grad
    second = 0.5 * second + 0.5 * grad * grad
    corr = 1.0 - 0.5**STEP
    update = first / corr / (jnp.sqrt(second / corr) + EPS) + 0.01 * weight
    return (first, second, update)


def local(
    x_in,
    seq_lens,
    routes,
    positions,
    targets,
    dense_w,
    small_w,
    expert_in,
    expert_out,
    table,
    dense_m,
    small_m,
    expin_m,
    expout_m,
    table_m,
    dense_v,
    small_v,
    expin_v,
    expout_v,
    table_v,
):
    shards = lax.axis_size("dp") // EXPERTS
    own = lax.axis_index("dp")
    device = own * lax.axis_size("rep") + lax.axis_index("rep")
    masters = (dense_w, small_w, expert_in, expert_out, table)
    dense_all, small_all = (
        lax.all_gather(dense_w.astype(LOWER), ("dp", "rep"), axis=1, tiled=True),
        lax.all_gather(small_w.astype(LOWER), ("dp", "rep"), axis=1, tiled=True),
    )
    w_in, w_out, table_all = (
        lax.all_gather(expert_in.astype(LOWER), "rep", axis=1, tiled=True),
        lax.all_gather(expert_out.astype(LOWER), "rep", axis=0, tiled=True),
        lax.all_gather(table.astype(LOWER), "rep", axis=0, tiled=True),
    )
    final_gain = small_all[2].astype(WIDE)
    hidden = x_in.astype(WIDE)
    third, kept = layer_forward(
        hidden, seq_lens[0], routes, dense_all, small_all, w_in, w_out, shards
    )
    loss_part, grad_third, grad_gain_final, grad_table = head_step(
        third, positions, targets, table_all, final_gain, own
    )
    dense_grad, small_parts, grad_w_in, grad_w_out = layer_backward(
        hidden, grad_third, kept, dense_all, small_all, w_in, w_out, shards
    )
    small_grad = jnp.concatenate(
        [
            small_parts[0],
            small_parts[1],
            grad_gain_final[None],
            small_parts[2],
            small_parts[3],
            small_parts[4],
        ],
        0,
    )
    dense_g, small_g = (
        lax.psum_scatter(dense_grad, ("dp", "rep"), scatter_dimension=1, tiled=True),
        lax.psum_scatter(small_grad, ("dp", "rep"), scatter_dimension=1, tiled=True),
    )
    ein_g, eout_g, table_g = (
        lax.psum_scatter(
            grad_w_in.astype(jnp.bfloat16), "rep", scatter_dimension=1, tiled=True
        ).astype(jnp.float32),
        lax.psum_scatter(
            grad_w_out.astype(jnp.bfloat16), "rep", scatter_dimension=0, tiled=True
        ).astype(jnp.float32),
        lax.psum_scatter(
            grad_table.astype(jnp.bfloat16), "rep", scatter_dimension=0, tiled=True
        ).astype(jnp.float32),
    )
    grads = (dense_g, small_g, ein_g, eout_g, table_g)
    firsts = (dense_m, small_m, expin_m, expout_m, table_m)
    seconds = (dense_v, small_v, expin_v, expout_v, table_v)
    results = [moments(w, m, v, g) for w, m, v, g in zip(masters, firsts, seconds, grads)]
    update_parts = group_squares(tuple((r[2] for r in results)), device)
    weight_sq, update_sq, loss = lax.psum(
        (group_squares(masters, device), update_parts, loss_part), ("dp", "rep")
    )
    weight_norm = jnp.sqrt(weight_sq)
    update_norm = jnp.sqrt(update_sq)
    trust = weight_norm / update_norm
    width = dense_w.shape[1]
    column = device * width + jnp.arange(width, dtype=jnp.int32)
    dense_scale = jnp.where(column < 3 * D, trust[0], trust[1])[None, :]
    small_scale = jnp.where(jnp.arange(21, dtype=jnp.int32) < 5, trust[2], trust[3])[:, None]
    scales = (dense_scale, small_scale, trust[4], trust[5], trust[6])
    outs = [loss, jnp.stack([weight_norm, update_norm, trust])]
    for w, r, factor in zip(masters, results, scales):
        fresh = w - 0.2 * factor * r[2]
        outs += [r[0], r[1], fresh, fresh.astype(LOWER)]
    return tuple(outs)


def solution(mesh):
    in_specs = (
        P(("dp", "rep"), None),
        P(("dp", "rep"), None),
        P(("dp", "rep"), None),
        P(("dp", "rep")),
        P("rep", None, None),
        P(None, ("dp", "rep")),
        P(None, ("dp", "rep")),
        P(None, "rep", "dp"),
        P(("dp", "rep"), None),
        P(("dp", "rep"), None),
        P(None, ("dp", "rep")),
        P(None, ("dp", "rep")),
        P(None, "rep", "dp"),
        P(("dp", "rep"), None),
        P(("dp", "rep"), None),
        P(None, ("dp", "rep")),
        P(None, ("dp", "rep")),
        P(None, "rep", "dp"),
        P(("dp", "rep"), None),
        P(("dp", "rep"), None),
    )
    out_specs = (
        P(),
        P(),
        P(None, ("dp", "rep")),
        P(None, ("dp", "rep")),
        P(None, ("dp", "rep")),
        P(None, ("dp", "rep")),
        P(None, ("dp", "rep")),
        P(None, ("dp", "rep")),
        P(None, ("dp", "rep")),
        P(None, ("dp", "rep")),
        P(None, "rep", "dp"),
        P(None, "rep", "dp"),
        P(None, "rep", "dp"),
        P(None, "rep", "dp"),
        P(("dp", "rep"), None),
        P(("dp", "rep"), None),
        P(("dp", "rep"), None),
        P(("dp", "rep"), None),
        P(("dp", "rep"), None),
        P(("dp", "rep"), None),
        P(("dp", "rep"), None),
        P(("dp", "rep"), None),
    )
    return jax.shard_map(local, mesh=mesh, in_specs=in_specs, out_specs=out_specs, check_vma=False)
```

profile of v0, /device:TPU:0, one launch (start us, length us, event | category | flops | bytes accessed | tf_op | source)
XLA Modules:
  0.0 1080.7 jit_solution(14419440147303347801)
XLA Ops:
  14.3 43.9 %all_gather.36 = bf16[21,768]{0,1:T(8,128)(2,1)S(1)} all-gather(bf16[21,24]{0,1:T(8,128)(2,1)S(1)} %copy.157), channel_id=1, replica_groups=mesh['dp'=8,'rep'=4] {'dp','rep'}, dimensions={1}, use_global_device_ids=true | all-gather | bytes 33264 | tf_op jit(solution)/shard_map/all_gather | solution.py:360
  60.9 17.3 %all-gather.9.cloned.1.call-done = bf16[768,3072]{0,1:T(8,128)(2,1)} async-done(((bf16[768,96]{0,1:T(8,128)(2,1)}), bf16[768,3072]{0,1:T(8,128)(2,1)}) %all-gather.9.cloned.1.call-update) | async-done | bytes 4718608 | tf_op jit(solution)/shard_map/all_gather | solution.py:359
  108.2 17.3 %all-gather.11.cloned.1.call-done = bf16[2,768,2048]{2,1,0:T(8,128)(2,1)} async-done(((bf16[2,192,2048]{2,1,0:T(8,128)(2,1)}), bf16[2,768,2048]{2,1,0:T(8,128)(2,1)}) %all-gather.11.cloned.1.call-update) | async-done | bytes 6291472 | tf_op jit(solution)/shard_map/all_gather | solution.py:363
  125.6 10.8 all-to-all-done
  144.1 6.6 multiply_convert_fusion.4
  173.0 24.3 %all-to-all-done.1 = bf16[8,96,768]{2,1,0:T(8,128)(2,1)} async-done(((bf16[8,96,768]{2,1,0:T(8,128)(2,1)}), bf16[8,96,768]{2,1,0:T(8,128)(2,1)}, u32[]{:S(2)}, u32[]{:S(2)}) %all-to-all-start.1) | async-done | bytes 1179680 | tf_op jit(solution)/shard_map/all_to_all | solution.py:137
  210.9 37.0 %all-gather.15.cloned.1.call-done = bf16[1024,768]{1,0:T(8,128)(2,1)} async-done(((bf16[128,768]{1,0:T(8,128)(2,1)}), bf16[1024,768]{1,0:T(8,128)(2,1)}) %all-gather.15.cloned.1.call-update) | async-done | bytes 1572880 | tf_op jit(solution)/shard_map/all_gather | solution.py:185
  247.9 82.9 %all-gather.17.cloned.1.call-done = bf16[8192,768]{1,0:T(8,128)(2,1)} async-done(((bf16[2048,768]{1,0:T(8,128)(2,1)}), bf16[8192,768]{1,0:T(8,128)(2,1)}) %all-gather.17.cloned.1.call-update) | async-done | bytes 12582928 | tf_op jit(solution)/shard_map/all_gather | solution.py:365
  330.8 22.8 %fusion.131 = (f32[1024]{0:T(1024)S(1)}, f32[1024,8192]{1,0:T(8,128)}) fusion(bf16[1024,768]{1,0:T(8,128)(2,1)} %all-gather.15.cloned.1.call-done, bf16[8192,768]{1,0:T(8,128)(2,1)} %all-gather.17.cloned.1.call-done), kind=kOutput, calls=%fused_computation.253 | convolution fusion | flops 12893289472 | bytes 47714304 | tf_op jit(solution)/shard_map/dot_general | solution.py:33
  353.6 30.5 %all-gather = f32[8192]{0:T(1024)S(1)} all-gather(f32[1024]{0:T(1024)S(1)} %get-tuple-element.300), channel_id=2, replica_groups=mesh['dp'=8,'rep'=4] {'dp'}, dimensions={0}, use_global_device_ids=true | all-gather | bytes 36864 | tf_op jit(solution)/shard_map/all_gather | solution.py:21
  384.0 16.3 %select_reduce_fusion = (f32[1024]{0:T(1024)S(1)}, f32[1024]{0:T(1024)S(1)}) fusion(f32[1024,8192]{1,0:T(8,128)} %get-tuple-element.301, s32[1024]{0:T(1024)S(1)} %subtract_bitcast_fusion, f32[1024]{0:T(1024)S(1)} %get-tuple-element.300), kind=kLoop, calls=%fused_computation.5 | loop fusion | flops 41940992 | bytes 33570816 | tf_op jit(solution)/shard_map/reduce_sum | solution.py:194
  400.3 30.4 %all-gather.1 = f32[8192]{0:T(1024)S(1)} all-gather(f32[1024]{0:T(1024)S(1)} %get-tuple-element.197), channel_id=3, replica_groups=mesh['dp'=8,'rep'=4] {'dp'}, dimensions={0}, use_global_device_ids=true | all-gather | bytes 36864 | tf_op jit(solution)/shard_map/all_gather | solution.py:21
  430.8 30.4 %all-gather.2 = f32[8192]{0:T(1024)S(1)} all-gather(f32[1024]{0:T(1024)S(1)} %get-tuple-element.196), channel_id=4, replica_groups=mesh['dp'=8,'rep'=4] {'dp'}, dimensions={0}, use_global_device_ids=true | all-gather | bytes 36864 | tf_op jit(solution)/shard_map/all_gather | solution.py:21
  462.4 15.3 %multiply_convert_fusion = bf16[1024,8192]{1,0:T(8,128)(2,1)S(1)} fusion(f32[1024,8192]{1,0:T(8,128)} %get-tuple-element.301, f32[1024]{0:T(1024)S(1)} %get-tuple-element.258, s32[1024]{0:T(1024)S(1)} %subtract_bitcast_fusion), kind=kLoop, calls=%fused_computation.4 | loop fusion | flops 50331648 | bytes 50339840 | tf_op jit(solution)/shard_map/convert_element_type | solution.py:198
  483.4 16.6 %convolution_convert_fusion.5 = bf16[1024,768]{1,0:T(8,128)(2,1)} fusion(bf16[1024,8192]{1,0:T(8,128)(2,1)S(1)} %multiply_convert_fusion, bf16[8192,768]{1,0:T(8,128)(2,1)} %all-gather.17.cloned.1.call-done), kind=kOutput, calls=%fused_computation.75 | convolution fusion | flops 12885688320 | bytes 30932992 | tf_op jit(solution)/shard_map/dot_general | solution.py:201
  500.3 64.7 %reduce-scatter.9.cloned.1.call-done = bf16[128,768]{1,0:T(8,128)(2,1)} async-done(((bf16[1024,768]{1,0:T(8,128)(2,1)}), bf16[128,768]{1,0:T(8,128)(2,1)}) %reduce-scatter.9.cloned.1.call-update) | async-done | bytes 196624 | tf_op jit(solution)/shard_map/reduce_scatter | solution.py:200
  572.7 31.1 %all_to_all.20 = bf16[8,96,768]{2,1,0:T(8,128)(2,1)S(1)} all-to-all(bf16[8,96,768]{2,1,0:T(8,128)(2,1)S(1)} %fusion.37), channel_id=1, replica_groups=mesh['dp'=8,'rep'=4] {'dp'}, dimensions={0} | all-to-all | bytes 2359296 | tf_op jit(solution)/shard_map/all_to_all | solution.py:245
  609.2 9.5 multiply_convert_fusion.2
  650.2 7.6 multiply_reduce_fusion.1
  660.2 13.6 %all-to-all-done.3 = bf16[8,96,768]{2,1,0:T(8,128)(2,1)} async-done(((bf16[8,96,768]{2,1,0:T(8,128)(2,1)}), bf16[8,96,768]{2,1,0:T(8,128)(2,1)}, u32[]{:S(2)}, u32[]{:S(2)}) %all-to-all-start.3) | async-done | bytes 1179680 | tf_op jit(solution)/shard_map/all_to_all | solution.py:258
  689.3 11.1 %multiply_reduce_fusion = (f32[12,512]{1,0:T(8,128)S(1)}, f32[12,512,512]{1,2,0:T(8,128)}) fusion(f32[12,512]{1,0:T(8,128)S(1)} %log_add_fusion, f32[12,512,512]{1,2,0:T(8,128)} %copy-done, pred[512,512]{0,1:T(8,128)(4,1)S(1)} %copy-done.16, bf16[512,12,64]{0,2,1:T(8,128)(2,1)S(1)} %bitcast.206, bf16[512,12,64]{0,2,1:T(8,128)(2,1)S(1)} %bitcast.205), kind=kOutput, calls=%fused_computation.10 | convolution fusion | flops 418375680 | bytes 27049984 | tf_op jit(solution)/shard_map/qhd,khd->hqk/dot_general | solution.py:278
  702.0 7.4 multiply_convert_fusion.1
  721.8 8.7 pad_maximum_fusion
  730.6 9.6 copy.185
  741.6 23.2 %convolution_convert_fusion = bf16[8192,768]{1,0:T(8,128)(2,1)} fusion(bf16[1024,8192]{1,0:T(8,128)(2,1)} %copy-done.4, bf16[1024,768]{1,0:T(8,128)(2,1)S(1)} %copy-done.75), kind=kOutput, calls=%fused_computation.8 | convolution fusion | flops 12891193344 | bytes 30932992 | tf_op jit(solution)/shard_map/dot_general | solution.py:29
  785.7 41.9 %all-reduce = f32[21,768]{1,0:T(8,128)S(1)} all-reduce(f32[21,768]{1,0:T(8,128)S(1)} %concatenate.16), channel_id=7, replica_groups=mesh['dp'=8,'rep'=4] {'dp','rep'}, use_global_device_ids=true, to_apply=%region_47.48.clone | all-reduce | flops 16128 | bytes 129024
  835.8 7.5 multiply_reduce_fusion.6
  843.3 32.7 %reduce-scatter.17.cloned.1.call-done = f32[96,768]{1,0:T(8,128)} async-done(((f32[3072,768]{1,0:T(8,128)}), f32[96,768]{1,0:T(8,128)}) %reduce-scatter.17.cloned.1.call-update) | async-done | bytes 294928
  882.7 93.9 %reduce-scatter.15.cloned.1.call-done = bf16[2048,768]{1,0:T(8,128)(2,1)} async-done(((bf16[8192,768]{1,0:T(8,128)(2,1)}), bf16[2048,768]{1,0:T(8,128)(2,1)}) %reduce-scatter.15.cloned.1.call-update) | async-done | bytes 3145744 | tf_op jit(solution)/shard_map/reduce_scatter | solution.py:400
  976.7 13.2 %multiply_reduce_fusion.3 = (f32[]{:T(128)}, f32[]{:T(128)}, f32[2048,768]{1,0:T(8,128)}, f32[2048,768]{1,0:T(8,128)}) fusion(f32[2048,768]{1,0:T(8,128)} %param.31, bf16[2048,768]{1,0:T(8,128)(2,1)} %reduce-scatter.15.cloned.1.call-done, f32[2048,768]{1,0:T(8,128)} %param.36, f32[2048,768]{1,0:T(8,128)} %param.41), kind=kLoop, calls=%fused_computation.30 | loop fusion | flops 26738688 | bytes 34603016 | tf_op jit(solution)/shard_map/reduce_sum | solution.py:319
  1001.4 39.8 %all-reduce.1 = (f32[]{:T(128)}, f32[7]{0:T(128)}, f32[7]{0:T(128)}) all-reduce(f32[]{:T(128)S(6)} %div.116, f32[7]{0:T(128)} %stack.99, f32[7]{0:T(128)S(1)} %stack.85), channel_id=1, replica_groups=mesh['dp'=8,'rep'=4] {'dp','rep'}, use_global_device_ids=true, to_apply=%region_20.21 | all-reduce | flops 15 | bytes 120 | tf_op jit(solution)/shard_map/psum | solution.py:409
  1054.7 10.4 fusion.117
  (368 shorter events, 234.1 us)
Async XLA Ops:
  7.2 71.0 %all-gather.9.cloned.1.call-start = ((), (), s32[]{:S(2)}) async-start(), calls=%async_computation.9 | async-start | bytes 4866048 | tf_op jit(solution)/shard_map/all_gather | solution.py:359
  9.7 115.9 %all-gather.11.cloned.1.call-start = ((), (), s32[]{:S(2)}) async-start(), calls=%async_computation.10 | async-start | bytes 7864320 | tf_op jit(solution)/shard_map/all_gather | solution.py:363
  13.1 45.5 %copy-start.30 = (bf16[512,768]{1,0:T(8,128)(2,1)S(1)}, bf16[512,768]{1,0:T(8,128)(2,1)}, u32[]{:S(2)}) copy-start(bf16[512,768]{1,0:T(8,128)(2,1)} %param.22) | copy-start | bytes 2359300
  13.2 45.7 %copy-start.76 = (s32[1,3]{1,0:T(1,128)S(1)}, s32[1,3]{1,0:T(1,128)}, u32[]{:S(2)}) copy-start(s32[1,3]{1,0:T(1,128)} %param.23) | copy-start | bytes 40
  13.2 46.2 %copy-start.67 = (s32[512,2]{0,1:T(2,128)S(1)}, s32[512,2]{0,1:T(2,128)}, u32[]{:S(2)}) copy-start(s32[512,2]{0,1:T(2,128)} %param.24) | copy-start | bytes 12292
  13.2 143.1 %all-gather.13.cloned.1.call-start = ((), (), s32[]{:S(2)}) async-start(), calls=%async_computation.11 | async-start | bytes 3932160 | tf_op jit(solution)/shard_map/all_gather | solution.py:364
  58.6 23.6 %copy-start.65 = (f32[768]{0:T(1024)}, f32[768]{0:T(1024)S(1)}, u32[]{:S(2)}) copy-start(f32[768]{0:T(1024)S(1)} %get-tuple-element.209) | copy-start | bytes 9220
  58.9 23.4 %copy-start.71 = (f32[512]{0:T(512)}, f32[512]{0:T(512)S(1)}, u32[]{:S(2)}) copy-start(f32[512]{0:T(512)S(1)} %add_rsqrt_fusion.2) | copy-start | bytes 6148
  59.4 31.0 %copy-start.15 = (pred[512,512]{0,1:T(8,128)(4,1)}, pred[512,512]{0,1:T(8,128)(4,1)S(1)}, u32[]{:S(2)}) copy-start(pred[512,512]{0,1:T(8,128)(4,1)S(1)} %fusion.50) | copy-start | bytes 786436
  59.5 109.4 %copy-start.27 = (f32[512,12]{0,1:T(8,128)}, f32[512,12]{0,1:T(8,128)S(1)}, u32[]{:S(2)}) copy-start(f32[512,12]{0,1:T(8,128)S(1)} %fusion.87) | copy-start | bytes 73732
  100.4 67.9 %copy-start.2 = (bf16[512,768]{1,0:T(8,128)(2,1)}, bf16[512,768]{1,0:T(8,128)(2,1)S(1)}, u32[]{:S(2)}) copy-start(bf16[512,768]{1,0:T(8,128)(2,1)S(1)} %get-tuple-element.267) | copy-start | bytes 2359300
  102.2 34.1 %all-to-all-start = ((bf16[8,96,768]{2,1,0:T(8,128)(2,1)}), bf16[8,96,768]{2,1,0:T(8,128)(2,1)}, u32[]{:S(2)}, u32[]{:S(2)}) async-start(bf16[8,96,768]{2,1,0:T(8,128)(2,1)} %convolution_convert_fusion.7), calls=%async_computation | async-start | bytes 2359296 | tf_op jit(solution)/shard_map/all_to_all | solution.py:129
  108.2 33.2 %copy-start.47 = (f32[512,4]{0,1:T(4,128)}, f32[512,4]{0,1:T(4,128)S(1)}, u32[]{:S(2)}) copy-start(f32[512,4]{0,1:T(4,128)S(1)} %fusion.79) | copy-start | bytes 24580
  162.7 34.6 %all-to-all-start.1 = ((bf16[8,96,768]{2,1,0:T(8,128)(2,1)}), bf16[8,96,768]{2,1,0:T(8,128)(2,1)}, u32[]{:S(2)}, u32[]{:S(2)}) async-start(bf16[8,96,768]{2,1,0:T(8,128)(2,1)} %bitcast.211), calls=%async_computation.1 | async-start | bytes 2359296 | tf_op jit(solution)/shard_map/all_to_all | solution.py:137
  168.2 79.6 %all-gather.15.cloned.1.call-start = ((), (), s32[]{:S(2)}) async-start(), calls=%async_computation.12 | async-start | bytes 1769472 | tf_op jit(solution)/shard_map/all_gather | solution.py:185
  168.7 33.8 %copy-start.25 = (f32[512,12]{0,1:T(8,128)}, f32[512,12]{0,1:T(8,128)S(1)}, u32[]{:S(2)}) copy-start(f32[512,12]{0,1:T(8,128)S(1)} %get-tuple-element.297) | copy-start | bytes 73732
  168.7 33.8 %copy-start.50 = (f32[512]{0:T(512)}, f32[512]{0:T(512)S(1)}, u32[]{:S(2)}) copy-start(f32[512]{0:T(512)S(1)} %get-tuple-element.296) | copy-start | bytes 6148
  168.8 33.8 %copy-start.55 = (f32[512]{0:T(512)}, f32[512]{0:T(512)S(1)}, u32[]{:S(2)}) copy-start(f32[512]{0:T(512)S(1)} %fusion.89) | copy-start | bytes 6148
  168.8 33.8 %copy-start.49 = (f32[512,2,2]{0,1,2:T(2,128)}, f32[512,2,2]{0,1,2:T(2,128)S(1)}, u32[]{:S(2)}) copy-start(f32[512,2,2]{0,1,2:T(2,128)S(1)} %broadcast_divide_fusion) | copy-start | bytes 24580
  168.9 33.7 %copy-start.42 = (f32[512,12]{0,1:T(8,128)}, f32[512,12]{0,1:T(8,128)S(1)}, u32[]{:S(2)}) copy-start(f32[512,12]{0,1:T(8,128)S(1)} %fusion.115) | copy-start | bytes 73732
  205.4 125.4 %all-gather.17.cloned.1.call-start = ((), (), s32[]{:S(2)}) async-start(), calls=%async_computation.13 | async-start | bytes 15728640 | tf_op jit(solution)/shard_map/all_gather | solution.py:365
  210.2 354.7 %reduce-scatter.9.cloned.1.call-start = ((), (), s32[]{:S(2)}) async-start(), calls=%async_computation.14 | async-start | bytes 1769472 | tf_op jit(solution)/shard_map/reduce_scatter | solution.py:200
  500.1 329.4 %reduce-scatter.13.cloned.1.call-start = ((), (), s32[]{:S(2)}) async-start(), calls=%async_computation.16 | async-start | bytes 3932160 | tf_op jit(solution)/shard_map/reduce_scatter | solution.py:397
  568.7 89.4 %copy-start.54 = (f32[512]{0:T(512)}, f32[512]{0:T(512)S(1)}, u32[]{:S(2)}) copy-start(f32[512]{0:T(512)S(1)} %get-tuple-element.255) | copy-start | bytes 6148
  568.7 36.2 %copy-start.83 = (bf16[768,2048]{1,0:T(8,128)(2,1)S(1)}, bf16[768,2048]{1,0:T(8,128)(2,1)}, u32[]{:S(2)}) copy-start(bf16[768,2048]{1,0:T(8,128)(2,1)} %get-tuple-element.294) | copy-start | bytes 9437188
  608.9 226.9 %reduce-scatter.11.cloned.1.call-start = ((), (), s32[]{:S(2)}) async-start(), calls=%async_computation.15 | async-start | bytes 7864320 | tf_op jit(solution)/shard_map/reduce_scatter | solution.py:394
  642.6 31.2 %all-to-all-start.3 = ((bf16[8,96,768]{2,1,0:T(8,128)(2,1)}), bf16[8,96,768]{2,1,0:T(8,128)(2,1)}, u32[]{:S(2)}, u32[]{:S(2)}) async-start(bf16[8,96,768]{2,1,0:T(8,128)(2,1)} %bitcast.210), calls=%async_computation.4 | async-start | bytes 2359296 | tf_op jit(solution)/shard_map/all_to_all | solution.py:258
  646.8 229.1 %reduce-scatter.17.cloned.1.call-start = ((), (), s32[]{:S(2)}) async-start(), calls=%async_computation.18 | async-start | bytes 9732096
  657.9 19.7 %copy-start.43 = (f32[8,512]{1,0:T(8,128)}, f32[8,512]{1,0:T(8,128)S(1)}, u32[]{:S(2)}) copy-start(f32[8,512]{1,0:T(8,128)S(1)} %multiply_reduce_fusion.1) | copy-start | bytes 49156
  740.2 236.4 %reduce-scatter.15.cloned.1.call-start = ((), (), s32[]{:S(2)}) async-start(), calls=%async_computation.17 | async-start | bytes 15728640 | tf_op jit(solution)/shard_map/reduce_scatter | solution.py:400
  781.3 46.3 %copy-start.60 = (f32[21,24]{1,0:T(8,128)S(1)}, f32[21,24]{1,0:T(8,128)}, u32[]{:S(2)}) copy-start(f32[21,24]{1,0:T(8,128)} %param.33) | copy-start | bytes 6052
  781.3 46.3 %copy-start.61 = (f32[21,24]{1,0:T(8,128)S(1)}, f32[21,24]{1,0:T(8,128)}, u32[]{:S(2)}) copy-start(f32[21,24]{1,0:T(8,128)} %param.38) | copy-start | bytes 6052
  (68 other events, 423.3 us)
Sparse Core Ops, SparseCore 0:
  11.5 66.6 all-gather.8
  80.3 45.1 all-gather.10
  127.7 28.5 all-gather.12
  205.5 42.3 all-gather.14
  249.8 80.8 all-gather.16
  500.2 64.7 reduce-scatter.8
  609.0 36.5 reduce-scatter.12
  648.8 58.3 reduce-scatter.10
  740.3 135.5 reduce-scatter.16
  878.4 98.1 reduce-scatter.14
where the time goes:
time: 1090 us; the launch traced here: 1080 us
  waiting for transfers between devices  400 us (37%)
  blocking collectives  248 us (23%)
  matrix products  198 us (18%)
  other arithmetic  138 us (13%)
  local copies, waits for them, and re-layouts  62 us (6%)
  between operations  18.7 us (2%)
  starting transfers between devices  15.6 us (1%)
    reduce_scatter x1, waiting for transfers between devices, local(): lax.psum_scatter(grad_table.astype(jnp.bfloat16), 'rep', scatter_dimensio...  93.9 us
    all_gather x3, blocking collectives, merged(): pieces = jax.tree.map(lambda part: lax.all_gather(part, axis), value)  91.3 us
    all_gather x1, waiting for transfers between devices, local(): lax.all_gather(table.astype(LOWER), 'rep', axis=0, tiled=True)  82.9 us
    reduce_scatter x1, waiting for transfers between devices, head_step(): lax.psum_scatter(jnp.dot(grad_logits, table_all, preferred_element_type=W...  64.7 us
    dot_general x8, matrix products, contract_cols(): lax.dot_general(left, right, (((1,), (1,)), ((), ())), preferred_element_...  51.5 us
    dot_general x6, matrix products, contract_rows(): lax.dot_general(left, right, (((0,), (0,)), ((), ())), preferred_element_...  45.1 us
    unnamed x186, local copies, waits for them, and re-layouts  44.4 us
    all_gather x1, blocking collectives, local(): lax.all_gather(small_w.astype(LOWER), ('dp', 'rep'), axis=1, tiled=True)  43.9 us
  transfers between devices with their start and end apart: 13, of which 11 were waited for; matrix products, arithmetic and copies ran while one was open for 21% of the time, Pallas kernels for 0%

commit v1 on v0

v1 whole, which is shorter than its diff:
```python
import jax
import jax.numpy as jnp
from jax import lax
from jax.sharding import PartitionSpec as P

D = 768
HDIM = 64
EXPERTS = 8
NULLS = 4
STEP = 5
CAP = 96


EPS = 1e-06
HIGH = lax.Precision.HIGHEST
LOWER = jnp.bfloat16
WIDE = jnp.float32
BOTH = ("dp", "rep")
LANES = 128


def contract_rows(left, right):
    return lax.dot_general(left, right, (((0,), (0,)), ((), ())), preferred_element_type=WIDE)


def contract_cols(left, right):
    return lax.dot_general(left, right, (((1,), (1,)), ((), ())), preferred_element_type=WIDE)


def plain(left, right):
    return jnp.dot(left, right, preferred_element_type=WIDE)


def rows_high(left, right):
    return lax.dot_general(left, right, (((0,), (0,)), ((), ())), precision=HIGH)


def swap(value, axis):
    return lax.all_to_all(value, axis, split_axis=0, concat_axis=0, tiled=True)


def share(value, axis, count):
    return swap(jnp.broadcast_to(value[None], (count,) + value.shape), axis)


def halve(buffer, axis, mask, size):
    own = (lax.axis_index(axis) & mask) // mask
    halves = buffer.reshape((buffer.shape[0] // 2, 2) + buffer.shape[1:])
    keep = lax.dynamic_index_in_dim(halves, own, 1, keepdims=False)
    give = lax.dynamic_index_in_dim(halves, 1 - own, 1, keepdims=False).astype(LOWER)
    take = lax.ppermute(give, axis, [(i, i ^ mask) for i in range(size)])
    return keep + take.astype(WIDE)


def scatter_sum(blocks, n_dp, n_rep):
    value = blocks.swapaxes(0, 1)
    mask = 1
    while mask < n_rep:
        value = halve(value, "rep", mask, n_rep)
        mask *= 2
    value = value[0]
    mask = 1
    while mask < n_dp:
        value = halve(value, "dp", mask, n_dp)
        mask *= 2
    return value[0]


def norm_fwd(hidden, gain):
    scale = lax.rsqrt(jnp.mean(hidden * hidden, -1, keepdims=True) + EPS)
    return (hidden * scale * gain, scale)


def norm_back(hidden, scale, gain, grad_out):
    normed = hidden * scale
    grad_gain = jnp.sum(grad_out * normed, 0)
    inner = grad_out * gain
    grad_in = scale * (inner - normed * jnp.mean(inner * normed, -1, keepdims=True))
    return (grad_in, grad_gain)


def seq_mask(lens, tokens):
    place = jnp.arange(tokens, dtype=jnp.int32)
    count = lens.shape[0]
    ends = [jnp.sum(lens[: i + 1]) for i in range(count)]
    segment = sum((place >= end).astype(jnp.int32) for end in ends)
    return (segment[:, None] == segment[None, :]) & (place[None, :] <= place[:, None])


def split_heads(qkv, which):
    return qkv[:, which * D : (which + 1) * D].reshape(qkv.shape[0], -1, HDIM)


def head_scores(qkv, mask):
    scores = jnp.einsum(
        "qhd,khd->hqk", split_heads(qkv, 0), split_heads(qkv, 1), preferred_element_type=WIDE
    )
    return jnp.where(mask[None], scores * HDIM ** (-0.5), -1e30)


def fan_out(buffer, shards):
    return jnp.broadcast_to(buffer[:, None], (EXPERTS, shards) + buffer.shape[1:]).reshape(
        (EXPERTS * shards,) + buffer.shape[1:]
    )


def pick_slots(picks, received, shards):
    parts = received.reshape((EXPERTS, shards) + received.shape[1:])
    total = plain(picks, parts[:, 0].reshape(-1, D))
    for s in range(1, shards):
        total = total + plain(picks, parts[:, s].reshape(-1, D))
    return total


def layer_forward(hidden, lens, routes, dense_t, small_all, w_in, w_out, shards):
    gains, const_vec, router, const_gate = (
        small_all[:3].astype(WIDE),
        small_all[3:5].astype(WIDE),
        small_all[5:17],
        small_all[17:21],
    )
    tokens = hidden.shape[0]
    mask = seq_mask(lens, tokens)
    normed, scale_one = norm_fwd(hidden, gains[0])
    normed_low = normed.astype(LOWER)
    qkv = contract_cols(normed_low, dense_t[: 3 * D]).astype(LOWER)
    scores = head_scores(qkv, mask)
    top = jnp.max(scores, -1, keepdims=True)
    expo = jnp.exp(scores - top)
    total = jnp.sum(expo, -1, keepdims=True)
    probs = (expo / total).astype(LOWER)
    mixed = jnp.einsum("hqk,khd->qhd", probs, split_heads(qkv, 2), preferred_element_type=WIDE)
    mixed = mixed.reshape(tokens, D).astype(LOWER)
    first = hidden + contract_cols(mixed, dense_t[3 * D :])
    second, scale_two = norm_fwd(first, gains[1])
    second_low = second.astype(LOWER)
    route_p = jax.nn.softmax(contract_cols(second_low, router), -1)
    hits = routes[:, :, None] == jnp.arange(EXPERTS + NULLS, dtype=jnp.int32)[None, None, :]
    used = jnp.sum(hits.astype(WIDE), 1)
    weight = route_p * used
    earlier = jnp.tril(jnp.ones((tokens, tokens), LOWER), -1)
    rank = plain(earlier, used[:, :EXPERTS].astype(LOWER)).astype(jnp.int32)
    place = jnp.arange(EXPERTS, dtype=jnp.int32)[None] * CAP + rank
    place = jnp.where(rank < CAP, place, -1)
    real_hits = hits[:, :, :EXPERTS]
    slot = jnp.max(jnp.where(real_hits, place[:, None, :], -1), -1)
    w_slot = jnp.sum(jnp.where(real_hits, weight[:, None, :EXPERTS], 0.0), -1)
    all_slots = jnp.arange(EXPERTS * CAP, dtype=jnp.int32)
    picks = [(slot[:, k : k + 1] == all_slots[None]).astype(LOWER) for k in range(2)]
    kept = [(slot[:, k : k + 1] >= 0).astype(WIDE) for k in range(2)]
    both = picks[0] + picks[1]
    buffer = contract_rows(both, second_low).astype(LOWER).reshape(EXPERTS, CAP, D)
    rows = swap(fan_out(buffer, shards), "dp").reshape(-1, D)
    gate_pre = plain(rows, w_in[0])
    up_pre = plain(rows, w_in[1])
    inner = (jax.nn.silu(gate_pre) * up_pre).astype(LOWER)
    part = plain(inner, w_out).astype(LOWER)
    returned = swap(part.reshape(EXPERTS * shards, CAP, D), "dp")
    outs = [pick_slots(picks[k], returned, shards) for k in range(2)]
    moe = w_slot[:, 0:1] * outs[0] + w_slot[:, 1:2] * outs[1]
    const_p = jax.nn.softmax(contract_cols(second_low, const_gate).reshape(tokens, 2, 2), -1)
    const_out = const_p[:, :, 0:1] * second[:, None, :] + const_p[:, :, 1:2] * const_vec[None]
    moe = moe + weight[:, EXPERTS + 1 : EXPERTS + 2] * second
    moe = (
        moe
        + weight[:, EXPERTS + 2 : EXPERTS + 3] * const_out[:, 0]
        + weight[:, EXPERTS + 3 :] * const_out[:, 1]
    )
    third = first + moe
    saved = dict(
        gains=gains,
        const_vec=const_vec,
        router=router,
        const_gate=const_gate,
        mask=mask,
        scale_one=scale_one,
        normed_low=normed_low,
        qkv=qkv,
        lse=top + jnp.log(total),
        mixed=mixed,
        first=first,
        second=second,
        scale_two=scale_two,
        second_low=second_low,
        route_p=route_p,
        hits=hits,
        used=used,
        weight=weight,
        w_slot=w_slot,
        picks=picks,
        kept=kept,
        both=both,
        rows=rows,
        gate_pre=gate_pre,
        up_pre=up_pre,
        inner=inner,
        outs=outs,
        const_p=const_p,
        const_out=const_out,
    )
    return (third, saved)


def head_step(third, positions, targets, table_all, gain, own, n_dp):
    final, scale_three = norm_fwd(third, gain)
    tokens = third.shape[0]
    count = positions.shape[0]
    pick = positions[:, None] == jnp.arange(tokens, dtype=jnp.int32)[None, :]
    chosen = plain(pick.astype(LOWER), final.astype(LOWER)).astype(LOWER)
    gathered = share(chosen, "dp", n_dp).reshape(-1, D)
    logits = contract_cols(gathered, table_all)
    local_rows = table_all.shape[0]
    aim = targets.reshape(-1)[:, None] - own * local_rows
    hit = aim == jnp.arange(local_rows, dtype=jnp.int32)[None, :]
    top = jnp.max(logits, -1)
    total = jnp.sum(jnp.exp(logits - top[:, None]), -1)
    aimed = jnp.sum(jnp.where(hit, logits, 0.0), -1)
    stats = jnp.stack([top, total, aimed]).reshape(-1, LANES)
    stats = share(stats, "dp", n_dp).reshape(n_dp, 3, -1)
    high = jnp.max(stats[:, 0], 0)
    sums = jnp.sum(stats[:, 1] * jnp.exp(stats[:, 0] - high[None]), 0)
    lse = high + jnp.log(sums)
    loss_rows = lse - jnp.sum(stats[:, 2], 0)
    loss_part = jnp.sum(lax.dynamic_slice_in_dim(loss_rows, own * count, count)) / count
    grad_logits = ((jnp.exp(logits - lse[:, None]) - hit.astype(WIDE)) / count).astype(LOWER)
    grad_rows = plain(grad_logits, table_all).astype(LOWER).reshape(n_dp, count, D)
    grad_chosen = jnp.sum(swap(grad_rows, "dp").astype(WIDE), 0)
    grad_table = contract_rows(grad_logits, gathered).astype(LOWER)
    grad_final = rows_high(pick.astype(WIDE), grad_chosen)
    grad_third, grad_gain = norm_back(third, scale_three, gain, grad_final)
    return (loss_part, grad_third, grad_gain, grad_table)


def layer_backward(hidden, grad_third, saved, dense_t, w_in, w_out, shards):
    gains, const_vec = saved["gains"], saved["const_vec"]
    router, const_gate = saved["router"], saved["const_gate"]
    tokens = hidden.shape[0]
    weight = saved["weight"]
    route_p = saved["route_p"]
    second_wide = saved["second_low"].astype(WIDE)
    w_slot, picks = saved["w_slot"], saved["picks"]
    grad_out = contract_rows(picks[0], (w_slot[:, 0:1] * grad_third).astype(LOWER))
    grad_out = grad_out + contract_rows(picks[1], (w_slot[:, 1:2] * grad_third).astype(LOWER))
    grad_out = grad_out.astype(LOWER).reshape(EXPERTS, CAP, D)
    grad_part = swap(fan_out(grad_out, shards), "dp").reshape(-1, D)
    gate_pre, up_pre = (saved["gate_pre"], saved["up_pre"])
    grad_inner = contract_cols(grad_part, w_out)
    sig = jax.nn.sigmoid(gate_pre)
    grad_gate = (grad_inner * up_pre * sig * (1.0 + gate_pre * (1.0 - sig))).astype(LOWER)
    grad_up = (grad_inner * gate_pre * sig).astype(LOWER)
    grad_rows = (contract_cols(grad_gate, w_in[0]) + contract_cols(grad_up, w_in[1])).astype(LOWER)
    came_back = swap(grad_rows.reshape(EXPERTS * shards, CAP, D), "dp")
    grad_w_out = contract_rows(saved["inner"], grad_part).astype(LOWER)
    grad_w_in = jnp.stack(
        [
            contract_rows(saved["rows"], grad_gate).astype(LOWER),
            contract_rows(saved["rows"], grad_up).astype(LOWER),
        ]
    )
    dots = [jnp.sum(saved["outs"][k] * grad_third, -1, keepdims=True) for k in range(2)]
    hits = saved["hits"].astype(WIDE)
    grad_real = (dots[0] * hits[:, 0] + dots[1] * hits[:, 1])[:, :EXPERTS]
    grad_copy = jnp.sum(grad_third * saved["second"], -1, keepdims=True)
    grad_const = jnp.sum(grad_third[:, None, :] * saved["const_out"], -1)
    grad_weight = jnp.concatenate(
        [grad_real, jnp.zeros((tokens, 1), WIDE), grad_copy, grad_const], 1
    )
    grad_p = grad_weight * saved["used"]
    grad_logit = route_p * (grad_p - jnp.sum(route_p * grad_p, -1, keepdims=True))
    const_p = saved["const_p"]
    w_const = weight[:, EXPERTS + 2 :]
    along_vec = jnp.dot(grad_third, const_vec.T, precision=HIGH)
    grad_alpha = w_const[:, :, None] * jnp.stack(
        [jnp.broadcast_to(grad_copy, along_vec.shape), along_vec], -1
    )
    grad_clog = (const_p * (grad_alpha - jnp.sum(const_p * grad_alpha, -1, keepdims=True))).reshape(
        tokens, 4
    )
    grad_cvec = rows_high(w_const * const_p[:, :, 1], grad_third)
    logit_all = jnp.concatenate([grad_logit, grad_clog], 1)
    grad_gates = rows_high(logit_all, second_wide)
    gates_all = jnp.concatenate([router, const_gate], 0).astype(WIDE)
    grad_second = jnp.dot(logit_all, gates_all, precision=HIGH)
    carry = weight[:, EXPERTS + 1 : EXPERTS + 2] + jnp.sum(
        w_const * const_p[:, :, 0], -1, keepdims=True
    )
    grad_second = grad_second + carry * grad_third
    grad_second = grad_second + pick_slots(saved["both"], came_back, shards)
    grad_first_norm, grad_gain_two = norm_back(
        saved["first"], saved["scale_two"], gains[1], grad_second
    )
    grad_first = grad_third + grad_first_norm
    grad_attn = grad_first.astype(LOWER)
    grad_wo = contract_rows(grad_attn, saved["mixed"])
    grad_mixed = plain(grad_attn, dense_t[3 * D :]).astype(LOWER).reshape(tokens, -1, HDIM)
    qkv = saved["qkv"]
    probs = jnp.exp(head_scores(qkv, saved["mask"]) - saved["lse"])
    grad_values = jnp.einsum(
        "hqk,qhd->khd", probs.astype(LOWER), grad_mixed, preferred_element_type=WIDE
    )
    grad_probs = jnp.einsum(
        "qhd,khd->hqk", grad_mixed, split_heads(qkv, 2), preferred_element_type=WIDE
    )
    grad_scores = (probs * (grad_probs - jnp.sum(probs * grad_probs, -1, keepdims=True))).astype(
        LOWER
    )
    grad_query = jnp.einsum(
        "hqk,khd->qhd", grad_scores, split_heads(qkv, 1), preferred_element_type=WIDE
    ) * HDIM ** (-0.5)
    grad_keys = jnp.einsum(
        "hqk,qhd->khd", grad_scores, split_heads(qkv, 0), preferred_element_type=WIDE
    ) * HDIM ** (-0.5)
    grad_qkv = jnp.concatenate(
        [
            grad_query.reshape(tokens, D),
            grad_keys.reshape(tokens, D),
            grad_values.reshape(tokens, D),
        ],
        1,
    ).astype(LOWER)
    grad_wqkv = contract_rows(grad_qkv, saved["normed_low"])
    grad_normed = plain(grad_qkv, dense_t[: 3 * D])
    unused, grad_gain_one = norm_back(hidden, saved["scale_one"], gains[0], grad_normed)
    dense_grad = jnp.concatenate([grad_wqkv, grad_wo], 0)
    return (dense_grad, grad_gain_one, grad_gain_two, grad_cvec, grad_gates, grad_w_in, grad_w_out)


def group_squares(arrays, device):
    dense, small, ein, eout, tab = arrays
    width = dense.shape[1]
    front = (device * width + jnp.arange(width, dtype=jnp.int32) < 3 * D).astype(WIDE)
    dense_sq = jnp.sum(dense * dense, 0)
    return jnp.stack(
        [
            jnp.sum(dense_sq * front),
            jnp.sum(dense_sq * (1.0 - front)),
            jnp.sum(small[:5] * small[:5]),
            jnp.sum(small[5:] * small[5:]),
            jnp.sum(ein * ein),
            jnp.sum(eout * eout),
            jnp.sum(tab * tab),
        ]
    )


def moments(weight, first, second, grad):
    first = 0.5 * first + 0.5 * grad
    second = 0.5 * second + 0.5 * grad * grad
    corr = 1.0 - 0.5**STEP
    update = first / corr / (jnp.sqrt(second / corr) + EPS) + 0.01 * weight
    return (first, second, update)


def local(
    x_in,
    seq_lens,
    routes,
    positions,
    targets,
    dense_w,
    small_w,
    expert_in,
    expert_out,
    table,
    dense_m,
    small_m,
    expin_m,
    expout_m,
    table_m,
    dense_v,
    small_v,
    expin_v,
    expout_v,
    table_v,
):
    n_dp, n_rep = lax.axis_size("dp"), lax.axis_size("rep")
    devices = n_dp * n_rep
    shards = n_dp // EXPERTS
    own = lax.axis_index("dp")
    device = own * n_rep + lax.axis_index("rep")
    masters = (dense_w, small_w, expert_in, expert_out, table)
    width, thin = dense_w.shape[1], small_w.shape[1]
    dense_t = lax.all_gather(dense_w.T.astype(LOWER), BOTH, axis=0, tiled=True)
    small_t = jnp.pad(small_w.T.astype(LOWER), ((0, 0), (0, LANES - small_w.shape[0])))
    small_all = share(small_t, BOTH, devices).reshape(-1, LANES).T
    w_in, w_out, table_all = (
        lax.all_gather(expert_in.astype(LOWER), "rep", axis=1, tiled=True),
        lax.all_gather(expert_out.astype(LOWER), "rep", axis=0, tiled=True),
        lax.all_gather(table.astype(LOWER), "rep", axis=0, tiled=True),
    )
    hidden = x_in.astype(WIDE)
    third, saved = layer_forward(
        hidden, seq_lens[0], routes, dense_t, small_all, w_in, w_out, shards
    )
    loss_part, grad_third, grad_gain_final, grad_table = head_step(
        third, positions, targets, table_all, saved["gains"][2], own, n_dp
    )
    table_g = lax.psum_scatter(grad_table, "rep", scatter_dimension=0, tiled=True)
    dense_grad, gain_one, gain_two, grad_cvec, grad_gates, grad_w_in, grad_w_out = layer_backward(
        hidden, grad_third, saved, dense_t, w_in, w_out, shards
    )
    ein_g, eout_g = (
        lax.psum_scatter(grad_w_in, "rep", scatter_dimension=1, tiled=True),
        lax.psum_scatter(grad_w_out, "rep", scatter_dimension=0, tiled=True),
    )
    small_grad = jnp.concatenate(
        [gain_one[None], gain_two[None], grad_gain_final[None], grad_cvec, grad_gates], 0
    )
    small_blocks = small_grad.reshape(-1, devices, thin).swapaxes(0, 1).reshape(devices, -1)
    extra = -(-small_blocks.shape[1] // (8 * D)) * 8 * D
    small_blocks = jnp.pad(small_blocks, ((0, 0), (0, extra - small_blocks.shape[1])))
    blocks = jnp.concatenate(
        [dense_grad.reshape(devices, width, D), small_blocks.reshape(devices, -1, D)], 1
    )
    block = scatter_sum(blocks.reshape((n_dp, n_rep) + blocks.shape[1:]), n_dp, n_rep)
    dense_g = block[:width].T
    small_g = block[width:].reshape(-1)[: small_w.size].reshape(small_w.shape)
    grads = (dense_g, small_g, ein_g.astype(WIDE), eout_g.astype(WIDE), table_g.astype(WIDE))
    firsts = (dense_m, small_m, expin_m, expout_m, table_m)
    seconds = (dense_v, small_v, expin_v, expout_v, table_v)
    results = [moments(w, m, v, g) for w, m, v, g in zip(masters, firsts, seconds, grads)]
    update_parts = group_squares(tuple((r[2] for r in results)), device)
    parts = jnp.concatenate([group_squares(masters, device), update_parts, loss_part[None]])
    parts = jnp.pad(parts, (0, 8 * LANES - parts.shape[0])).reshape(8, LANES)
    sums = jnp.sum(share(parts, BOTH, devices), 0).reshape(-1)
    loss = sums[14]
    weight_norm = jnp.sqrt(sums[:7])
    update_norm = jnp.sqrt(sums[7:14])
    trust = weight_norm / update_norm
    column = device * width + jnp.arange(width, dtype=jnp.int32)
    dense_scale = jnp.where(column < 3 * D, trust[0], trust[1])[None, :]
    small_scale = jnp.where(jnp.arange(21, dtype=jnp.int32) < 5, trust[2], trust[3])[:, None]
    scales = (dense_scale, small_scale, trust[4], trust[5], trust[6])
    outs = [loss, jnp.stack([weight_norm, update_norm, trust])]
    for w, r, factor in zip(masters, results, scales):
        fresh = w - 0.2 * factor * r[2]
        outs += [r[0], r[1], fresh, fresh.astype(LOWER)]
    return tuple(outs)


def solution(mesh):
    in_specs = (
        P(("dp", "rep"), None),
        P(("dp", "rep"), None),
        P(("dp", "rep"), None),
        P(("dp", "rep")),
        P("rep", None, None),
        P(None, ("dp", "rep")),
        P(None, ("dp", "rep")),
        P(None, "rep", "dp"),
        P(("dp", "rep"), None),
        P(("dp", "rep"), None),
        P(None, ("dp", "rep")),
        P(None, ("dp", "rep")),
        P(None, "rep", "dp"),
        P(("dp", "rep"), None),
        P(("dp", "rep"), None),
        P(None, ("dp", "rep")),
        P(None, ("dp", "rep")),
        P(None, "rep", "dp"),
        P(("dp", "rep"), None),
        P(("dp", "rep"), None),
    )
    out_specs = (
        P(),
        P(),
        P(None, ("dp", "rep")),
        P(None, ("dp", "rep")),
        P(None, ("dp", "rep")),
        P(None, ("dp", "rep")),
        P(None, ("dp", "rep")),
        P(None, ("dp", "rep")),
        P(None, ("dp", "rep")),
        P(None, ("dp", "rep")),
        P(None, "rep", "dp"),
        P(None, "rep", "dp"),
        P(None, "rep", "dp"),
        P(None, "rep", "dp"),
        P(("dp", "rep"), None),
        P(("dp", "rep"), None),
        P(("dp", "rep"), None),
        P(("dp", "rep"), None),
        P(("dp", "rep"), None),
        P(("dp", "rep"), None),
        P(("dp", "rep"), None),
        P(("dp", "rep"), None),
    )
    return jax.shard_map(local, mesh=mesh, in_specs=in_specs, out_specs=out_specs, check_vma=False)
```

time: 1090 us -> 780 us (0.72)
  waiting for transfers between devices: 400 us -> 237 us
  blocking collectives: 248 us -> 94 us
  other arithmetic: 138 us -> 158 us
  local copies, waits for them, and re-layouts: 62 us -> 44.2 us
  starting transfers between devices: 15.6 us -> 33 us
  matrix products: 198 us -> 184 us
    reduce_scatter x4 -> x3, waiting for transfers between devices: 159 us -> 0.01 us  [the longest x1 0.01 us: local(): lax.psum_scatter(grad_w_out, 'rep', scatter_dimension=0, tiled=True)]
    all_gather x4 -> x0, blocking collectives: 135 us -> none  [the longest x3 91.3 us: merged(): pieces = jax.tree.map(lambda part: lax.all_gather(part, axis), value)]
    all_gather x1, waiting for transfers between devices: 82.9 us -> 0.01 us  [local(): lax.all_gather(table.astype(LOWER), 'rep', axis=0, tiled=True)]
    ppermute x0 -> x5, waiting for transfers between devices: none -> 76.4 us  [halve(): take = lax.ppermute(give, axis, [(i, i ^ mask) for i in range(size)])]
    all_to_all x1 -> x4, blocking collectives: 31.1 us -> 94 us  [swap(): return lax.all_to_all(value, axis, split_axis=0, concat_axis=0, tiled=True)]
    all_to_all x3 -> x5, waiting for transfers between devices: 48.6 us -> 94.7 us  [swap(): return lax.all_to_all(value, axis, split_axis=0, concat_axis=0, tiled=True)]
    unnamed x1 -> x0, blocking collectives: 41.9 us -> none
    psum x1 -> x0, blocking collectives: 39.8 us -> none  [local(): lax.psum((group_squares(masters, device), update_parts, loss_part), ('dp'...]
  transfers between devices with their start and end apart: 13 -> 17, of which waited for: 11 -> 12; matrix products, arithmetic and copies ran while one was open for 21% -> 30% of each run, Pallas kernels for 0% -> 0%
where the time goes in v1:
time: 780 us; the launch traced here: 770 us
  waiting for transfers between devices  237 us (30%)
  matrix products  184 us (24%)
  other arithmetic  158 us (20%)
  blocking collectives  94 us (12%)
  local copies, waits for them, and re-layouts  44.2 us (6%)
  starting transfers between devices  33 us (4%)
  between operations  19 us (2%)
    all_to_all x5, waiting for transfers between devices, swap(): return lax.all_to_all(value, axis, split_axis=0, concat_axis=0, tiled=True)  94.7 us
    all_to_all x4, blocking collectives, swap(): return lax.all_to_all(value, axis, split_axis=0, concat_axis=0, tiled=True)  94 us
    ppermute x5, waiting for transfers between devices, halve(): take = lax.ppermute(give, axis, [(i, i ^ mask) for i in range(size)])  76.4 us
    dot_general x8, matrix products, contract_cols(): lax.dot_general(left, right, (((1,), (1,)), ((), ())), preferred_element_...  54.4 us
    dot_general x11, matrix products, plain(): return jnp.dot(left, right, preferred_element_type=WIDE)  53 us
    dot_general x9, matrix products, contract_rows(): lax.dot_general(left, right, (((0,), (0,)), ((), ())), preferred_element_...  45.6 us
    all_gather x1, waiting for transfers between devices, local(): dense_t = lax.all_gather(dense_w.T.astype(LOWER), BOTH, axis=0, tiled=True)  41.8 us
    all_to_all x5, starting transfers between devices, swap(): return lax.all_to_all(value, axis, split_axis=0, concat_axis=0, tiled=True)  26.4 us
  transfers between devices with their start and end apart: 17, of which 12 were waited for; matrix products, arithmetic and copies ran while one was open for 30% of the time, Pallas kernels for 0%

profile of v1, /device:TPU:0, one launch (start us, length us, event | category | flops | bytes accessed | tf_op | source)
XLA Modules:
  0.0 769.7 jit_solution(13017863282938023400)
XLA Ops:
  19.7 7.3 all-to-all-start
  31.2 6.2 all-to-all-done
  37.7 41.8 %all-gather.5.cloned.1.call-done = bf16[3072,768]{1,0:T(8,128)(2,1)} async-done(((bf16[96,768]{1,0:T(8,128)(2,1)}), bf16[3072,768]{1,0:T(8,128)(2,1)}) %all-gather.5.cloned.1.call-update) | async-done | bytes 4718608 | tf_op jit(solution)/shard_map/all_gather | solution.py:383
  109.1 17.7 %all-gather.7.cloned.1.call-done = bf16[2,768,2048]{2,1,0:T(8,128)(2,1)} async-done(((bf16[2,192,2048]{2,1,0:T(8,128)(2,1)}), bf16[2,768,2048]{2,1,0:T(8,128)(2,1)}) %all-gather.7.cloned.1.call-update) | async-done | bytes 6291472 | tf_op jit(solution)/shard_map/all_gather | solution.py:387
  126.8 9.2 %all-to-all-done.1 = bf16[8,96,768]{2,1,0:T(8,128)(2,1)} async-done(((bf16[8,96,768]{2,1,0:T(8,128)(2,1)}), bf16[8,96,768]{2,1,0:T(8,128)(2,1)}, u32[]{:S(2)}, u32[]{:S(2)}) %all-to-all-start.1) | async-done | bytes 1179680 | tf_op jit(solution)/shard_map/all_to_all | solution.py:39
  144.2 6.6 multiply_convert_fusion.4
  150.8 6.6 all-gather.9.cloned.1.call-done
  157.5 6.5 convolution_convert_fusion.6
  174.7 23.8 %all-to-all-done.2 = bf16[8,96,768]{2,1,0:T(8,128)(2,1)} async-done(((bf16[8,96,768]{2,1,0:T(8,128)(2,1)}), bf16[8,96,768]{2,1,0:T(8,128)(2,1)}, u32[]{:S(2)}, u32[]{:S(2)}) %all-to-all-start.2) | async-done | bytes 1179680 | tf_op jit(solution)/shard_map/all_to_all | solution.py:39
  211.5 36.6 %all-to-all-done.3 = bf16[8,128,768]{2,1,0:T(8,128)(2,1)} async-done(((bf16[8,128,768]{2,1,0:T(8,128)(2,1)}), bf16[8,128,768]{2,1,0:T(8,128)(2,1)}, u32[]{:S(2)}, u32[]{:S(2)}) %all-to-all-start.3) | async-done | bytes 1572896 | tf_op jit(solution)/shard_map/all_to_all | solution.py:39
  248.1 22.5 %fusion.132 = (f32[1024]{0:T(1024)S(1)}, f32[1024,8192]{1,0:T(8,128)}) fusion(bf16[1024,768]{1,0:T(8,128)(2,1)} %bitcast.34, bf16[8192,768]{1,0:T(8,128)(2,1)} %all-gather.11.cloned.1.call-done), kind=kOutput, calls=%fused_computation.291 | convolution fusion | flops 12893289472 | bytes 47714304 | tf_op jit(solution)/shard_map/dot_general | solution.py:27
  270.7 16.3 %exponential_reduce_fusion = (f32[1024]{0:T(1024)S(1)}, f32[1024]{0:T(1024)S(1)}) fusion(f32[1024,8192]{1,0:T(8,128)} %get-tuple-element.119, f32[1024]{0:T(1024)S(1)} %get-tuple-element.118, s32[1024]{0:T(1024)S(1)} %subtract_bitcast_fusion), kind=kLoop, calls=%fused_computation.3 | loop fusion | flops 41940992 | bytes 33570816 | tf_op jit(solution)/shard_map/reduce_sum | solution.py:216
  287.1 10.7 %all_to_all.45 = f32[8,24,128]{2,1,0:T(8,128)S(1)} all-to-all(f32[8,24,128]{2,1,0:T(8,128)S(1)} %broadcast_in_dim.166), channel_id=1, replica_groups=mesh['dp'=8,'rep'=4] {'dp'}, dimensions={0} | all-to-all | bytes 196608 | tf_op jit(solution)/shard_map/all_to_all | solution.py:39
  298.6 20.4 %multiply_convert_fusion = bf16[1024,8192]{1,0:T(8,128)(2,1)} fusion(f32[1024,8192]{1,0:T(8,128)} %get-tuple-element.119, f32[1024]{0:T(1024)S(1)} %get-tuple-element.59, s32[1024]{0:T(1024)S(1)} %subtract_bitcast_fusion), kind=kLoop, calls=%fused_computation | loop fusion | flops 50331648 | bytes 50339840 | tf_op jit(solution)/shard_map/convert_element_type | solution.py:225
  319.0 18.7 %convolution_convert_fusion.5 = bf16[1024,768]{1,0:T(8,128)(2,1)S(1)} fusion(bf16[1024,8192]{1,0:T(8,128)(2,1)} %multiply_convert_fusion, bf16[8192,768]{1,0:T(8,128)(2,1)} %all-gather.11.cloned.1.call-done), kind=kOutput, calls=%fused_computation.71 | convolution fusion | flops 12885688320 | bytes 30932992 | tf_op jit(solution)/shard_map/dot_general | solution.py:31
  337.7 38.5 %all_to_all.46 = bf16[8,128,768]{2,1,0:T(8,128)(2,1)S(1)} all-to-all(bf16[8,128,768]{2,1,0:T(8,128)(2,1)S(1)} %bitcast.252), channel_id=1, replica_groups=mesh['dp'=8,'rep'=4] {'dp'}, dimensions={0} | all-to-all | bytes 3145728 | tf_op jit(solution)/shard_map/all_to_all | solution.py:39
  382.6 32.0 %all_to_all.47 = bf16[8,96,768]{2,1,0:T(8,128)(2,1)S(1)} all-to-all(bf16[8,96,768]{2,1,0:T(8,128)(2,1)S(1)} %bitcast.241), channel_id=1, replica_groups=mesh['dp'=8,'rep'=4] {'dp'}, dimensions={0} | all-to-all | bytes 2359296 | tf_op jit(solution)/shard_map/all_to_all | solution.py:39
  419.8 9.5 %multiply_convert_fusion.2 = (bf16[768,2048]{1,0:T(8,128)(2,1)S(1)}, bf16[768,2048]{1,0:T(8,128)(2,1)S(1)}) fusion(f32[768,2048]{1,0:T(8,128)} %copy-done.88, f32[768,2048]{1,0:T(8,128)} %get-tuple-element.114, bf16[768,768]{1,0:T(8,128)(2,1)} %bitcast.256, bf16[2048,768]{1,0:T(8,128)(2,1)} %all-gather.9.cloned.1.call-done), kind=kOutput, calls=%fused_computation.23 | convolution fusion | flops 2436366336 | bytes 23199744 | tf_op jit(solution)/shard_map/dot_general | solution.py:27
  442.2 20.9 %convolution_convert_fusion = bf16[8192,768]{1,0:T(8,128)(2,1)} fusion(bf16[1024,8192]{1,0:T(8,128)(2,1)} %multiply_convert_fusion, bf16[1024,768]{1,0:T(8,128)(2,1)} %bitcast.34), kind=kOutput, calls=%fused_computation.4 | convolution fusion | flops 12891193344 | bytes 30932992 | tf_op jit(solution)/shard_map/dot_general | solution.py:23
  465.7 7.2 fusion.14
  490.7 18.8 %all-to-all-done.7 = bf16[8,96,768]{2,1,0:T(8,128)(2,1)} async-done(((bf16[8,96,768]{2,1,0:T(8,128)(2,1)}), bf16[8,96,768]{2,1,0:T(8,128)(2,1)}, u32[]{:S(2)}, u32[]{:S(2)}) %all-to-all-start.7) | async-done | bytes 1179680 | tf_op jit(solution)/shard_map/all_to_all | solution.py:39
  518.8 11.5 %multiply_reduce_fusion = (f32[12,512]{1,0:T(8,128)S(1)}, f32[12,512,512]{1,2,0:T(8,128)}) fusion(f32[12,512]{1,0:T(8,128)S(1)} %log_add_fusion, f32[12,512,512]{1,2,0:T(8,128)} %copy-done, pred[512,512]{0,1:T(8,128)(4,1)S(1)} %copy-done.16, bf16[512,12,64]{0,2,1:T(8,128)(2,1)S(1)} %bitcast.246, bf16[512,12,64]{0,2,1:T(8,128)(2,1)S(1)} %bitcast.245), kind=kOutput, calls=%fused_computation.6 | convolution fusion | flops 418375680 | bytes 27049984 | tf_op jit(solution)/shard_map/qhd,khd->hqk/dot_general | solution.py:301
  532.6 8.6 %multiply_convert_fusion.1 = bf16[12,512,512]{1,2,0:T(8,128)(2,1)S(1)} fusion(f32[12,512,512]{1,2,0:T(8,128)} %get-tuple-element.123, f32[12,512]{1,0:T(8,128)S(1)} %get-tuple-element.122, f32[12,512]{1,0:T(8,128)S(1)} %log_add_fusion, f32[12,512,512]{1,2,0:T(8,128)S(1)} %bitcast.227, pred[512,512]{0,1:T(8,128)(4,1)S(1)} %copy-done.16), kind=kLoop, calls=%fused_computation.5 | loop fusion | flops 18874368 | bytes 31768576 | tf_op jit(solution)/shard_map/convert_element_type | solution.py:304
  559.1 7.5 pad_maximum_fusion.1
  591.4 53.2 %collective-permute-done.1 = bf16[1,8,104,768]{3,2,1,0:T(8,128)(2,1)} collective-permute-done((bf16[1,8,104,768]{3,2,1,0:T(8,128)(2,1)S(1)}, bf16[1,8,104,768]{3,2,1,0:T(8,128)(2,1)}, u32[]{:S(2)}, u32[]{:S(2)}) %collective-permute-start.1) | collective-permute-done | bytes 1277984 | tf_op jit(solution)/shard_map/ppermute | solution.py:51
  648.6 14.7 %collective-permute-done.2 = bf16[4,104,768]{2,1,0:T(8,128)(2,1)} collective-permute-done((bf16[4,104,768]{2,1,0:T(8,128)(2,1)S(1)}, bf16[4,104,768]{2,1,0:T(8,128)(2,1)}, u32[]{:S(2)}, u32[]{:S(2)}) %collective-permute-start.2) | collective-permute-done | bytes 639008 | tf_op jit(solution)/shard_map/ppermute | solution.py:51
  679.1 6.3 multiply_reduce_fusion.6
  693.2 7.2 multiply_reduce_fusion.3
  700.4 13.2 %multiply_reduce_fusion.1 = (f32[]{:T(128)}, f32[]{:T(128)}, f32[2048,768]{1,0:T(8,128)}, f32[2048,768]{1,0:T(8,128)}) fusion(f32[2048,768]{1,0:T(8,128)} %param.29, bf16[2048,768]{1,0:T(8,128)(2,1)} %reduce-scatter.8.cloned.1.call-done, f32[2048,768]{1,0:T(8,128)} %param.34, f32[2048,768]{1,0:T(8,128)} %param.39), kind=kLoop, calls=%fused_computation.21 | loop fusion | flops 26738688 | bytes 34603016 | tf_op jit(solution)/shard_map/reduce_sum | solution.py:341
  713.6 9.0 %concatenate.55 = f32[15]{0:T(128)S(1)} concatenate(f32[1]{0:T(128)} %bitcast, f32[1]{0:T(128)} %bitcast.1, f32[1]{0:T(128)} %bitcast.2, f32[1]{0:T(128)} %bitcast.3, f32[1]{0:T(128)} %bitcast.4, f32[1]{0:T(128)} %bitcast.5, f32[1]{0:T(128)} %bitcast.6, f32[1]{0:T(128)} %bitcast.75, f32[1]{0:T(128)} %bitcast.76, f32[1]{0:T(128)} %bitcast.77, f32[1]{0:T(128)} %bitcast.78, ...), dimensions={0} | concatenate | bytes 120 | tf_op jit(solution)/shard_map/concatenate | solution.py:423
  722.7 12.7 %all_to_all.48 = f32[32,8,128]{2,1,0:T(8,128)} all-to-all(f32[32,8,128]{2,1,0:T(8,128)S(1)} %broadcast_in_dim.172), channel_id=1, replica_groups=mesh['dp'=8,'rep'=4] {'dp','rep'}, dimensions={0} | all-to-all | bytes 262144 | tf_op jit(solution)/shard_map/all_to_all | solution.py:39
  750.4 6.3 fusion.117
  (396 shorter events, 222.4 us)
Async XLA Ops:
  7.2 72.2 %all-gather.5.cloned.1.call-start = ((), (), s32[]{:S(2)}) async-start(), calls=%async_computation.12 | async-start | bytes 4866048 | tf_op jit(solution)/shard_map/all_gather | solution.py:383
  8.9 117.9 %all-gather.7.cloned.1.call-start = ((), (), s32[]{:S(2)}) async-start(), calls=%async_computation.13 | async-start | bytes 7864320 | tf_op jit(solution)/shard_map/all_gather | solution.py:387
  12.4 145.1 %all-gather.9.cloned.1.call-start = ((), (), s32[]{:S(2)}) async-start(), calls=%async_computation.14 | async-start | bytes 3932160 | tf_op jit(solution)/shard_map/all_gather | solution.py:388
  13.4 234.7 %all-gather.11.cloned.1.call-start = ((), (), s32[]{:S(2)}) async-start(), calls=%async_computation.15 | async-start | bytes 15728640 | tf_op jit(solution)/shard_map/all_gather | solution.py:389
  19.7 17.7 %all-to-all-start = ((bf16[32,24,128]{2,1,0:T(8,128)(2,1)}), bf16[32,24,128]{2,1,0:T(8,128)(2,1)S(1)}, u32[]{:S(2)}, u32[]{:S(2)}) async-start(bf16[32,24,128]{2,1,0:T(8,128)(2,1)} %broadcast_in_dim.86), calls=%async_computation | async-start | bytes 393216 | tf_op jit(solution)/shard_map/all_to_all | solution.py:39
  27.1 144.1 %copy-start.39 = (f32[512,12]{0,1:T(8,128)}, f32[512,12]{0,1:T(8,128)S(1)}, u32[]{:S(2)}) copy-start(f32[512,12]{0,1:T(8,128)S(1)} %convert_reduce_fusion.1) | copy-start | bytes 73732
  28.4 55.1 %copy-start.82 = (f32[512]{0:T(512)}, f32[512]{0:T(512)S(1)}, u32[]{:S(2)}) copy-start(f32[512]{0:T(512)S(1)} %add_rsqrt_fusion.2) | copy-start | bytes 6148
  28.4 352.2 %copy-start.74 = (s32[512,1]{0,1:T(1,128)}, s32[512,1]{0,1:T(1,128)S(1)}, u32[]{:S(2)}) copy-start(s32[512,1]{0,1:T(1,128)S(1)} %get-tuple-element.100) | copy-start | bytes 6148
  28.4 353.2 %copy-start.73 = (s32[512,1]{0,1:T(1,128)}, s32[512,1]{0,1:T(1,128)S(1)}, u32[]{:S(2)}) copy-start(s32[512,1]{0,1:T(1,128)S(1)} %get-tuple-element.101) | copy-start | bytes 6148
  31.2 58.1 %copy-start.15 = (pred[512,512]{0,1:T(8,128)(4,1)}, pred[512,512]{0,1:T(8,128)(4,1)S(1)}, u32[]{:S(2)}) copy-start(pred[512,512]{0,1:T(8,128)(4,1)S(1)} %fusion.41) | copy-start | bytes 786436
  37.6 41.8 %copy-start.41 = (bf16[768,128]{0,1:T(8,128)(2,1)}, bf16[768,128]{0,1:T(8,128)(2,1)S(1)}, u32[]{:S(2)}) copy-start(bf16[768,128]{0,1:T(8,128)(2,1)S(1)} %copy.127) | copy-start | bytes 589828
  37.6 45.9 %copy-start.79 = (f32[768]{0:T(1024)}, f32[768]{0:T(1024)S(1)}, u32[]{:S(2)}) copy-start(f32[768]{0:T(1024)S(1)} %get-tuple-element.43) | copy-start | bytes 9220
  99.3 73.4 %copy-start.6 = (f32[512,768]{1,0:T(8,128)}, f32[512,768]{1,0:T(8,128)S(1)}, u32[]{:S(2)}) copy-start(f32[512,768]{1,0:T(8,128)S(1)} %get-tuple-element.79) | copy-start | bytes 4718596
  102.2 33.8 %all-to-all-start.1 = ((bf16[8,96,768]{2,1,0:T(8,128)(2,1)}), bf16[8,96,768]{2,1,0:T(8,128)(2,1)}, u32[]{:S(2)}, u32[]{:S(2)}) async-start(bf16[8,96,768]{2,1,0:T(8,128)(2,1)} %bitcast.257), calls=%async_computation.1 | async-start | bytes 2359296 | tf_op jit(solution)/shard_map/all_to_all | solution.py:39
  107.6 65.1 %copy-start.62 = (f32[2,768]{1,0:T(2,128)}, f32[2,768]{1,0:T(2,128)S(1)}, u32[]{:S(2)}) copy-start(f32[2,768]{1,0:T(2,128)S(1)} %slice_convert_fusion.3) | copy-start | bytes 18436
  109.0 62.1 %copy-start.30 = (f32[512,12]{0,1:T(8,128)}, f32[512,12]{0,1:T(8,128)S(1)}, u32[]{:S(2)}) copy-start(f32[512,12]{0,1:T(8,128)S(1)} %get-tuple-element.116) | copy-start | bytes 73732
  109.1 62.1 %copy-start.64 = (f32[512]{0:T(512)}, f32[512]{0:T(512)S(1)}, u32[]{:S(2)}) copy-start(f32[512]{0:T(512)S(1)} %get-tuple-element.115) | copy-start | bytes 6148
  163.9 34.6 %all-to-all-start.2 = ((bf16[8,96,768]{2,1,0:T(8,128)(2,1)}), bf16[8,96,768]{2,1,0:T(8,128)(2,1)}, u32[]{:S(2)}, u32[]{:S(2)}) async-start(bf16[8,96,768]{2,1,0:T(8,128)(2,1)} %bitcast.254), calls=%async_computation.2 | async-start | bytes 2359296 | tf_op jit(solution)/shard_map/all_to_all | solution.py:39
  171.1 29.7 %copy-start.56 = (f32[512,4]{0,1:T(4,128)}, f32[512,4]{0,1:T(4,128)S(1)}, u32[]{:S(2)}) copy-start(f32[512,4]{0,1:T(4,128)S(1)} %fusion.90) | copy-start | bytes 24580
  171.1 29.7 %copy-start.45 = (f32[512,2,2]{0,2,1:T(2,128)}, f32[512,2,2]{0,2,1:T(2,128)S(1)}, u32[]{:S(2)}) copy-start(f32[512,2,2]{0,2,1:T(2,128)S(1)} %reshape.344) | copy-start | bytes 24580
  205.5 171.0 %copy-start.3 = (f32[512,768]{1,0:T(8,128)}, f32[512,768]{1,0:T(8,128)S(1)}, u32[]{:S(2)}) copy-start(f32[512,768]{1,0:T(8,128)S(1)} %get-tuple-element.73) | copy-start | bytes 4718596
  207.2 41.0 %all-to-all-start.3 = ((bf16[8,128,768]{2,1,0:T(8,128)(2,1)}), bf16[8,128,768]{2,1,0:T(8,128)(2,1)}, u32[]{:S(2)}, u32[]{:S(2)}) async-start(bf16[8,128,768]{2,1,0:T(8,128)(2,1)} %broadcast_in_dim.100), calls=%async_computation.3 | async-start | bytes 3145728 | tf_op jit(solution)/shard_map/all_to_all | solution.py:39
  211.4 467.7 %reduce-scatter.6.cloned.1.call-start = ((), (), s32[]{:S(2)}) async-start(), calls=%async_computation.17 | async-start | bytes 3932160 | tf_op jit(solution)/shard_map/reduce_scatter | solution.py:404
  381.6 34.1 %copy-start.92 = (bf16[768,2048]{1,0:T(8,128)(2,1)S(1)}, bf16[768,2048]{1,0:T(8,128)(2,1)}, u32[]{:S(2)}) copy-start(bf16[768,2048]{1,0:T(8,128)(2,1)} %get-tuple-element.113) | copy-start | bytes 9437188
  419.8 273.5 %reduce-scatter.4.cloned.1.call-start = ((), (), s32[]{:S(2)}) async-start(), calls=%async_computation.16 | async-start | bytes 7864320 | tf_op jit(solution)/shard_map/reduce_scatter | solution.py:403
  442.1 258.3 %reduce-scatter.8.cloned.1.call-start = ((), (), s32[]{:S(2)}) async-start(), calls=%async_computation.18 | async-start | bytes 15728640 | tf_op jit(solution)/shard_map/reduce_scatter | solution.py:398
  478.5 31.0 %all-to-all-start.7 = ((bf16[8,96,768]{2,1,0:T(8,128)(2,1)}), bf16[8,96,768]{2,1,0:T(8,128)(2,1)}, u32[]{:S(2)}, u32[]{:S(2)}) async-start(bf16[8,96,768]{2,1,0:T(8,128)(2,1)} %bitcast.253), calls=%async_computation.7 | async-start | bytes 2359296 | tf_op jit(solution)/shard_map/all_to_all | solution.py:39
  579.2 5.0 collective-permute-start
  590.8 53.8 %collective-permute-start.1 = (bf16[1,8,104,768]{3,2,1,0:T(8,128)(2,1)S(1)}, bf16[1,8,104,768]{3,2,1,0:T(8,128)(2,1)}, u32[]{:S(2)}, u32[]{:S(2)}) collective-permute-start(bf16[1,8,104,768]{3,2,1,0:T(8,128)(2,1)S(1)} %dynamic-slice_convert_fusion.1), channel_id=1, source_target_pairs={{0,2},{1,3},{2,0},{3,1},{4,6},{5,7},{6,4},{7,5},{8,10},{9,11},{10,... | collective-permute-start | bytes 3833864 | tf_op jit(solution)/shard_map/ppermute | solution.py:51
  647.0 16.2 %collective-permute-start.2 = (bf16[4,104,768]{2,1,0:T(8,128)(2,1)S(1)}, bf16[4,104,768]{2,1,0:T(8,128)(2,1)}, u32[]{:S(2)}, u32[]{:S(2)}) collective-permute-start(bf16[4,104,768]{2,1,0:T(8,128)(2,1)S(1)} %fusion.61), channel_id=1, source_target_pairs={{0,4},{4,0},{8,12},{12,8},{16,20},{20,16},{24,28},{28,24},{1,5},{5... | collective-permute-start | bytes 1916936 | tf_op jit(solution)/shard_map/ppermute | solution.py:51
  665.6 8.4 %collective-permute-start.3 = (bf16[2,104,768]{2,1,0:T(8,128)(2,1)S(1)}, bf16[2,104,768]{2,1,0:T(8,128)(2,1)S(1)}, u32[]{:S(2)}, u32[]{:S(2)}) collective-permute-start(bf16[2,104,768]{2,1,0:T(8,128)(2,1)S(1)} %fusion.64), channel_id=1, source_target_pairs={{0,8},{4,12},{8,0},{12,4},{16,24},{20,28},{24,16},{28,20},{1,9},{5... | collective-permute-start | bytes 958472 | tf_op jit(solution)/shard_map/ppermute | solution.py:51
  676.7 8.7 %collective-permute-start.4 = (bf16[1,104,768]{2,1,0:T(8,128)(2,1)}, bf16[1,104,768]{2,1,0:T(8,128)(2,1)}, u32[]{:S(2)}, u32[]{:S(2)}) collective-permute-start(bf16[1,104,768]{2,1,0:T(8,128)(2,1)} %dynamic-slice_convert_fusion.4), channel_id=1, source_target_pairs={{0,16},{4,20},{8,24},{12,28},{16,0},{20,4},{24,8},{28,12},{1,17},{... | collective-permute-start | bytes 479240 | tf_op jit(solution)/shard_map/ppermute | solution.py:51
  (87 other events, 642.1 us)
Sparse Core Ops, SparseCore 0:
  11.5 67.8 all-gather.4
  81.6 45.1 all-gather.6
  128.9 28.5 all-gather.8
  159.5 82.0 all-gather.10
  419.9 35.6 reduce-scatter.5
  458.7 58.3 reduce-scatter.3
  519.7 122.6 reduce-scatter.7

commit v2 on v1

v2 whole, which is shorter than its diff:
```python
import functools

import jax
import jax.numpy as jnp
from jax import lax
from jax.experimental import pallas as pl
from jax.experimental.pallas import tpu as pltpu
from jax.sharding import PartitionSpec as P

D = 768
HDIM = 64
EXPERTS = 8
NULLS = 4
STEP = 5
CAP = 96


EPS = 1e-06
HIGH = lax.Precision.HIGHEST
LOWER = jnp.bfloat16
WIDE = jnp.float32
BOTH = ("dp", "rep")
LANES = 128
MOST_FLIPS = 8
ROWS = 256
VMEM_BYTES = 48 << 20


def contract_rows(left, right):
    return lax.dot_general(left, right, (((0,), (0,)), ((), ())), preferred_element_type=WIDE)


def contract_cols(left, right):
    return lax.dot_general(left, right, (((1,), (1,)), ((), ())), preferred_element_type=WIDE)


def plain(left, right):
    return jnp.dot(left, right, preferred_element_type=WIDE)


def rows_high(left, right):
    return lax.dot_general(left, right, (((0,), (0,)), ((), ())), precision=HIGH)


def swap(value, axis):
    return lax.all_to_all(value, axis, split_axis=0, concat_axis=0, tiled=True)


def share(value, axis, count):
    return swap(jnp.broadcast_to(value[None], (count,) + value.shape), axis)


def flip(value, axis, mask, size):
    return lax.ppermute(value, axis, [(i, i ^ mask) for i in range(size)])


def by_distance(value, own):
    shape = value.shape
    mask = 1
    while mask < shape[0]:
        pairs = value.reshape((shape[0] // (2 * mask), 2, mask) + shape[1:])
        value = jnp.where((own & mask) != 0, jnp.flip(pairs, 1), pairs).reshape(shape)
        mask *= 2
    return value


def trade(blocks, n_dp):
    if n_dp > MOST_FLIPS:
        own = lax.axis_index("dp")
        return list(by_distance(swap(by_distance(jnp.stack(blocks), own), "dp"), own))
    half = n_dp // 2
    far = [flip(blocks[m], "dp", m, n_dp) for m in range(half, n_dp)]
    return blocks[:1] + [flip(blocks[m], "dp", m, n_dp) for m in range(1, half)] + far


def gather_flips(block, n_dp):
    half = n_dp // 2
    if n_dp > MOST_FLIPS:
        pieces = list(by_distance(lax.all_gather(block, "dp"), lax.axis_index("dp")))
        return pieces[:half], pieces[half:]
    cross = flip(block, "dp", half, n_dp)
    near = [block] + [flip(block, "dp", m, n_dp) for m in range(1, half)]
    far = [cross] + [flip(cross, "dp", m, n_dp) for m in range(1, half)]
    return near, far


def sum_flips(parts, n_dp):
    half = n_dp // 2
    if n_dp > MOST_FLIPS:
        pieces = by_distance(jnp.stack(parts).astype(LOWER), lax.axis_index("dp"))
        return jnp.sum(swap(pieces, "dp").astype(WIDE), 0)
    aims = [flip(parts[half + m].astype(LOWER), "dp", m, n_dp) for m in range(1, half)]
    across = sum([a.astype(WIDE) for a in aims], parts[half].astype(WIDE)).astype(LOWER)
    cross = flip(across, "dp", half, n_dp)
    near = [flip(parts[m].astype(LOWER), "dp", m, n_dp) for m in range(1, half)]
    total = sum([a.astype(WIDE) for a in near], parts[0].astype(WIDE))
    return total + cross.astype(WIDE)


def halve(buffer, axis, mask, size):
    own = (lax.axis_index(axis) & mask) // mask
    halves = buffer.reshape((buffer.shape[0] // 2, 2) + buffer.shape[1:])
    keep = lax.dynamic_index_in_dim(halves, own, 1, keepdims=False)
    give = lax.dynamic_index_in_dim(halves, 1 - own, 1, keepdims=False).astype(LOWER)
    take = lax.ppermute(give, axis, [(i, i ^ mask) for i in range(size)])
    return keep + take.astype(WIDE)


def scatter_sum(blocks, n_dp, n_rep):
    value = blocks.swapaxes(0, 1)
    mask = 1
    while mask < n_rep:
        value = halve(value, "rep", mask, n_rep)
        mask *= 2
    value = value[0]
    mask = 1
    while mask < n_dp:
        value = halve(value, "dp", mask, n_dp)
        mask *= 2
    return value[0]


def pack_body(dense_ref, small_ref, out_ref):
    width = dense_ref.shape[1]
    rows, thin = small_ref.shape
    out_ref[:width, :] = dense_ref[...].T.astype(LOWER)
    out_ref[width:, :] = jnp.zeros((8, D), LOWER)
    turned = small_ref[...].T.astype(LOWER)
    for g in range(thin // 8):
        out_ref[width:, g * LANES : g * LANES + rows] = turned[g * 8 : g * 8 + 8, :]


def pack(dense_w, small_w):
    return pl.pallas_call(
        pack_body,
        out_shape=jax.ShapeDtypeStruct((dense_w.shape[1] + 8, D), LOWER),
        compiler_params=pltpu.CompilerParams(vmem_limit_bytes=VMEM_BYTES),
        name="pack",
    )(dense_w, small_w)


def assemble_body(place_ref, *refs, n_dp, width, thin):
    pieces = refs[: 2 * n_dp]
    dense_ref, small_ref, raw_ref, turned_ref, dense_sem, small_sem = refs[2 * n_dp :]
    own, rep = place_ref[0], place_ref[1]
    copies = []
    for m in range(n_dp):
        for pair in range(2):
            for core in range(2):
                piece = pieces[core * n_dp + m]
                device = (own ^ m) * 4 + (rep ^ (2 * pair + core))
                top = pair * (width + 8)
                number = m * 4 + pair * 2 + core
                copies.append(
                    pltpu.make_async_copy(
                        piece.at[pl.ds(top + width, 8), :],
                        raw_ref.at[device],
                        small_sem.at[number],
                    )
                )
                copies.append(
                    pltpu.make_async_copy(
                        piece.at[pl.ds(top, width), :],
                        dense_ref.at[device],
                        dense_sem.at[number],
                    )
                )
    for copy in copies:
        copy.start()
    for copy in copies[::2]:
        copy.wait()
    for device in range(4 * n_dp):
        for g in range(thin // 8):
            start = device * thin + g * 8
            tile = raw_ref[device, :, g * LANES : (g + 1) * LANES]
            turned_ref[start : start + 8, :] = tile.astype(WIDE)
    small_ref[...] = turned_ref[...].T[: small_ref.shape[0], :]
    for copy in copies[1::2]:
        copy.wait()


def assemble(pieces, place, n_dp, width, thin):
    return pl.pallas_call(
        functools.partial(assemble_body, n_dp=n_dp, width=width, thin=thin),
        in_specs=[pl.BlockSpec(memory_space=pltpu.SMEM)]
        + [pl.BlockSpec(memory_space=pl.ANY)] * len(pieces),
        out_specs=[
            pl.BlockSpec(memory_space=pl.ANY),
            pl.BlockSpec(memory_space=pltpu.VMEM),
        ],
        out_shape=[
            jax.ShapeDtypeStruct((4 * n_dp, width, D), LOWER),
            jax.ShapeDtypeStruct((24, D), WIDE),
        ],
        scratch_shapes=[
            pltpu.VMEM((4 * n_dp, 8, D), LOWER),
            pltpu.VMEM((4 * n_dp * thin, LANES), WIDE),
            pltpu.SemaphoreType.DMA((4 * n_dp,)),
            pltpu.SemaphoreType.DMA((4 * n_dp,)),
        ],
        compiler_params=pltpu.CompilerParams(vmem_limit_bytes=VMEM_BYTES),
        name="assemble",
    )(place, *pieces)


def gather_weights(dense_w, small_w, place, n_dp):
    width, thin = dense_w.shape[1], small_w.shape[1]
    block = pack(dense_w, small_w)
    both = jnp.concatenate([block, flip(block, "rep", 2, 4)])
    near, far = gather_flips(both, n_dp)
    mine = near + far
    theirs = [flip(piece, "rep", 1, 4) for piece in mine]
    dense, small = assemble(mine + theirs, place, n_dp, width, thin)
    return dense.reshape(-1, D), small


def dense_grad_body(
    place_ref, qkv_ref, attn_ref, normed_ref, mixed_ref, small_ref, mine_ref, other_ref, sum_ref
):
    j = pl.program_id(0)
    width, thin = mine_ref.shape[2] - 8, small_ref.shape[0] // (4 * pl.num_programs(0))
    front = 3 * D // (4 * width)

    @pl.when(j < front)
    def _():
        sum_ref[...] = contract_rows(qkv_ref[...], normed_ref[...])

    @pl.when(j >= front)
    def _():
        sum_ref[...] = contract_rows(attn_ref[...], mixed_ref[...])

    rep = place_ref[1]
    for pair in range(2):
        for core, out_ref in enumerate((mine_ref, other_ref)):
            r = rep ^ (2 * pair + core)
            rows = pl.multiple_of(r * width, 8)
            out_ref[0, pair, :width, :] = sum_ref[pl.ds(rows, width), :].astype(out_ref.dtype)
            out_ref[0, pair, width:, :] = jnp.zeros((8, D), out_ref.dtype)
            for g in range(thin // 8):
                start = pl.multiple_of((j * 4 + r) * thin + g * 8, 8)
                tile = small_ref[pl.ds(start, 8), :].astype(out_ref.dtype)
                out_ref[0, pair, width:, g * LANES : (g + 1) * LANES] = tile


def dense_grads(place, grad_qkv, grad_attn, normed, mixed, small_turned, n_dp, width):
    tokens = grad_qkv.shape[0]
    wide = 4 * width
    front = 3 * D // wide
    block = (1, 2, width + 8, D)
    whole = lambda shape: pl.BlockSpec(shape, lambda j, place: (0, 0))
    out_spec = pl.BlockSpec(block, lambda j, place: (j ^ place[0], 0, 0, 0))
    return pl.pallas_call(
        dense_grad_body,
        grid_spec=pltpu.PrefetchScalarGridSpec(
            num_scalar_prefetch=1,
            grid=(n_dp,),
            in_specs=[
                pl.BlockSpec((tokens, wide), lambda j, place: (0, jnp.minimum(j, front - 1))),
                pl.BlockSpec((tokens, wide), lambda j, place: (0, jnp.maximum(j - front, 0))),
                whole((tokens, D)),
                whole((tokens, D)),
                whole(small_turned.shape),
            ],
            out_specs=[out_spec, out_spec],
            scratch_shapes=[pltpu.VMEM((wide, D), WIDE)],
        ),
        out_shape=[
            jax.ShapeDtypeStruct((n_dp,) + block[1:], WIDE),
            jax.ShapeDtypeStruct((n_dp,) + block[1:], LOWER),
        ],
        compiler_params=pltpu.CompilerParams(vmem_limit_bytes=VMEM_BYTES),
        name="dense_grads",
    )(place, grad_qkv, grad_attn, normed, mixed, small_turned)


def sum_weights(mine, other, n_dp):
    both = mine + flip(other, "rep", 1, 4).astype(WIDE)
    pair = sum_flips([both[m] for m in range(n_dp)], n_dp)
    return pair[0] + flip(pair[1].astype(LOWER), "rep", 2, 4).astype(WIDE)


def norm_fwd(hidden, gain):
    scale = lax.rsqrt(jnp.mean(hidden * hidden, -1, keepdims=True) + EPS)
    return (hidden * scale * gain, scale)


def norm_back(hidden, scale, gain, grad_out):
    normed = hidden * scale
    grad_gain = jnp.sum(grad_out * normed, 0)
    inner = grad_out * gain
    grad_in = scale * (inner - normed * jnp.mean(inner * normed, -1, keepdims=True))
    return (grad_in, grad_gain)


def segments(lens, tokens):
    place = jnp.arange(tokens, dtype=jnp.int32)
    ends = [jnp.sum(lens[: i + 1]) for i in range(lens.shape[0])]
    return sum((place >= end).astype(jnp.int32) for end in ends)


def build_bias(bias_ref, key_dim):
    shape = bias_ref.shape
    query = lax.broadcasted_iota(jnp.int32, shape, 1 - key_dim)
    key = lax.broadcasted_iota(jnp.int32, shape, key_dim)
    return key <= query


def lane_masks():
    lane = lax.broadcasted_iota(jnp.int32, (1, 2 * HDIM), 1)
    low = (lane < HDIM).astype(WIDE)
    return (low.astype(LOWER), (1.0 - low).astype(LOWER))


def attend_body(seg_col, seg_row, q_ref, k_ref, v_ref, out_ref, bias_ref):
    tokens = q_ref.shape[0]

    @pl.when(pl.program_id(0) == 0)
    def _():
        counts = build_bias(bias_ref, 1) & (seg_col[...] == seg_row[...])
        bias_ref[...] = jnp.where(counts, 0.0, -1e30)

    masks = lane_masks()
    for start in range(0, tokens, ROWS):
        keys = start + ROWS
        k = k_ref[:keys, :]
        v = v_ref[:keys, :]
        q = q_ref[start : start + ROWS, :]
        acc = jnp.zeros((ROWS, 2 * HDIM), WIDE)
        for mine in masks:
            scores = contract_cols(q * mine, k) * HDIM ** (-0.5)
            scores = scores + bias_ref[start : start + ROWS, :keys]
            expo = jnp.exp(scores - jnp.max(scores, -1, keepdims=True))
            total = jnp.sum(expo, -1, keepdims=True)
            probs = (expo * (1.0 / total)).astype(LOWER)
            acc = acc + plain(probs, v * mine)
        out_ref[start : start + ROWS, :] = acc.astype(LOWER)


def head_specs(tokens, first):
    return [
        pl.BlockSpec((tokens, 2 * HDIM), lambda j, base=base: (0, base + j)) for base in first
    ]


def attend(qkv, segment):
    tokens = qkv.shape[0]
    pairs = D // (2 * HDIM)
    return pl.pallas_call(
        attend_body,
        grid=(pairs,),
        in_specs=[
            pl.BlockSpec((tokens, 1), lambda j: (0, 0)),
            pl.BlockSpec((1, tokens), lambda j: (0, 0)),
        ]
        + head_specs(tokens, (0, pairs, 2 * pairs)),
        out_specs=pl.BlockSpec((tokens, 2 * HDIM), lambda j: (0, j)),
        out_shape=jax.ShapeDtypeStruct((tokens, D), LOWER),
        scratch_shapes=[pltpu.VMEM((tokens, tokens), WIDE)],
        compiler_params=pltpu.CompilerParams(vmem_limit_bytes=VMEM_BYTES),
        name="attend",
    )(segment[:, None], segment[None, :], qkv, qkv, qkv)


def attend_back_body(seg_col, seg_row, q_ref, k_ref, v_ref, do_ref, out_ref, bias_ref):
    tokens = q_ref.shape[0]
    step = pl.program_id(0)

    @pl.when(step == 0)
    def _():
        counts = build_bias(bias_ref, 0) & (seg_col[...] == seg_row[...])
        bias_ref[...] = jnp.where(counts, 0.0, -1e30)

    masks = lane_masks()
    scale = HDIM ** (-0.5)
    grad_k = [jnp.zeros((ROWS, 2 * HDIM), WIDE) for _ in range(tokens // ROWS)]
    grad_v = [jnp.zeros((ROWS, 2 * HDIM), WIDE) for _ in range(tokens // ROWS)]
    col = pl.multiple_of(step * 2 * HDIM, 2 * HDIM)
    for block, start in enumerate(range(0, tokens, ROWS)):
        keys = start + ROWS
        k = k_ref[:keys, :]
        v = v_ref[:keys, :]
        q = q_ref[start : start + ROWS, :]
        do = do_ref[start : start + ROWS, :]
        grad_q = jnp.zeros((ROWS, 2 * HDIM), WIDE)
        for mine in masks:
            q_own = q * mine
            do_own = do * mine
            scores = contract_cols(k, q_own) * scale + bias_ref[:keys, start : start + ROWS]
            expo = jnp.exp(scores - jnp.max(scores, 0, keepdims=True))
            total = jnp.sum(expo, 0, keepdims=True)
            probs = expo * (1.0 / total)
            grad_p = contract_cols(v, do_own)
            inner = jnp.sum(probs * grad_p, 0, keepdims=True)
            grad_s = (probs * (grad_p - inner)).astype(LOWER)
            grad_q = grad_q + contract_rows(grad_s, k * mine)
            into_v = plain(probs.astype(LOWER), do_own)
            into_k = plain(grad_s, q_own)
            for b in range(block + 1):
                grad_v[b] = grad_v[b] + into_v[b * ROWS : (b + 1) * ROWS]
                grad_k[b] = grad_k[b] + into_k[b * ROWS : (b + 1) * ROWS]
        out_ref[start : start + ROWS, pl.ds(col, 2 * HDIM)] = (grad_q * scale).astype(LOWER)
    for b in range(tokens // ROWS):
        rows = slice(b * ROWS, (b + 1) * ROWS)
        out_ref[rows, pl.ds(D + col, 2 * HDIM)] = (grad_k[b] * scale).astype(LOWER)
        out_ref[rows, pl.ds(2 * D + col, 2 * HDIM)] = grad_v[b].astype(LOWER)


def attend_back(qkv, grad_mixed, segment):
    tokens = qkv.shape[0]
    pairs = D // (2 * HDIM)
    return pl.pallas_call(
        attend_back_body,
        grid=(pairs,),
        in_specs=[
            pl.BlockSpec((tokens, 1), lambda j: (0, 0)),
            pl.BlockSpec((1, tokens), lambda j: (0, 0)),
        ]
        + head_specs(tokens, (0, pairs, 2 * pairs))
        + head_specs(tokens, (0,)),
        out_specs=pl.BlockSpec((tokens, 3 * D), lambda j: (0, 0)),
        out_shape=jax.ShapeDtypeStruct((tokens, 3 * D), LOWER),
        scratch_shapes=[pltpu.VMEM((tokens, tokens), WIDE)],
        compiler_params=pltpu.CompilerParams(vmem_limit_bytes=VMEM_BYTES),
        name="attend_back",
    )(segment[:, None], segment[None, :], qkv, qkv, qkv, grad_mixed)


def experts_forward(rows, w_in, w_out):
    gate_pre = plain(rows, w_in[0])
    up_pre = plain(rows, w_in[1])
    inner = (jax.nn.silu(gate_pre) * up_pre).astype(LOWER)
    part = plain(inner, w_out).astype(LOWER)
    return gate_pre, up_pre, inner, part


def experts_backward(grad_part, gate_pre, up_pre, w_in, w_out):
    grad_inner = contract_cols(grad_part, w_out)
    sig = jax.nn.sigmoid(gate_pre)
    grad_gate = (grad_inner * up_pre * sig * (1.0 + gate_pre * (1.0 - sig))).astype(LOWER)
    grad_up = (grad_inner * gate_pre * sig).astype(LOWER)
    grad_rows = (contract_cols(grad_gate, w_in[0]) + contract_cols(grad_up, w_in[1])).astype(LOWER)
    return grad_gate, grad_up, grad_rows


def cut(value, count):
    size = value.shape[0] // count
    return [value[i * size : (i + 1) * size] for i in range(count)]


def send_slots(buffer, n_dp, shards):
    half = n_dp // 2
    blocks = trade([b for b in cut(buffer, EXPERTS) for _ in range(shards)], n_dp)
    return jnp.concatenate(blocks[:half]), jnp.concatenate(blocks[half:])


def return_slots(near, far, n_dp, shards):
    half = n_dp // 2
    blocks = trade(cut(near, half) + cut(far, half), n_dp)
    return [jnp.concatenate(blocks[s::shards]) for s in range(shards)]


def pick_slots(picks, received):
    return sum(plain(picks, part) for part in received)


def layer_forward(hidden, lens, routes, dense_t, small_all, w_in, w_out, own, n_dp):
    shards = n_dp // EXPERTS
    gains, const_vec, router, const_gate = (
        small_all[:3].astype(WIDE),
        small_all[3:5].astype(WIDE),
        small_all[5:17].astype(LOWER),
        small_all[17:21].astype(LOWER),
    )
    tokens = hidden.shape[0]
    segment = segments(lens, tokens)
    normed, scale_one = norm_fwd(hidden, gains[0])
    normed_low = normed.astype(LOWER)
    qkv = contract_cols(normed_low, dense_t[: 3 * D]).astype(LOWER)
    mixed = attend(qkv, segment)
    first = hidden + contract_cols(mixed, dense_t[3 * D :])
    second, scale_two = norm_fwd(first, gains[1])
    second_low = second.astype(LOWER)
    route_p = jax.nn.softmax(contract_cols(second_low, router), -1)
    hits = routes[:, :, None] == jnp.arange(EXPERTS + NULLS, dtype=jnp.int32)[None, None, :]
    used = jnp.sum(hits.astype(WIDE), 1)
    weight = route_p * used
    earlier = jnp.tril(jnp.ones((tokens, tokens), LOWER), -1)
    rank = plain(earlier, used[:, :EXPERTS].astype(LOWER)).astype(jnp.int32)
    apart = jnp.arange(EXPERTS, dtype=jnp.int32) ^ (own // shards)
    place = apart[None] * CAP + rank
    place = jnp.where(rank < CAP, place, -1)
    real_hits = hits[:, :, :EXPERTS]
    slot = jnp.max(jnp.where(real_hits, place[:, None, :], -1), -1)
    w_slot = jnp.sum(jnp.where(real_hits, weight[:, None, :EXPERTS], 0.0), -1)
    all_slots = jnp.arange(EXPERTS * CAP, dtype=jnp.int32)
    picks = [(slot[:, k : k + 1] == all_slots[None]).astype(LOWER) for k in range(2)]
    both = picks[0] + picks[1]
    buffer = contract_rows(both, second_low).astype(LOWER)
    sent = send_slots(buffer, n_dp, shards)
    near, far = (experts_forward(rows, w_in, w_out) for rows in sent)
    returned = return_slots(near[3], far[3], n_dp, shards)
    outs = [pick_slots(picks[k], returned) for k in range(2)]
    moe = w_slot[:, 0:1] * outs[0] + w_slot[:, 1:2] * outs[1]
    const_p = jax.nn.softmax(contract_cols(second_low, const_gate).reshape(tokens, 2, 2), -1)
    const_out = const_p[:, :, 0:1] * second[:, None, :] + const_p[:, :, 1:2] * const_vec[None]
    moe = moe + weight[:, EXPERTS + 1 : EXPERTS + 2] * second
    moe = (
        moe
        + weight[:, EXPERTS + 2 : EXPERTS + 3] * const_out[:, 0]
        + weight[:, EXPERTS + 3 :] * const_out[:, 1]
    )
    third = first + moe
    saved = dict(
        gains=gains,
        const_vec=const_vec,
        router=router,
        const_gate=const_gate,
        segment=segment,
        scale_one=scale_one,
        normed_low=normed_low,
        qkv=qkv,
        mixed=mixed,
        first=first,
        second=second,
        scale_two=scale_two,
        second_low=second_low,
        route_p=route_p,
        hits=hits,
        used=used,
        weight=weight,
        w_slot=w_slot,
        picks=picks,
        both=both,
        rows=sent,
        near=near,
        far=far,
        outs=outs,
        const_p=const_p,
        const_out=const_out,
    )
    return (third, saved)


def vocab_tile(rows):
    return min(1024, (1 << 20) // rows)


def scores_body(aim_ref, rows_ref, table_ref, expo_ref, tops_ref, stats_ref, *, step_rows):
    tile = table_ref.shape[0]
    j = pl.program_id(0)

    @pl.when(j == 0)
    def _():
        stats_ref[0:1, :] = jnp.full((1, stats_ref.shape[1]), -1e30, WIDE)
        stats_ref[1:8, :] = jnp.zeros((7, stats_ref.shape[1]), WIDE)

    table = table_ref[...]
    for start in range(0, rows_ref.shape[0], step_rows):
        cols = slice(start, start + step_rows)
        logits = contract_cols(table, rows_ref[cols, :])
        top = jnp.max(logits, 0, keepdims=True)
        expo = jnp.exp(logits - top)
        expo_ref[:, cols] = expo.astype(LOWER)
        total = jnp.sum(expo, 0, keepdims=True)
        place = lax.broadcasted_iota(jnp.int32, logits.shape, 0)
        hit = place == aim_ref[:, cols] - j * tile
        aimed = jnp.sum(jnp.where(hit, logits, 0.0), 0, keepdims=True)
        tops_ref[0, :, cols] = top
        old = stats_ref[0:1, cols]
        high = jnp.maximum(old, top)
        stats_ref[1:2, cols] = stats_ref[1:2, cols] * jnp.exp(old - high) + total * jnp.exp(
            top - high
        )
        stats_ref[0:1, cols] = high
        stats_ref[2:3, cols] = stats_ref[2:3, cols] + aimed


def vocab_scores(rows, table, aim):
    count, vocab = rows.shape[0], table.shape[0]
    tile = vocab_tile(count)
    steps = vocab // tile
    return pl.pallas_call(
        functools.partial(scores_body, step_rows=ROWS),
        grid=(steps,),
        in_specs=[
            pl.BlockSpec((1, count), lambda j: (0, 0)),
            pl.BlockSpec((count, D), lambda j: (0, 0)),
            pl.BlockSpec((tile, D), lambda j: (j, 0)),
        ],
        out_specs=[
            pl.BlockSpec((tile, count), lambda j: (j, 0)),
            pl.BlockSpec((1, 1, count), lambda j: (j, 0, 0)),
            pl.BlockSpec((8, count), lambda j: (0, 0)),
        ],
        out_shape=[
            jax.ShapeDtypeStruct((vocab, count), LOWER),
            jax.ShapeDtypeStruct((steps, 1, count), WIDE),
            jax.ShapeDtypeStruct((8, count), WIDE),
        ],
        compiler_params=pltpu.CompilerParams(vmem_limit_bytes=VMEM_BYTES),
        name="vocab_scores",
    )(aim, rows, table)


def dlogits_body(aim_ref, scale_ref, expo_ref, table_ref, grad_ref, out_ref, *, step_rows, unit):
    tile = table_ref.shape[0]
    j = pl.program_id(0)

    @pl.when(j == 0)
    def _():
        out_ref[...] = jnp.zeros(out_ref.shape, WIDE)

    table = table_ref[...]
    for start in range(0, expo_ref.shape[1], step_rows):
        cols = slice(start, start + step_rows)
        expo = expo_ref[:, cols].astype(WIDE)
        place = lax.broadcasted_iota(jnp.int32, expo.shape, 0)
        hit = place == aim_ref[:, cols] - j * tile
        grad = (expo * scale_ref[0, :, cols] - jnp.where(hit, unit, 0.0)).astype(LOWER)
        grad_ref[:, cols] = grad
        out_ref[cols, :] += contract_rows(grad, table)


def vocab_grad_rows(expo, table, aim, scale, unit):
    vocab, count = expo.shape
    tile = vocab_tile(count)
    steps = vocab // tile
    return pl.pallas_call(
        functools.partial(dlogits_body, step_rows=ROWS, unit=unit),
        grid=(steps,),
        in_specs=[
            pl.BlockSpec((1, count), lambda j: (0, 0)),
            pl.BlockSpec((1, 1, count), lambda j: (j, 0, 0)),
            pl.BlockSpec((tile, count), lambda j: (j, 0)),
            pl.BlockSpec((tile, D), lambda j: (j, 0)),
        ],
        out_specs=[
            pl.BlockSpec((tile, count), lambda j: (j, 0)),
            pl.BlockSpec((count, D), lambda j: (0, 0)),
        ],
        out_shape=[
            jax.ShapeDtypeStruct((vocab, count), LOWER),
            jax.ShapeDtypeStruct((count, D), WIDE),
        ],
        compiler_params=pltpu.CompilerParams(vmem_limit_bytes=VMEM_BYTES),
        name="vocab_grad_rows",
    )(aim, scale, expo, table)


def vocab_grad_table_body(grad_ref, rows_ref, out_ref):
    out_ref[...] = plain(grad_ref[...], rows_ref[...]).astype(LOWER)


def vocab_grad_table(grad, rows):
    vocab, count = grad.shape
    tile = 2 * vocab_tile(count)
    return pl.pallas_call(
        vocab_grad_table_body,
        grid=(vocab // tile,),
        in_specs=[
            pl.BlockSpec((tile, count), lambda j: (j, 0)),
            pl.BlockSpec((count, D), lambda j: (0, 0)),
        ],
        out_specs=pl.BlockSpec((tile, D), lambda j: (j, 0)),
        out_shape=jax.ShapeDtypeStruct((vocab, D), LOWER),
        compiler_params=pltpu.CompilerParams(vmem_limit_bytes=VMEM_BYTES),
        name="vocab_grad_table",
    )(grad, rows)


def head_step(third, positions, targets, table_all, gain, own, n_dp):
    final, scale_three = norm_fwd(third, gain)
    tokens = third.shape[0]
    count = positions.shape[0]
    pick = positions[:, None] == jnp.arange(tokens, dtype=jnp.int32)[None, :]
    chosen = plain(pick.astype(LOWER), final.astype(LOWER)).astype(LOWER)
    near, far = gather_flips(chosen, n_dp)
    gathered = jnp.concatenate(near + far)
    aim = by_distance(targets, own).reshape(1, -1) - own * table_all.shape[0]
    expo, tops, stats = vocab_scores(gathered, table_all, aim)
    stats = by_distance(stats.reshape(8, n_dp, count).swapaxes(0, 1), own)
    stats = swap(jnp.broadcast_to(stats[None], (n_dp,) + stats.shape), "dp")
    high = jnp.max(stats[:, :, 0], 0)
    sums = jnp.sum(stats[:, :, 1] * jnp.exp(stats[:, :, 0] - high[None]), 0)
    lse = high + jnp.log(sums)
    lse = by_distance(lse, own)
    loss_part = jnp.sum(lse[0] - by_distance(jnp.sum(stats[:, :, 2], 0), own)[0]) / count
    lse = lse.reshape(1, 1, -1)
    scale = jnp.exp(tops - lse) / count
    grad_logits, grad_rows = vocab_grad_rows(expo, table_all, aim, scale, 1.0 / count)
    grad_rows = grad_rows.astype(LOWER)
    grad_chosen = sum_flips(cut(grad_rows, n_dp), n_dp)
    grad_table = vocab_grad_table(grad_logits, gathered)
    grad_chosen, grad_table = lax.optimization_barrier((grad_chosen, grad_table))
    grad_final = rows_high(pick.astype(WIDE), grad_chosen)
    grad_third, grad_gain = norm_back(third, scale_three, gain, grad_final)
    return (loss_part, grad_third, grad_gain, grad_table)


def layer_backward(hidden, grad_third, saved, dense_t, w_in, w_out, n_dp):
    shards = n_dp // EXPERTS
    gains, const_vec = saved["gains"], saved["const_vec"]
    router, const_gate = saved["router"], saved["const_gate"]
    tokens = hidden.shape[0]
    weight = saved["weight"]
    route_p = saved["route_p"]
    second_wide = saved["second_low"].astype(WIDE)
    w_slot, picks = saved["w_slot"], saved["picks"]
    grad_out = contract_rows(picks[0], (w_slot[:, 0:1] * grad_third).astype(LOWER))
    grad_out = grad_out + contract_rows(picks[1], (w_slot[:, 1:2] * grad_third).astype(LOWER))
    sent = send_slots(grad_out.astype(LOWER), n_dp, shards)
    near, far = saved["near"], saved["far"]
    near_back = experts_backward(sent[0], near[0], near[1], w_in, w_out)
    far_back = experts_backward(sent[1], far[0], far[1], w_in, w_out)
    came_back = return_slots(near_back[2], far_back[2], n_dp, shards)
    rows = jnp.concatenate(saved["rows"])
    grad_w_out = contract_rows(
        jnp.concatenate([near[2], far[2]]), jnp.concatenate(sent)
    ).astype(LOWER)
    grad_w_in = jnp.stack(
        [
            contract_rows(rows, jnp.concatenate([near_back[k], far_back[k]])).astype(LOWER)
            for k in range(2)
        ]
    )
    dots = [jnp.sum(saved["outs"][k] * grad_third, -1, keepdims=True) for k in range(2)]
    hits = saved["hits"].astype(WIDE)
    grad_real = (dots[0] * hits[:, 0] + dots[1] * hits[:, 1])[:, :EXPERTS]
    grad_copy = jnp.sum(grad_third * saved["second"], -1, keepdims=True)
    grad_const = jnp.sum(grad_third[:, None, :] * saved["const_out"], -1)
    grad_weight = jnp.concatenate(
        [grad_real, jnp.zeros((tokens, 1), WIDE), grad_copy, grad_const], 1
    )
    grad_p = grad_weight * saved["used"]
    grad_logit = route_p * (grad_p - jnp.sum(route_p * grad_p, -1, keepdims=True))
    const_p = saved["const_p"]
    w_const = weight[:, EXPERTS + 2 :]
    along_vec = jnp.dot(grad_third, const_vec.T, precision=HIGH)
    grad_alpha = w_const[:, :, None] * jnp.stack(
        [jnp.broadcast_to(grad_copy, along_vec.shape), along_vec], -1
    )
    grad_clog = (const_p * (grad_alpha - jnp.sum(const_p * grad_alpha, -1, keepdims=True))).reshape(
        tokens, 4
    )
    grad_cvec = rows_high(w_const * const_p[:, :, 1], grad_third)
    logit_all = jnp.concatenate([grad_logit, grad_clog], 1)
    grad_gates = rows_high(logit_all, second_wide)
    gates_all = jnp.concatenate([router, const_gate], 0).astype(WIDE)
    grad_second = jnp.dot(logit_all, gates_all, precision=HIGH)
    carry = weight[:, EXPERTS + 1 : EXPERTS + 2] + jnp.sum(
        w_const * const_p[:, :, 0], -1, keepdims=True
    )
    grad_second = grad_second + carry * grad_third
    grad_second = grad_second + pick_slots(saved["both"], came_back)
    grad_first_norm, grad_gain_two = norm_back(
        saved["first"], saved["scale_two"], gains[1], grad_second
    )
    grad_first = grad_third + grad_first_norm
    grad_attn = grad_first.astype(LOWER)
    grad_mixed = plain(grad_attn, dense_t[3 * D :]).astype(LOWER)
    grad_qkv = attend_back(saved["qkv"], grad_mixed, saved["segment"])
    grad_normed = plain(grad_qkv, dense_t[: 3 * D])
    unused, grad_gain_one = norm_back(hidden, saved["scale_one"], gains[0], grad_normed)
    left = (grad_qkv, grad_attn)
    return (left, grad_gain_one, grad_gain_two, grad_cvec, grad_gates, grad_w_in, grad_w_out)


def fold(value):
    rows, cols = value.shape
    if rows % 8 or cols % LANES:
        return jnp.pad(jnp.sum(value * value)[None], (0, LANES - 1))
    squares = jnp.sum((value * value).reshape(rows // 8, 8, cols), 0)
    return jnp.sum(squares.reshape(8, cols // LANES, LANES), (0, 1))


def group_squares(arrays, device):
    dense, small, ein, eout, tab = arrays
    width = dense.shape[1]
    front = (device * width + jnp.arange(width, dtype=jnp.int32) < 3 * D).astype(WIDE)
    lanes = (0, LANES - width)
    dense_sq = jnp.sum(dense * dense, 0)
    return [
        jnp.pad(dense_sq * front, lanes),
        jnp.pad(dense_sq * (1.0 - front), lanes),
        jnp.pad(jnp.sum(small[:5] * small[:5], 0), (0, LANES - small.shape[1])),
        jnp.pad(jnp.sum(small[5:] * small[5:], 0), (0, LANES - small.shape[1])),
        fold(ein.reshape(-1, ein.shape[-1])),
        fold(eout),
        fold(tab),
    ]


def moments(weight, first, second, grad):
    first = 0.5 * first + 0.5 * grad
    second = 0.5 * second + 0.5 * grad * grad
    corr = 1.0 - 0.5**STEP
    update = first / corr / (jnp.sqrt(second / corr) + EPS) + 0.01 * weight
    return (first, second, update)


def local(
    x_in,
    seq_lens,
    routes,
    positions,
    targets,
    dense_w,
    small_w,
    expert_in,
    expert_out,
    table,
    dense_m,
    small_m,
    expin_m,
    expout_m,
    table_m,
    dense_v,
    small_v,
    expin_v,
    expout_v,
    table_v,
):
    n_dp, n_rep = lax.axis_size("dp"), lax.axis_size("rep")
    devices = n_dp * n_rep
    own = lax.axis_index("dp")
    device = own * n_rep + lax.axis_index("rep")
    masters = (dense_w, small_w, expert_in, expert_out, table)
    width, thin = dense_w.shape[1], small_w.shape[1]
    place = jnp.stack([own, lax.axis_index("rep")]).astype(jnp.int32)
    flips = n_rep == 4 and width % 16 == 0 and thin % 8 == 0
    if flips:
        dense_t, small_all = gather_weights(dense_w, small_w, place, n_dp)
    else:
        dense_t = lax.all_gather(dense_w.T.astype(LOWER), BOTH, axis=0, tiled=True)
        small_t = jnp.pad(small_w.T.astype(LOWER), ((0, 0), (0, LANES - small_w.shape[0])))
        small_all = share(small_t, BOTH, devices).reshape(-1, LANES).T
    w_in, w_out, table_all = (
        lax.all_gather(expert_in.astype(LOWER), "rep", axis=1, tiled=True),
        lax.all_gather(expert_out.astype(LOWER), "rep", axis=0, tiled=True),
        lax.all_gather(table.astype(LOWER), "rep", axis=0, tiled=True),
    )
    hidden = x_in.astype(WIDE)
    third, saved = layer_forward(
        hidden, seq_lens[0], routes, dense_t, small_all, w_in, w_out, own, n_dp
    )
    loss_part, grad_third, grad_gain_final, grad_table = head_step(
        third, positions, targets[0], table_all, saved["gains"][2], own, n_dp
    )
    table_g = lax.psum_scatter(grad_table, "rep", scatter_dimension=0, tiled=True)
    left, gain_one, gain_two, grad_cvec, grad_gates, grad_w_in, grad_w_out = layer_backward(
        hidden, grad_third, saved, dense_t, w_in, w_out, n_dp
    )
    ein_g, eout_g = (
        lax.psum_scatter(grad_w_in, "rep", scatter_dimension=1, tiled=True),
        lax.psum_scatter(grad_w_out, "rep", scatter_dimension=0, tiled=True),
    )
    small_grad = jnp.concatenate(
        [gain_one[None], gain_two[None], grad_gain_final[None], grad_cvec, grad_gates], 0
    )
    normed, mixed = saved["normed_low"], saved["mixed"]
    if flips:
        turned = jnp.pad(small_grad, ((0, LANES - small_grad.shape[0]), (0, 0))).T
        mine, other = dense_grads(place, *left, normed, mixed, turned, n_dp, width)
        block = sum_weights(mine, other, n_dp)
        small_g = block[width:].reshape(8, -1, LANES)[:, : thin // 8].swapaxes(0, 1)
        small_g = small_g.reshape(thin, LANES)[:, : small_w.shape[0]].T
    else:
        dense_grad = jnp.concatenate(
            [contract_rows(left[0], normed), contract_rows(left[1], mixed)]
        )
        small_blocks = small_grad.reshape(-1, devices, thin).swapaxes(0, 1).reshape(devices, -1)
        extra = -(-small_blocks.shape[1] // (8 * D)) * 8 * D
        small_blocks = jnp.pad(small_blocks, ((0, 0), (0, extra - small_blocks.shape[1])))
        blocks = jnp.concatenate(
            [dense_grad.reshape(devices, width, D), small_blocks.reshape(devices, -1, D)], 1
        )
        block = scatter_sum(blocks.reshape((n_dp, n_rep) + blocks.shape[1:]), n_dp, n_rep)
        small_g = block[width:].reshape(-1)[: small_w.size].reshape(small_w.shape)
    dense_g = block[:width].T
    grads = (dense_g, small_g, ein_g.astype(WIDE), eout_g.astype(WIDE), table_g.astype(WIDE))
    firsts = (dense_m, small_m, expin_m, expout_m, table_m)
    seconds = (dense_v, small_v, expin_v, expout_v, table_v)
    results = [moments(w, m, v, g) for w, m, v, g in zip(masters, firsts, seconds, grads)]
    update_parts = group_squares(tuple((r[2] for r in results)), device)
    loss_row = jnp.pad(loss_part[None], (0, LANES - 1))
    parts = jnp.stack(group_squares(masters, device) + update_parts + [loss_row, loss_row * 0.0])
    sums = jnp.sum(share(parts, BOTH, devices), (0, 2))
    loss = sums[14]
    weight_norm = jnp.sqrt(sums[:7])
    update_norm = jnp.sqrt(sums[7:14])
    trust = weight_norm / update_norm
    column = device * width + jnp.arange(width, dtype=jnp.int32)
    dense_scale = jnp.where(column < 3 * D, trust[0], trust[1])[None, :]
    small_scale = jnp.where(jnp.arange(21, dtype=jnp.int32) < 5, trust[2], trust[3])[:, None]
    scales = (dense_scale, small_scale, trust[4], trust[5], trust[6])
    outs = [loss, jnp.stack([weight_norm, update_norm, trust])]
    for w, r, factor in zip(masters, results, scales):
        fresh = w - 0.2 * factor * r[2]
        outs += [r[0], r[1], fresh, fresh.astype(LOWER)]
    return tuple(outs)


def solution(mesh):
    in_specs = (
        P(("dp", "rep"), None),
        P(("dp", "rep"), None),
        P(("dp", "rep"), None),
        P(("dp", "rep")),
        P("rep", None, None),
        P(None, ("dp", "rep")),
        P(None, ("dp", "rep")),
        P(None, "rep", "dp"),
        P(("dp", "rep"), None),
        P(("dp", "rep"), None),
        P(None, ("dp", "rep")),
        P(None, ("dp", "rep")),
        P(None, "rep", "dp"),
        P(("dp", "rep"), None),
        P(("dp", "rep"), None),
        P(None, ("dp", "rep")),
        P(None, ("dp", "rep")),
        P(None, "rep", "dp"),
        P(("dp", "rep"), None),
        P(("dp", "rep"), None),
    )
    out_specs = (
        P(),
        P(),
        P(None, ("dp", "rep")),
        P(None, ("dp", "rep")),
        P(None, ("dp", "rep")),
        P(None, ("dp", "rep")),
        P(None, ("dp", "rep")),
        P(None, ("dp", "rep")),
        P(None, ("dp", "rep")),
        P(None, ("dp", "rep")),
        P(None, "rep", "dp"),
        P(None, "rep", "dp"),
        P(None, "rep", "dp"),
        P(None, "rep", "dp"),
        P(("dp", "rep"), None),
        P(("dp", "rep"), None),
        P(("dp", "rep"), None),
        P(("dp", "rep"), None),
        P(("dp", "rep"), None),
        P(("dp", "rep"), None),
        P(("dp", "rep"), None),
        P(("dp", "rep"), None),
    )
    return jax.shard_map(local, mesh=mesh, in_specs=in_specs, out_specs=out_specs, check_vma=False)
```

time: 780 us -> 641 us (0.82)
  matrix products: 184 us -> 78.6 us
  Pallas kernels: 0 us -> 99.9 us
  waiting for transfers between devices: 237 us -> 152 us
  blocking collectives: 94 us -> 11.7 us
  starting transfers between devices: 33 us -> 107 us
  other arithmetic: 158 us -> 103 us
  local copies, waits for them, and re-layouts: 44.2 us -> 56.9 us
    pallas_call x0 -> x8, Pallas kernels: none -> 99.9 us  [the longest x1 27.1 us: vocab_scores(): pl.pallas_call(functools.partial(scores_body, step_rows=ROWS), grid=(step...]
    ppermute x5 -> x67, starting transfers between devices: 6.27 us -> 102 us  [flip(): return lax.ppermute(value, axis, [(i, i ^ mask) for i in range(size)])]
    all_to_all x5 -> x1, waiting for transfers between devices: 94.7 us -> 9.22 us  [swap(): return lax.all_to_all(value, axis, split_axis=0, concat_axis=0, tiled=True)]
    all_to_all x4 -> x1, blocking collectives: 94 us -> 11.7 us  [swap(): return lax.all_to_all(value, axis, split_axis=0, concat_axis=0, tiled=True)]
    ppermute x5 -> x67, waiting for transfers between devices: 76.4 us -> 124 us  [flip(): return lax.ppermute(value, axis, [(i, i ^ mask) for i in range(size)])]
    all_gather x1 -> x0, waiting for transfers between devices: 41.8 us -> none  [local(): dense_t = lax.all_gather(dense_w.T.astype(LOWER), BOTH, axis=0, tiled=True)]
    dot_general x8 -> x10, matrix products: 54.4 us -> 22.9 us  [contract_cols(): lax.dot_general(left, right, (((1,), (1,)), ((), ())), preferred_element_...]
    convert_element_type x6 -> x4, other arithmetic: 31.4 us -> 1.35 us  [the longest x2 0.95 us: sum_flips(): sum([a.astype(WIDE) for a in aims], parts[half].astype(WIDE)).astype(LOWER)]
  transfers between devices with their start and end apart: 17 -> 74, of which waited for: 12 -> 31; matrix products, arithmetic and copies ran while one was open for 30% -> 24% of each run, Pallas kernels for 0% -> 8%
where the time goes in v2:
time: 641 us; the launch traced here: 629 us
  waiting for transfers between devices  152 us (24%)
  starting transfers between devices  107 us (17%)
  other arithmetic  103 us (16%)
  Pallas kernels  99.9 us (16%)
  matrix products  78.6 us (12%)
  local copies, waits for them, and re-layouts  56.9 us (9%)
  between operations  19.4 us (3%)
  blocking collectives  11.7 us (2%)
    ppermute x67, waiting for transfers between devices, flip(): return lax.ppermute(value, axis, [(i, i ^ mask) for i in range(size)])  124 us
    ppermute x67, starting transfers between devices, flip(): return lax.ppermute(value, axis, [(i, i ^ mask) for i in range(size)])  102 us
    unnamed x316, local copies, waits for them, and re-layouts  32.9 us
    dot_general x13, matrix products, plain(): return jnp.dot(left, right, preferred_element_type=WIDE)  29.5 us
    pallas_call x1, Pallas kernels, vocab_scores(): pl.pallas_call(functools.partial(scores_body, step_rows=ROWS), grid=(step...  27.1 us
    reduce_sum x9, other arithmetic, fold(): return jnp.sum(squares.reshape(8, cols // LANES, LANES), (0, 1))  24.9 us
    dot_general x10, matrix products, contract_cols(): lax.dot_general(left, right, (((1,), (1,)), ((), ())), preferred_element_...  22.9 us
    pallas_call x1, Pallas kernels, vocab_grad_rows(): pl.pallas_call(functools.partial(dlogits_body, step_rows=ROWS, unit=unit)...  21.6 us
  transfers between devices with their start and end apart: 74, of which 31 were waited for; matrix products, arithmetic and copies ran while one was open for 24% of the time, Pallas kernels for 8%

profile of v2, /device:TPU:0, one launch (start us, length us, event | category | flops | bytes accessed | tf_op | source)
XLA Modules:
  0.0 628.6 jit_solution(36880296896781762)
XLA Ops:
  35.9 15.6 %collective-permute-done.4.refs_4_ = bf16[208,768]{1,0:T(8,128)(2,1)S(1)} collective-permute-done((bf16[208,768]{1,0:T(8,128)(2,1)S(1)}, bf16[208,768]{1,0:T(8,128)(2,1)S(1)}, u32[]{:S(2)}, u32[]{:S(2)}) %collective-permute-start.4) | collective-permute-done | bytes 319520 | tf_op jit(solution)/shard_map/ppermute | solution.py:54
  82.9 8.1 %attend.1.mixed_ref = bf16[512,768]{1,0:T(8,128)(2,1)S(1)} custom-call(s32[512,1]{1,0:T(8,128)S(1)} %convert_add_fusion.3.seg_col, s32[1,512]{1,0:T(1,128)S(1)} %fusion.118.seg_row, bf16[512,2304]{1,0:T(8,128)(2,1)S(1)} %convolution_convert_fusion.q_ref.k_ref.v_ref, bf16[512,2304]{1,0:T(8,128)(2,1)S(1)} %convolution_convert_fusion.q_ref.k_ref.v_ref, ...), custom_call_target="tpu_custom_call" | custom-call | tf_op jit(solution)/shard_map/attend/pallas_call | solution.py:348
  134.2 4.9 multiply_convert_fusion.5
  150.2 4.8 multiply_convert_fusion.4
  164.4 11.6 %collective-permute-done.26 = bf16[96,768]{1,0:T(8,128)(2,1)S(1)} collective-permute-done((bf16[96,768]{1,0:T(8,128)(2,1)S(1)}, bf16[96,768]{1,0:T(8,128)(2,1)S(1)}, u32[]{:S(2)}, u32[]{:S(2)}) %collective-permute-start.26) | collective-permute-done | bytes 147488 | tf_op jit(solution)/shard_map/ppermute | solution.py:54
  185.2 5.5 collective-permute-start.31
  192.9 7.3 %collective-permute-done.33 = bf16[128,768]{1,0:T(8,128)(2,1)S(1)} collective-permute-done((bf16[128,768]{1,0:T(8,128)(2,1)S(1)}, bf16[128,768]{1,0:T(8,128)(2,1)S(1)}, u32[]{:S(2)}, u32[]{:S(2)}) %collective-permute-start.33) | collective-permute-done | bytes 196640 | tf_op jit(solution)/shard_map/ppermute | solution.py:54
  213.9 27.1 %vocab_scores.1 = (bf16[8192,1024]{1,0:T(8,128)(2,1)}, f32[8,1,1024]{2,1,0:T(1,128)S(1)}, f32[8,1024]{1,0:T(8,128)S(1)}) custom-call(s32[1,1024]{1,0:T(1,128)S(1)} %bitcast.278, bf16[1024,768]{1,0:T(8,128)(2,1)S(1)} %copy-done.3, bf16[8192,768]{1,0:T(8,128)(2,1)} %all-gather.8.cloned.1.call-done.table_ref), custom_call_target="tpu_custom_call" | custom-call | tf_op jit(solution)/shard_map/vocab_scores/pallas_call | solution.py:582
  241.1 11.7 %all_to_all.10 = f32[8,8,8,128]{3,1,2,0:T(8,128)S(1)} all-to-all(f32[8,8,8,128]{3,1,2,0:T(8,128)S(1)} %broadcast_in_dim.126), channel_id=1, replica_groups=mesh['dp'=8,'rep'=4] {'dp'}, dimensions={0} | all-to-all | bytes 524288 | tf_op jit(solution)/shard_map/all_to_all | solution.py:46
  260.2 21.6 %vocab_grad_rows.1 = (bf16[8192,1024]{1,0:T(8,128)(2,1)}, f32[1024,768]{1,0:T(8,128)S(1)}) custom-call(s32[1,1024]{1,0:T(1,128)S(1)} %bitcast.279, f32[8,1,1024]{2,1,0:T(1,128)S(1)} %exponential_multiply_fusion.scale_ref, bf16[8192,1024]{1,0:T(8,128)(2,1)} %get-tuple-element.37.expo_ref, bf16[8192,768]{1,0:T(8,128)(2,1)} %all-gather.8.cloned.1.call-done.table_ref), custom_call_target="tpu_custom_call" | custom-call | tf_op jit(solution)/shard_map/vocab_grad_rows/pallas_call | solution.py:628
  287.8 5.9 collective-permute-done.42
  296.5 17.9 %vocab_grad_table.1 = bf16[8192,768]{1,0:T(8,128)(2,1)} custom-call(bf16[8192,1024]{1,0:T(8,128)(2,1)} %get-tuple-element.39.grad_ref, bf16[1024,768]{1,0:T(8,128)(2,1)S(1)} %copy-done.4), custom_call_target="tpu_custom_call" | custom-call | tf_op jit(solution)/shard_map/vocab_grad_table/pallas_call | solution.py:657
  340.5 7.7 %collective-permute-done.50 = bf16[96,768]{1,0:T(8,128)(2,1)S(1)} collective-permute-done((bf16[96,768]{1,0:T(8,128)(2,1)S(1)}, bf16[96,768]{1,0:T(8,128)(2,1)S(1)}, u32[]{:S(2)}, u32[]{:S(2)}) %collective-permute-start.50) | collective-permute-done | bytes 147488 | tf_op jit(solution)/shard_map/ppermute | solution.py:54
  354.3 6.1 multiply_convert_fusion
  364.6 5.1 fusion.14
  415.5 8.1 %collective-permute-done.54 = bf16[96,768]{1,0:T(8,128)(2,1)S(1)} collective-permute-done((bf16[96,768]{1,0:T(8,128)(2,1)S(1)}, bf16[96,768]{1,0:T(8,128)(2,1)S(1)}, u32[]{:S(2)}, u32[]{:S(2)}) %collective-permute-start.54) | collective-permute-done | bytes 147488 | tf_op jit(solution)/shard_map/ppermute | solution.py:54
  432.9 14.2 %attend_back.1.qkv_ref = bf16[512,2304]{1,0:T(8,128)(2,1)S(1)} custom-call(s32[512,1]{1,0:T(8,128)S(1)} %convert_add_fusion.3.seg_col, s32[1,512]{1,0:T(1,128)S(1)} %fusion.118.seg_row, bf16[512,2304]{1,0:T(8,128)(2,1)S(1)} %convolution_convert_fusion.q_ref.k_ref.v_ref, bf16[512,2304]{1,0:T(8,128)(2,1)S(1)} %convolution_convert_fusion.q_ref.k_ref.v_ref, ...), custom_call_target="tpu_custom_call" | custom-call | tf_op jit(solution)/shard_map/attend_back/pallas_call | solution.py:411
  452.0 7.6 %dense_grads.1 = (f32[8,2,104,768]{3,2,1,0:T(8,128)}, bf16[8,2,104,768]{3,2,1,0:T(8,128)(2,1)}) custom-call(s32[2]{0:T(128)S(1)} %pad_add_fusion.place_ref, bf16[512,2304]{1,0:T(8,128)(2,1)S(1)} %copy-done.1, bf16[512,768]{1,0:T(8,128)(2,1)S(1)} %copy-done.8, bf16[512,768]{1,0:T(8,128)(2,1)S(1)} %copy-done.6, bf16[512,768]{1,0:T(8,128)(2,1)S(1)} %attend.1.mixed_ref, ...), custom_call_target="tpu_custom_call" | custom-call | tf_op jit(solution)/shard_map/dense_grads/pallas_call | solution.py:252
  466.1 6.0 fusion.152
  486.8 5.9 collective-permute-done.63
  493.3 5.5 collective-permute-start.65
  500.7 6.1 collective-permute-done.61
  506.8 5.5 collective-permute-done.60
  513.8 6.5 %collective-permute-start.66 = (bf16[104,768]{1,0:T(8,128)(2,1)S(1)}, bf16[104,768]{1,0:T(8,128)(2,1)S(1)}, u32[]{:S(2)}, u32[]{:S(2)}) collective-permute-start(bf16[104,768]{1,0:T(8,128)(2,1)S(1)} %fusion.93), channel_id=1, source_target_pairs={{0,2},{1,3},{2,0},{3,1},{4,6},{5,7},{6,4},{7,5},{8,10},{9,11},{10,... | collective-permute-start | bytes 479240 | tf_op jit(solution)/shard_map/ppermute | solution.py:54
  520.3 7.9 %collective-permute-done.66 = bf16[104,768]{1,0:T(8,128)(2,1)S(1)} collective-permute-done((bf16[104,768]{1,0:T(8,128)(2,1)S(1)}, bf16[104,768]{1,0:T(8,128)(2,1)S(1)}, u32[]{:S(2)}, u32[]{:S(2)}) %collective-permute-start.66) | collective-permute-done | bytes 159776 | tf_op jit(solution)/shard_map/ppermute | solution.py:54
  530.9 5.7 multiply_reduce_fusion.5
  536.7 6.4 %multiply_reduce_fusion.2 = (f32[2048]{0:T(1024)S(1)}, f32[2048]{0:T(1024)S(1)}, f32[2,192,2048]{2,1,0:T(8,128)}, f32[2,192,2048]{2,1,0:T(8,128)}) fusion(f32[2,192,2048]{2,1,0:T(8,128)S(1)} %copy-done.16, bf16[2,192,2048]{2,1,0:T(8,128)(2,1)} %reduce-scatter.4.cloned.1.call-done, f32[2,192,2048]{2,1,0:T(8,128)} %param.32, f32[2,192,2048]{2,1,0:T(8,128)} %param.37), kind=kLoop, calls=%fused_computation.28 | loop fusion | flops 13365248 | bytes 17317888 | tf_op jit(solution)/shard_map/reduce_sum | solution.py:773
  543.1 18.2 %reduce-scatter.8.cloned.1.call-done = bf16[2048,768]{1,0:T(8,128)(2,1)} async-done(((bf16[8192,768]{1,0:T(8,128)(2,1)}), bf16[2048,768]{1,0:T(8,128)(2,1)}) %reduce-scatter.8.cloned.1.call-update) | async-done | bytes 3145744 | tf_op jit(solution)/shard_map/reduce_scatter | solution.py:849
  561.3 12.8 %multiply_reduce_fusion = (f32[768]{0:T(1024)S(1)}, f32[768]{0:T(1024)S(1)}, f32[2048,768]{1,0:T(8,128)}, f32[2048,768]{1,0:T(8,128)}) fusion(f32[2048,768]{1,0:T(8,128)} %param.29, bf16[2048,768]{1,0:T(8,128)(2,1)} %reduce-scatter.8.cloned.1.call-done, f32[2048,768]{1,0:T(8,128)} %param.34, f32[2048,768]{1,0:T(8,128)} %param.39), kind=kLoop, calls=%fused_computation.5 | loop fusion | flops 26737152 | bytes 34609152 | tf_op jit(solution)/shard_map/reduce_sum | solution.py:773
  581.7 9.2 %all-to-all-done.1 = f32[32,16,128]{2,1,0:T(8,128)} async-done(((f32[32,16,128]{2,1,0:T(8,128)}), f32[32,16,128]{2,1,0:T(8,128)}, u32[]{:S(2)}, u32[]{:S(2)}) %all-to-all-start.1) | async-done | bytes 262176 | tf_op jit(solution)/shard_map/all_to_all | solution.py:46
  601.9 7.8 %fusion.144 = (bf16[2,192,2048]{2,1,0:T(8,128)(2,1)}, f32[2,192,2048]{2,1,0:T(8,128)}) fusion(f32[2,192,2048]{2,1,0:T(8,128)S(1)} %copy-done.16, f32[2,192,2048]{2,1,0:T(8,128)} %get-tuple-element.168, f32[2,192,2048]{2,1,0:T(8,128)} %get-tuple-element.167, f32[]{:T(128)} %bitcast.94), kind=kLoop, calls=%fused_computation.369 | loop fusion | flops 7077888 | bytes 14155780 | tf_op jit(solution)/shard_map/convert_element_type | solution.py:899
  613.9 7.4 %fusion.142 = (bf16[2048,768]{1,0:T(8,128)(2,1)}, f32[2048,768]{1,0:T(8,128)}) fusion(f32[2048,768]{1,0:T(8,128)} %param.29, f32[2048,768]{1,0:T(8,128)S(1)} %bitcast.284, f32[2048,768]{1,0:T(8,128)S(1)} %bitcast.282, f32[]{:T(128)} %bitcast.96), kind=kLoop, calls=%fused_computation.367 | loop fusion | flops 14155776 | bytes 28311556 | tf_op jit(solution)/shard_map/convert_element_type | solution.py:899
  (633 shorter events, 307.5 us)
Async XLA Ops:
  7.2 121.6 %all-gather.4.cloned.1.call-start = ((), (), s32[]{:S(2)}) async-start(), calls=%async_computation.5 | async-start | bytes 7864320 | tf_op jit(solution)/shard_map/all_gather | solution.py:838
  10.5 128.5 %all-gather.6.cloned.1.call-start = ((), (), s32[]{:S(2)}) async-start(), calls=%async_computation.6 | async-start | bytes 3932160 | tf_op jit(solution)/shard_map/all_gather | solution.py:839
  12.9 199.6 %all-gather.8.cloned.1.call-start = ((), (), s32[]{:S(2)}) async-start(), calls=%async_computation.7 | async-start | bytes 15728640 | tf_op jit(solution)/shard_map/all_gather | solution.py:840
  17.8 513.2 %reduce-scatter.6.cloned.1.call-start = ((), (), s32[]{:S(2)}) async-start(), calls=%async_computation.9 | async-start | bytes 3932160 | tf_op jit(solution)/shard_map/reduce_scatter | solution.py:855
  29.1 22.8 %collective-permute-start.1 = (bf16[208,768]{1,0:T(8,128)(2,1)S(1)}, bf16[208,768]{1,0:T(8,128)(2,1)S(1)}, u32[]{:S(2)}, u32[]{:S(2)}) collective-permute-start(bf16[208,768]{1,0:T(8,128)(2,1)S(1)} %pad_maximum_fusion.2.refs_0_), channel_id=1, source_target_pairs={{0,4},{4,0},{8,12},{12,8},{16,20},{20,16},{24,28},{28,24},{1,5},{5... | collective-permute-start | bytes 958472 | tf_op jit(solution)/shard_map/ppermute | solution.py:54
  31.2 24.4 %collective-permute-start.2 = (bf16[208,768]{1,0:T(8,128)(2,1)S(1)}, bf16[208,768]{1,0:T(8,128)(2,1)S(1)}, u32[]{:S(2)}, u32[]{:S(2)}) collective-permute-start(bf16[208,768]{1,0:T(8,128)(2,1)S(1)} %pad_maximum_fusion.2.refs_0_), channel_id=1, source_target_pairs={{0,8},{4,12},{8,0},{12,4},{16,24},{20,28},{24,16},{28,20},{1,9},{5... | collective-permute-start | bytes 958472 | tf_op jit(solution)/shard_map/ppermute | solution.py:54
  32.8 24.3 %collective-permute-start.3 = (bf16[208,768]{1,0:T(8,128)(2,1)S(1)}, bf16[208,768]{1,0:T(8,128)(2,1)S(1)}, u32[]{:S(2)}, u32[]{:S(2)}) collective-permute-start(bf16[208,768]{1,0:T(8,128)(2,1)S(1)} %pad_maximum_fusion.2.refs_0_), channel_id=1, source_target_pairs={{0,12},{4,8},{8,4},{12,0},{16,28},{20,24},{24,20},{28,16},{1,13},{... | collective-permute-start | bytes 958472 | tf_op jit(solution)/shard_map/ppermute | solution.py:54
  32.8 18.7 %collective-permute-start.4 = (bf16[208,768]{1,0:T(8,128)(2,1)S(1)}, bf16[208,768]{1,0:T(8,128)(2,1)S(1)}, u32[]{:S(2)}, u32[]{:S(2)}) collective-permute-start(bf16[208,768]{1,0:T(8,128)(2,1)S(1)} %pad_maximum_fusion.2.refs_0_), channel_id=1, source_target_pairs={{0,16},{4,20},{8,24},{12,28},{16,0},{20,4},{24,8},{28,12},{1,17},{... | collective-permute-start | bytes 958472 | tf_op jit(solution)/shard_map/ppermute | solution.py:54
  35.9 21.2 %collective-permute-start.8 = (bf16[208,768]{1,0:T(8,128)(2,1)S(1)}, bf16[208,768]{1,0:T(8,128)(2,1)S(1)}, u32[]{:S(2)}, u32[]{:S(2)}) collective-permute-start(bf16[208,768]{1,0:T(8,128)(2,1)S(1)} %pad_maximum_fusion.2.refs_0_), channel_id=1, source_target_pairs={{0,1},{1,0},{2,3},{3,2},{4,5},{5,4},{6,7},{7,6},{8,9},{9,8},{10,11... | collective-permute-start | bytes 958472 | tf_op jit(solution)/shard_map/ppermute | solution.py:54
  95.7 26.7 %collective-permute-start.18 = (bf16[96,768]{1,0:T(8,128)(2,1)}, bf16[96,768]{1,0:T(8,128)(2,1)}, u32[]{:S(2)}, u32[]{:S(2)}) collective-permute-start(bf16[96,768]{1,0:T(8,128)(2,1)} %get-tuple-element.208), channel_id=1, source_target_pairs={{0,12},{4,8},{8,4},{12,0},{16,28},{20,24},{24,20},{28,16},{1,13},{... | collective-permute-start | bytes 442376 | tf_op jit(solution)/shard_map/ppermute | solution.py:54
  97.7 22.0 %collective-permute-start.17 = (bf16[96,768]{1,0:T(8,128)(2,1)}, bf16[96,768]{1,0:T(8,128)(2,1)}, u32[]{:S(2)}, u32[]{:S(2)}) collective-permute-start(bf16[96,768]{1,0:T(8,128)(2,1)} %get-tuple-element.209), channel_id=1, source_target_pairs={{0,8},{4,12},{8,0},{12,4},{16,24},{20,28},{24,16},{28,20},{1,9},{5... | collective-permute-start | bytes 442376 | tf_op jit(solution)/shard_map/ppermute | solution.py:54
  99.2 24.8 %collective-permute-start.22 = (bf16[96,768]{1,0:T(8,128)(2,1)}, bf16[96,768]{1,0:T(8,128)(2,1)}, u32[]{:S(2)}, u32[]{:S(2)}) collective-permute-start(bf16[96,768]{1,0:T(8,128)(2,1)} %get-tuple-element.207), channel_id=1, source_target_pairs={{0,16},{4,20},{8,24},{12,28},{16,0},{20,4},{24,8},{28,12},{1,17},{... | collective-permute-start | bytes 442376 | tf_op jit(solution)/shard_map/ppermute | solution.py:54
  101.2 24.5 %collective-permute-start.23 = (bf16[96,768]{1,0:T(8,128)(2,1)}, bf16[96,768]{1,0:T(8,128)(2,1)}, u32[]{:S(2)}, u32[]{:S(2)}) collective-permute-start(bf16[96,768]{1,0:T(8,128)(2,1)} %get-tuple-element.206), channel_id=1, source_target_pairs={{0,20},{4,16},{8,28},{12,24},{16,4},{20,0},{24,12},{28,8},{1,21},{... | collective-permute-start | bytes 442376 | tf_op jit(solution)/shard_map/ppermute | solution.py:54
  143.9 18.1 %collective-permute-start.20 = (bf16[96,768]{1,0:T(8,128)(2,1)S(1)}, bf16[96,768]{1,0:T(8,128)(2,1)S(1)}, u32[]{:S(2)}, u32[]{:S(2)}) collective-permute-start(bf16[96,768]{1,0:T(8,128)(2,1)S(1)} %get-tuple-element.225), channel_id=1, source_target_pairs={{0,8},{4,12},{8,0},{12,4},{16,24},{20,28},{24,16},{28,20},{1,9},{5... | collective-permute-start | bytes 442376 | tf_op jit(solution)/shard_map/ppermute | solution.py:54
  156.5 19.5 %collective-permute-start.26 = (bf16[96,768]{1,0:T(8,128)(2,1)S(1)}, bf16[96,768]{1,0:T(8,128)(2,1)S(1)}, u32[]{:S(2)}, u32[]{:S(2)}) collective-permute-start(bf16[96,768]{1,0:T(8,128)(2,1)S(1)} %get-tuple-element.223), channel_id=1, source_target_pairs={{0,16},{4,20},{8,24},{12,28},{16,0},{20,4},{24,8},{28,12},{1,17},{... | collective-permute-start | bytes 442376 | tf_op jit(solution)/shard_map/ppermute | solution.py:54
  159.1 20.2 %collective-permute-start.27 = (bf16[96,768]{1,0:T(8,128)(2,1)S(1)}, bf16[96,768]{1,0:T(8,128)(2,1)S(1)}, u32[]{:S(2)}, u32[]{:S(2)}) collective-permute-start(bf16[96,768]{1,0:T(8,128)(2,1)S(1)} %get-tuple-element.222), channel_id=1, source_target_pairs={{0,20},{4,16},{8,28},{12,24},{16,4},{20,0},{24,12},{28,8},{1,21},{... | collective-permute-start | bytes 442376 | tf_op jit(solution)/shard_map/ppermute | solution.py:54
  159.7 19.7 %collective-permute-start.28 = (bf16[96,768]{1,0:T(8,128)(2,1)S(1)}, bf16[96,768]{1,0:T(8,128)(2,1)S(1)}, u32[]{:S(2)}, u32[]{:S(2)}) collective-permute-start(bf16[96,768]{1,0:T(8,128)(2,1)S(1)} %get-tuple-element.221), channel_id=1, source_target_pairs={{0,24},{4,28},{8,16},{12,20},{16,8},{20,12},{24,0},{28,4},{1,25},{... | collective-permute-start | bytes 442376 | tf_op jit(solution)/shard_map/ppermute | solution.py:54
  161.9 17.5 %collective-permute-start.29 = (bf16[96,768]{1,0:T(8,128)(2,1)S(1)}, bf16[96,768]{1,0:T(8,128)(2,1)S(1)}, u32[]{:S(2)}, u32[]{:S(2)}) collective-permute-start(bf16[96,768]{1,0:T(8,128)(2,1)S(1)} %get-tuple-element.220), channel_id=1, source_target_pairs={{0,28},{4,24},{8,20},{12,16},{16,12},{20,8},{24,4},{28,0},{1,29},{... | collective-permute-start | bytes 442376 | tf_op jit(solution)/shard_map/ppermute | solution.py:54
  183.9 19.5 %collective-permute-start.30 = (bf16[128,768]{1,0:T(8,128)(2,1)S(1)}, bf16[128,768]{1,0:T(8,128)(2,1)S(1)}, u32[]{:S(2)}, u32[]{:S(2)}) collective-permute-start(bf16[128,768]{1,0:T(8,128)(2,1)S(1)} %get-tuple-element.276), channel_id=1, source_target_pairs={{0,4},{4,0},{8,12},{12,8},{16,20},{20,16},{24,28},{28,24},{1,5},{5... | collective-permute-start | bytes 589832 | tf_op jit(solution)/shard_map/ppermute | solution.py:54
  185.2 19.0 %collective-permute-start.31 = (bf16[128,768]{1,0:T(8,128)(2,1)S(1)}, bf16[128,768]{1,0:T(8,128)(2,1)S(1)}, u32[]{:S(2)}, u32[]{:S(2)}) collective-permute-start(bf16[128,768]{1,0:T(8,128)(2,1)S(1)} %get-tuple-element.276), channel_id=1, source_target_pairs={{0,8},{4,12},{8,0},{12,4},{16,24},{20,28},{24,16},{28,20},{1,9},{5... | collective-permute-start | bytes 589832 | tf_op jit(solution)/shard_map/ppermute | solution.py:54
  286.3 28.1 %collective-permute-start.39 = (bf16[128,768]{1,0:T(8,128)(2,1)}, bf16[128,768]{1,0:T(8,128)(2,1)}, u32[]{:S(2)}, u32[]{:S(2)}) collective-permute-start(bf16[128,768]{1,0:T(8,128)(2,1)} %get-tuple-element.192), channel_id=1, source_target_pairs={{0,12},{4,8},{8,4},{12,0},{16,28},{20,24},{24,20},{28,16},{1,13},{... | collective-permute-start | bytes 589832 | tf_op jit(solution)/shard_map/ppermute | solution.py:54
  287.2 27.2 %collective-permute-start.38 = (bf16[128,768]{1,0:T(8,128)(2,1)}, bf16[128,768]{1,0:T(8,128)(2,1)}, u32[]{:S(2)}, u32[]{:S(2)}) collective-permute-start(bf16[128,768]{1,0:T(8,128)(2,1)} %get-tuple-element.193), channel_id=1, source_target_pairs={{0,8},{4,12},{8,0},{12,4},{16,24},{20,28},{24,16},{28,20},{1,9},{5... | collective-permute-start | bytes 589832 | tf_op jit(solution)/shard_map/ppermute | solution.py:54
  293.7 20.7 %collective-permute-start.37 = (bf16[128,768]{1,0:T(8,128)(2,1)}, bf16[128,768]{1,0:T(8,128)(2,1)}, u32[]{:S(2)}, u32[]{:S(2)}) collective-permute-start(bf16[128,768]{1,0:T(8,128)(2,1)} %get-tuple-element.188), channel_id=1, source_target_pairs={{0,4},{4,0},{8,12},{12,8},{16,20},{20,16},{24,28},{28,24},{1,5},{5... | collective-permute-start | bytes 589832 | tf_op jit(solution)/shard_map/ppermute | solution.py:54
  296.2 18.2 %collective-permute-start.43 = (bf16[128,768]{1,0:T(8,128)(2,1)}, bf16[128,768]{1,0:T(8,128)(2,1)}, u32[]{:S(2)}, u32[]{:S(2)}) collective-permute-start(bf16[128,768]{1,0:T(8,128)(2,1)} %add_convert_fusion.2), channel_id=1, source_target_pairs={{0,16},{4,20},{8,24},{12,28},{16,0},{20,4},{24,8},{28,12},{1,17},{... | collective-permute-start | bytes 589832 | tf_op jit(solution)/shard_map/ppermute | solution.py:54
  329.5 18.8 %collective-permute-start.53 = (bf16[96,768]{1,0:T(8,128)(2,1)S(1)}, bf16[96,768]{1,0:T(8,128)(2,1)S(1)}, u32[]{:S(2)}, u32[]{:S(2)}) collective-permute-start(bf16[96,768]{1,0:T(8,128)(2,1)S(1)} %get-tuple-element.195), channel_id=1, source_target_pairs={{0,28},{4,24},{8,20},{12,16},{16,12},{20,8},{24,4},{28,0},{1,29},{... | collective-permute-start | bytes 442376 | tf_op jit(solution)/shard_map/ppermute | solution.py:54
  354.1 182.5 %reduce-scatter.4.cloned.1.call-start = ((), (), s32[]{:S(2)}) async-start(), calls=%async_computation.8 | async-start | bytes 7864320 | tf_op jit(solution)/shard_map/reduce_scatter | solution.py:854
  377.3 184.0 %reduce-scatter.8.cloned.1.call-start = ((), (), s32[]{:S(2)}) async-start(), calls=%async_computation.10 | async-start | bytes 15728640 | tf_op jit(solution)/shard_map/reduce_scatter | solution.py:849
  408.4 18.4 %collective-permute-start.55 = (bf16[96,768]{1,0:T(8,128)(2,1)S(1)}, bf16[96,768]{1,0:T(8,128)(2,1)S(1)}, u32[]{:S(2)}, u32[]{:S(2)}) collective-permute-start(bf16[96,768]{1,0:T(8,128)(2,1)S(1)} %get-tuple-element.214), channel_id=1, source_target_pairs={{0,20},{4,16},{8,28},{12,24},{16,4},{20,0},{24,12},{28,8},{1,21},{... | collective-permute-start | bytes 442376 | tf_op jit(solution)/shard_map/ppermute | solution.py:54
  478.4 28.4 %collective-permute-start.61 = (bf16[2,104,768]{2,1,0:T(8,128)(2,1)}, bf16[2,104,768]{2,1,0:T(8,128)(2,1)S(1)}, u32[]{:S(2)}, u32[]{:S(2)}) collective-permute-start(bf16[2,104,768]{2,1,0:T(8,128)(2,1)} %get-tuple-element.184), channel_id=1, source_target_pairs={{0,12},{4,8},{8,4},{12,0},{16,28},{20,24},{24,20},{28,16},{1,13},{... | collective-permute-start | bytes 958472 | tf_op jit(solution)/shard_map/ppermute | solution.py:54
  481.4 30.9 %collective-permute-start.60 = (bf16[2,104,768]{2,1,0:T(8,128)(2,1)}, bf16[2,104,768]{2,1,0:T(8,128)(2,1)S(1)}, u32[]{:S(2)}, u32[]{:S(2)}) collective-permute-start(bf16[2,104,768]{2,1,0:T(8,128)(2,1)} %get-tuple-element.185), channel_id=1, source_target_pairs={{0,8},{4,12},{8,0},{12,4},{16,24},{20,28},{24,16},{28,20},{1,9},{5... | collective-permute-start | bytes 958472 | tf_op jit(solution)/shard_map/ppermute | solution.py:54
  486.2 26.1 %collective-permute-start.59 = (bf16[2,104,768]{2,1,0:T(8,128)(2,1)S(1)}, bf16[2,104,768]{2,1,0:T(8,128)(2,1)S(1)}, u32[]{:S(2)}, u32[]{:S(2)}) collective-permute-start(bf16[2,104,768]{2,1,0:T(8,128)(2,1)S(1)} %get-tuple-element.180), channel_id=1, source_target_pairs={{0,4},{4,0},{8,12},{12,8},{16,20},{20,16},{24,28},{28,24},{1,5},{5... | collective-permute-start | bytes 958472 | tf_op jit(solution)/shard_map/ppermute | solution.py:54
  493.3 19.2 %collective-permute-start.65 = (bf16[2,104,768]{2,1,0:T(8,128)(2,1)S(1)}, bf16[2,104,768]{2,1,0:T(8,128)(2,1)S(1)}, u32[]{:S(2)}, u32[]{:S(2)}) collective-permute-start(bf16[2,104,768]{2,1,0:T(8,128)(2,1)S(1)} %fusion.65), channel_id=1, source_target_pairs={{0,16},{4,20},{8,24},{12,28},{16,0},{20,4},{24,8},{28,12},{1,17},{... | collective-permute-start | bytes 958472 | tf_op jit(solution)/shard_map/ppermute | solution.py:54
  (180 other events, 1864.2 us)
Sparse Core Ops, SparseCore 0:
  10.7 50.8 all-gather.3
  63.7 30.0 all-gather.5
  95.9 82.0 all-gather.7
  354.3 39.2 reduce-scatter.5
  396.7 58.4 reduce-scatter.3
  457.6 103.6 reduce-scatter.7

commit v3 on v2

--- a/solution.py
+++ b/solution.py
@@ -24,6 +24,16 @@
 MOST_FLIPS = 8
 ROWS = 256
 VMEM_BYTES = 48 << 20
+
+
+def params(name, products=0, moved=0, exps=0):
+    return dict(
+        compiler_params=pltpu.CompilerParams(vmem_limit_bytes=VMEM_BYTES),
+        cost_estimate=pl.CostEstimate(
+            flops=2 * products, bytes_accessed=moved, transcendentals=exps
+        ),
+        name=name,
+    )
 
 
 def contract_rows(left, right):
@@ -134,16 +144,16 @@
     return pl.pallas_call(
         pack_body,
         out_shape=jax.ShapeDtypeStruct((dense_w.shape[1] + 8, D), LOWER),
-        compiler_params=pltpu.CompilerParams(vmem_limit_bytes=VMEM_BYTES),
-        name="pack",
+        **params("pack", 0, 6 * dense_w.size),
     )(dense_w, small_w)
 
 
 def assemble_body(place_ref, *refs, n_dp, width, thin):
     pieces = refs[: 2 * n_dp]
-    dense_ref, small_ref, raw_ref, turned_ref, dense_sem, small_sem = refs[2 * n_dp :]
+    qkv_ref, out_ref, small_ref, raw_ref, turned_ref, dense_sem, small_sem = refs[2 * n_dp :]
     own, rep = place_ref[0], place_ref[1]
-    copies = []
+    front = qkv_ref.shape[0]
+    small_waits, dense_waits = [], []
     for m in range(n_dp):
         for pair in range(2):
             for core in range(2):
@@ -151,23 +161,22 @@
                 device = (own ^ m) * 4 + (rep ^ (2 * pair + core))
                 top = pair * (width + 8)
                 number = m * 4 + pair * 2 + core
-                copies.append(
-                    pltpu.make_async_copy(
-                        piece.at[pl.ds(top + width, 8), :],
-                        raw_ref.at[device],
-                        small_sem.at[number],
-                    )
+                small = pltpu.make_async_copy(
+                    piece.at[pl.ds(top + width, 8), :], raw_ref.at[device], small_sem.at[number]
                 )
-                copies.append(
-                    pltpu.make_async_copy(
-                        piece.at[pl.ds(top, width), :],
-                        dense_ref.at[device],
-                        dense_sem.at[number],
-                    )
+                small.start()
+                rows = piece.at[pl.ds(top, width), :]
+                into_qkv = pltpu.make_async_copy(
+                    rows, qkv_ref.at[jnp.minimum(device, front - 1)], dense_sem.at[number]
                 )
-    for copy in copies:
-        copy.start()
-    for copy in copies[::2]:
+                into_out = pltpu.make_async_copy(
+                    rows, out_ref.at[jnp.maximum(device - front, 0)], dense_sem.at[number]
+                )
+                pl.when(device < front)(into_qkv.start)
+                pl.when(device >= front)(into_out.start)
+                small_waits.append(small)
+                dense_waits.append(into_qkv)
+    for copy in small_waits:
         copy.wait()
     for device in range(4 * n_dp):
         for g in range(thin // 8):
@@ -175,7 +184,7 @@
             tile = raw_ref[device, :, g * LANES : (g + 1) * LANES]
             turned_ref[start : start + 8, :] = tile.astype(WIDE)
     small_ref[...] = turned_ref[...].T[: small_ref.shape[0], :]
-    for copy in copies[1::2]:
+    for copy in dense_waits:
         copy.wait()
 
 
@@ -186,10 +195,12 @@
         + [pl.BlockSpec(memory_space=pl.ANY)] * len(pieces),
         out_specs=[
             pl.BlockSpec(memory_space=pl.ANY),
+            pl.BlockSpec(memory_space=pl.ANY),
             pl.BlockSpec(memory_space=pltpu.VMEM),
         ],
         out_shape=[
-            jax.ShapeDtypeStruct((4 * n_dp, width, D), LOWER),
+            jax.ShapeDtypeStruct((3 * n_dp, width, D), LOWER),
+            jax.ShapeDtypeStruct((n_dp, width, D), LOWER),
             jax.ShapeDtypeStruct((24, D), WIDE),
         ],
         scratch_shapes=[
@@ -198,20 +209,17 @@
             pltpu.SemaphoreType.DMA((4 * n_dp,)),
             pltpu.SemaphoreType.DMA((4 * n_dp,)),
         ],
-        compiler_params=pltpu.CompilerParams(vmem_limit_bytes=VMEM_BYTES),
-        name="assemble",
+        **params("assemble", 0, 32 * n_dp * width * D),
     )(place, *pieces)
 
 
-def gather_weights(dense_w, small_w, place, n_dp):
-    width, thin = dense_w.shape[1], small_w.shape[1]
-    block = pack(dense_w, small_w)
+def gather_weights(block, place, n_dp, width, thin):
     both = jnp.concatenate([block, flip(block, "rep", 2, 4)])
     near, far = gather_flips(both, n_dp)
     mine = near + far
     theirs = [flip(piece, "rep", 1, 4) for piece in mine]
-    dense, small = assemble(mine + theirs, place, n_dp, width, thin)
-    return dense.reshape(-1, D), small
+    qkv, out, small = assemble(mine + theirs, place, n_dp, width, thin)
+    return qkv.reshape(-1, D), out.reshape(-1, D), small
 
 
 def dense_grad_body(
@@ -268,15 +276,32 @@
             jax.ShapeDtypeStruct((n_dp,) + block[1:], WIDE),
             jax.ShapeDtypeStruct((n_dp,) + block[1:], LOWER),
         ],
-        compiler_params=pltpu.CompilerParams(vmem_limit_bytes=VMEM_BYTES),
-        name="dense_grads",
+        **params("dense_grads", tokens * 4 * D * D, 12 * tokens * D + 24 * D * D),
     )(place, grad_qkv, grad_attn, normed, mixed, small_turned)
 
 
-def sum_weights(mine, other, n_dp):
+def sum_weights(mine, other, n_dp, jobs):
     both = mine + flip(other, "rep", 1, 4).astype(WIDE)
-    pair = sum_flips([both[m] for m in range(n_dp)], n_dp)
-    return pair[0] + flip(pair[1].astype(LOWER), "rep", 2, 4).astype(WIDE)
+    parts = [both[m] for m in range(n_dp)]
+    done = []
+
+    def beside(value, job):
+        value, result = lax.optimization_barrier((value, job(done)))
+        done.append(result)
+        return value
+
+    if n_dp > MOST_FLIPS:
+        pair = beside(beside(sum_flips(parts, n_dp), jobs[0]), jobs[1])
+    else:
+        half = n_dp // 2
+        aims = [flip(parts[half + m].astype(LOWER), "dp", m, n_dp) for m in range(1, half)]
+        near = [flip(parts[m].astype(LOWER), "dp", m, n_dp) for m in range(1, half)]
+        aims = beside(aims, jobs[0])
+        cross = flip(add_up([parts[half]] + aims).astype(LOWER), "dp", half, n_dp)
+        cross = beside(cross, jobs[1])
+        pair = add_up([parts[0]] + near + [cross])
+    far = beside(flip(pair[1].astype(LOWER), "rep", 2, 4), jobs[2])
+    return pair[0] + far.astype(WIDE), done
 
 
 def norm_fwd(hidden, gain):
@@ -356,8 +381,7 @@
         out_specs=pl.BlockSpec((tokens, 2 * HDIM), lambda j: (0, j)),
         out_shape=jax.ShapeDtypeStruct((tokens, D), LOWER),
         scratch_shapes=[pltpu.VMEM((tokens, tokens), WIDE)],
-        compiler_params=pltpu.CompilerParams(vmem_limit_bytes=VMEM_BYTES),
-        name="attend",
+        **params("attend", 2 * tokens * tokens * D, 8 * tokens * D, tokens * tokens * D // HDIM),
     )(segment[:, None], segment[None, :], qkv, qkv, qkv)
 
 
@@ -420,26 +444,212 @@
         out_specs=pl.BlockSpec((tokens, 3 * D), lambda j: (0, 0)),
         out_shape=jax.ShapeDtypeStruct((tokens, 3 * D), LOWER),
         scratch_shapes=[pltpu.VMEM((tokens, tokens), WIDE)],
-        compiler_params=pltpu.CompilerParams(vmem_limit_bytes=VMEM_BYTES),
-        name="attend_back",
+        **params("attend_back", 5 * tokens * tokens * D, 14 * tokens * D, tokens * tokens * D // HDIM),
     )(segment[:, None], segment[None, :], qkv, qkv, qkv, grad_mixed)
 
 
-def experts_forward(rows, w_in, w_out):
-    gate_pre = plain(rows, w_in[0])
-    up_pre = plain(rows, w_in[1])
-    inner = (jax.nn.silu(gate_pre) * up_pre).astype(LOWER)
-    part = plain(inner, w_out).astype(LOWER)
-    return gate_pre, up_pre, inner, part
-
-
-def experts_backward(grad_part, gate_pre, up_pre, w_in, w_out):
-    grad_inner = contract_cols(grad_part, w_out)
-    sig = jax.nn.sigmoid(gate_pre)
-    grad_gate = (grad_inner * up_pre * sig * (1.0 + gate_pre * (1.0 - sig))).astype(LOWER)
-    grad_up = (grad_inner * gate_pre * sig).astype(LOWER)
-    grad_rows = (contract_cols(grad_gate, w_in[0]) + contract_cols(grad_up, w_in[1])).astype(LOWER)
-    return grad_gate, grad_up, grad_rows
+def full(shape):
+    return pl.BlockSpec(shape, lambda *index: (0,) * len(shape))
+
+
+def experts_forward_body(*refs):
+    (*pieces, w_in_ref, w_out_ref, gate_ref, up_ref, inner_ref, rows_ref), rest = (
+        refs[: len(refs) // 2 + 3],
+        refs[len(refs) // 2 + 3 :],
+    )
+    *parts, acc_ref = rest
+    j = pl.program_id(0)
+
+    @pl.when(j == 0)
+    def _():
+        for i, piece in enumerate(pieces):
+            rows_ref[i * CAP : (i + 1) * CAP, :] = piece[...]
+        acc_ref[...] = jnp.zeros(acc_ref.shape, WIDE)
+
+    rows = rows_ref[...]
+    gate = plain(rows, w_in_ref[0])
+    up = plain(rows, w_in_ref[1])
+    inner = (jax.nn.silu(gate) * up).astype(LOWER)
+    gate_ref[...] = gate
+    up_ref[...] = up
+    inner_ref[...] = inner
+    acc_ref[...] += plain(inner, w_out_ref[...])
+
+    @pl.when(j == pl.num_programs(0) - 1)
+    def _():
+        for i, part in enumerate(parts):
+            part[...] = acc_ref[i * CAP : (i + 1) * CAP, :].astype(LOWER)
+
+
+def experts_forward(pieces, w_in, w_out):
+    rows, hidden = len(pieces) * CAP, w_out.shape[0]
+    tile = min(hidden, 512)
+    piece = full((CAP, D))
+    band = pl.BlockSpec((rows, tile), lambda j: (0, j))
+    gate, up, inner, joined, *parts = pl.pallas_call(
+        experts_forward_body,
+        grid=(hidden // tile,),
+        in_specs=[piece] * len(pieces)
+        + [
+            pl.BlockSpec((2, D, tile), lambda j: (0, 0, j)),
+            pl.BlockSpec((tile, D), lambda j: (j, 0)),
+        ],
+        out_specs=[band, band, band, full((rows, D))] + [piece] * len(pieces),
+        out_shape=[
+            jax.ShapeDtypeStruct((rows, hidden), WIDE),
+            jax.ShapeDtypeStruct((rows, hidden), WIDE),
+            jax.ShapeDtypeStruct((rows, hidden), LOWER),
+            jax.ShapeDtypeStruct((rows, D), LOWER),
+        ]
+        + [jax.ShapeDtypeStruct((CAP, D), LOWER)] * len(pieces),
+        scratch_shapes=[pltpu.VMEM((rows, D), WIDE)],
+        **params("experts_forward", 3 * rows * hidden * D, 6 * hidden * D + 10 * rows * hidden),
+    )(*pieces, w_in, w_out)
+    return gate, up, inner, joined, parts
+
+
+def experts_backward_body(*refs):
+    count = (len(refs) - 7) // 2
+    pieces, refs = refs[:count], refs[count:]
+    gate_ref, up_ref, w_in_ref, w_out_ref, backs_ref, rows_ref, *parts, acc_ref = refs
+    j = pl.program_id(0)
+
+    @pl.when(j == 0)
+    def _():
+        for i, piece in enumerate(pieces):
+            rows_ref[i * CAP : (i + 1) * CAP, :] = piece[...]
+        acc_ref[...] = jnp.zeros(acc_ref.shape, WIDE)
+
+    grad_inner = contract_cols(rows_ref[...], w_out_ref[...])
+    gate, up = gate_ref[...], up_ref[...]
+    sig = jax.nn.sigmoid(gate)
+    grad_gate = (grad_inner * up * sig * (1.0 + gate * (1.0 - sig))).astype(LOWER)
+    grad_up = (grad_inner * gate * sig).astype(LOWER)
+    backs_ref[0] = grad_gate
+    backs_ref[1] = grad_up
+    acc_ref[...] += contract_cols(grad_gate, w_in_ref[0]) + contract_cols(grad_up, w_in_ref[1])
+
+    @pl.when(j == pl.num_programs(0) - 1)
+    def _():
+        for i, part in enumerate(parts):
+            part[...] = acc_ref[i * CAP : (i + 1) * CAP, :].astype(LOWER)
+
+
+def experts_backward(pieces, gate, up, w_in, w_out):
+    rows, hidden = gate.shape
+    tile = min(hidden, 512)
+    piece = full((CAP, D))
+    band = pl.BlockSpec((rows, tile), lambda j: (0, j))
+    backs, joined, *parts = pl.pallas_call(
+        experts_backward_body,
+        grid=(hidden // tile,),
+        in_specs=[piece] * len(pieces)
+        + [
+            band,
+            band,
+            pl.BlockSpec((2, D, tile), lambda j: (0, 0, j)),
+            pl.BlockSpec((tile, D), lambda j: (j, 0)),
+        ],
+        out_specs=[pl.BlockSpec((2, rows, tile), lambda j: (0, 0, j)), full((rows, D))]
+        + [piece] * len(pieces),
+        out_shape=[
+            jax.ShapeDtypeStruct((2, rows, hidden), LOWER),
+            jax.ShapeDtypeStruct((rows, D), LOWER),
+        ]
+        + [jax.ShapeDtypeStruct((CAP, D), LOWER)] * len(pieces),
+        scratch_shapes=[pltpu.VMEM((rows, D), WIDE)],
+        **params("experts_backward", 3 * rows * hidden * D, 6 * hidden * D + 12 * rows * hidden),
+    )(*pieces, gate, up, w_in, w_out)
+    return backs, joined, parts
+
+
+def grads_in_body(
+    place_ref, rows_a, rows_b, back_a, back_b, keep_ref, give_ref, sum_ref, turned_a, turned_b
+):
+    @pl.when((pl.program_id(0) == 0) & (pl.program_id(1) == 0))
+    def _():
+        turned_a[...] = rows_a[...].T
+        turned_b[...] = rows_b[...].T
+
+    sum_ref[...] = plain(turned_a[...], back_a[0]) + plain(turned_b[...], back_b[0])
+    size = keep_ref.shape[2]
+    for pair in range(2):
+        for core, out_ref in enumerate((keep_ref, give_ref)):
+            start = pl.multiple_of((place_ref[1] ^ (2 * pair + core)) * size, 8)
+            out_ref[0, pair] = sum_ref[pl.ds(start, size), :].astype(LOWER)
+
+
+def grads_in(place, rows_a, rows_b, back_a, back_b):
+    rows, hidden = back_a.shape[1:]
+    tile = 512
+    size = D // 4
+    back = pl.BlockSpec((1, rows, tile), lambda k, j, place: (k, 0, j))
+    out = pl.BlockSpec((1, 2, size, tile), lambda k, j, place: (k, 0, 0, j))
+    return pl.pallas_call(
+        grads_in_body,
+        grid_spec=pltpu.PrefetchScalarGridSpec(
+            num_scalar_prefetch=1,
+            grid=(2, hidden // tile),
+            in_specs=[full((rows, D)), full((rows, D)), back, back],
+            out_specs=[out, out],
+            scratch_shapes=[pltpu.VMEM((D, tile), WIDE)] + [pltpu.VMEM((D, rows), LOWER)] * 2,
+        ),
+        out_shape=[jax.ShapeDtypeStruct((2, 2, size, hidden), LOWER)] * 2,
+        **params("grads_in", 4 * rows * hidden * D, 4 * hidden * D + 8 * rows * hidden),
+    )(place, rows_a, rows_b, back_a, back_b)
+
+
+def grads_out_body(place_ref, inner_a, inner_b, back_a, back_b, out_ref):
+    total = contract_rows(inner_a[...], back_a[...]) + contract_rows(inner_b[...], back_b[...])
+    out_ref[0] = total.astype(LOWER)
+
+
+def grads_out(place, core, inner_a, inner_b, back_a, back_b):
+    rows, hidden = inner_a.shape
+    size = hidden // 4
+    band = pl.BlockSpec((rows, size), lambda x, place: (0, place[1] ^ (2 * x + core)))
+    return pl.pallas_call(
+        grads_out_body,
+        grid_spec=pltpu.PrefetchScalarGridSpec(
+            num_scalar_prefetch=1,
+            grid=(2,),
+            in_specs=[band, band, full((rows, D)), full((rows, D))],
+            out_specs=pl.BlockSpec((1, size, D), lambda x, place: (x, 0, 0)),
+        ),
+        out_shape=jax.ShapeDtypeStruct((2, size, D), LOWER),
+        **params("grads_out", rows * hidden * D, hidden * D + 2 * rows * hidden),
+    )(place, inner_a, inner_b, back_a, back_b)
+
+
+def sum_experts_out(place, near, far, near_back, far_back, came_back):
+    if lax.axis_size("rep") != 4:
+        grad = contract_rows(
+            jnp.concatenate([near[2], far[2]]), jnp.concatenate([near_back[1], far_back[1]])
+        ).astype(LOWER)
+        return [lax.psum_scatter(grad, "rep", scatter_dimension=0, tiled=True)], came_back
+    came_back, rows = lax.optimization_barrier((came_back, (near_back[1], far_back[1])))
+    ends = (near[2], far[2]) + rows
+    give, keep = grads_out(place, 1, *ends), grads_out(place, 0, *ends)
+    came_back, give, keep = lax.optimization_barrier((came_back, give, keep))
+    take = flip(give, "rep", 1, 4)
+    return [keep[0], take[0], (keep[1].astype(WIDE) + take[1].astype(WIDE)).astype(LOWER)], came_back
+
+
+def sum_experts_in(place, near, far, near_back, far_back, after):
+    if lax.axis_size("rep") != 4:
+        rows = jnp.concatenate([near[3], far[3]])
+        backs = jnp.concatenate([near_back[0], far_back[0]], 1)
+        grad = jnp.stack([contract_rows(rows, back).astype(LOWER) for back in backs])
+        return [lax.psum_scatter(grad, "rep", scatter_dimension=1, tiled=True)], after
+    after, backs = lax.optimization_barrier((after, (near_back[0], far_back[0])))
+    keep, give = grads_in(place, near[3], far[3], *backs)
+    take = flip(give, "rep", 1, 4)
+    far = [(keep[k, 1].astype(WIDE) + take[k, 1].astype(WIDE)).astype(LOWER) for k in range(2)]
+    return [keep[:, 0], take[:, 0], far], after
+
+
+def add_up(parts):
+    return sum([part.astype(WIDE) for part in parts[1:]], parts[0].astype(WIDE))
 
 
 def cut(value, count):
@@ -450,12 +660,11 @@
 def send_slots(buffer, n_dp, shards):
     half = n_dp // 2
     blocks = trade([b for b in cut(buffer, EXPERTS) for _ in range(shards)], n_dp)
-    return jnp.concatenate(blocks[:half]), jnp.concatenate(blocks[half:])
+    return blocks[:half], blocks[half:]
 
 
 def return_slots(near, far, n_dp, shards):
-    half = n_dp // 2
-    blocks = trade(cut(near, half) + cut(far, half), n_dp)
+    blocks = trade(list(near) + list(far), n_dp)
     return [jnp.concatenate(blocks[s::shards]) for s in range(shards)]
 
 
@@ -463,7 +672,7 @@
     return sum(plain(picks, part) for part in received)
 
 
-def layer_forward(hidden, lens, routes, dense_t, small_all, w_in, w_out, own, n_dp):
+def layer_forward(hidden, lens, routes, w_qkv, w_attn, small_all, w_in, w_out, own, n_dp):
     shards = n_dp // EXPERTS
     gains, const_vec, router, const_gate = (
         small_all[:3].astype(WIDE),
@@ -475,9 +684,9 @@
     segment = segments(lens, tokens)
     normed, scale_one = norm_fwd(hidden, gains[0])
     normed_low = normed.astype(LOWER)
-    qkv = contract_cols(normed_low, dense_t[: 3 * D]).astype(LOWER)
+    qkv = contract_cols(normed_low, w_qkv).astype(LOWER)
     mixed = attend(qkv, segment)
-    first = hidden + contract_cols(mixed, dense_t[3 * D :])
+    first = hidden + contract_cols(mixed, w_attn)
     second, scale_two = norm_fwd(first, gains[1])
     second_low = second.astype(LOWER)
     route_p = jax.nn.softmax(contract_cols(second_low, router), -1)
@@ -498,7 +707,7 @@
     buffer = contract_rows(both, second_low).astype(LOWER)
     sent = send_slots(buffer, n_dp, shards)
     near, far = (experts_forward(rows, w_in, w_out) for rows in sent)
-    returned = return_slots(near[3], far[3], n_dp, shards)
+    returned = return_slots(near[4], far[4], n_dp, shards)
     outs = [pick_slots(picks[k], returned) for k in range(2)]
     moe = w_slot[:, 0:1] * outs[0] + w_slot[:, 1:2] * outs[1]
     const_p = jax.nn.softmax(contract_cols(second_low, const_gate).reshape(tokens, 2, 2), -1)
@@ -531,7 +740,6 @@
         w_slot=w_slot,
         picks=picks,
         both=both,
-        rows=sent,
         near=near,
         far=far,
         outs=outs,
@@ -597,8 +805,7 @@
             jax.ShapeDtypeStruct((steps, 1, count), WIDE),
             jax.ShapeDtypeStruct((8, count), WIDE),
         ],
-        compiler_params=pltpu.CompilerParams(vmem_limit_bytes=VMEM_BYTES),
-        name="vocab_scores",
+        **params("vocab_scores", count * vocab * D, 2 * vocab * (count + D), count * vocab),
     )(aim, rows, table)
 
 
@@ -642,8 +849,7 @@
             jax.ShapeDtypeStruct((vocab, count), LOWER),
             jax.ShapeDtypeStruct((count, D), WIDE),
         ],
-        compiler_params=pltpu.CompilerParams(vmem_limit_bytes=VMEM_BYTES),
-        name="vocab_grad_rows",
+        **params("vocab_grad_rows", count * vocab * D, 2 * vocab * (2 * count + D)),
     )(aim, scale, expo, table)
 
 
@@ -663,8 +869,7 @@
         ],
         out_specs=pl.BlockSpec((tile, D), lambda j: (j, 0)),
         out_shape=jax.ShapeDtypeStruct((vocab, D), LOWER),
-        compiler_params=pltpu.CompilerParams(vmem_limit_bytes=VMEM_BYTES),
-        name="vocab_grad_table",
+        **params("vocab_grad_table", count * vocab * D, 2 * vocab * (count + D)),
     )(grad, rows)
 
 
@@ -697,7 +902,7 @@
     return (loss_part, grad_third, grad_gain, grad_table)
 
 
-def layer_backward(hidden, grad_third, saved, dense_t, w_in, w_out, n_dp):
+def layer_backward(hidden, grad_third, saved, w_qkv, w_attn, w_in, w_out, n_dp, place):
     shards = n_dp // EXPERTS
     gains, const_vec = saved["gains"], saved["const_vec"]
     router, const_gate = saved["router"], saved["const_gate"]
@@ -713,16 +918,8 @@
     near_back = experts_backward(sent[0], near[0], near[1], w_in, w_out)
     far_back = experts_backward(sent[1], far[0], far[1], w_in, w_out)
     came_back = return_slots(near_back[2], far_back[2], n_dp, shards)
-    rows = jnp.concatenate(saved["rows"])
-    grad_w_out = contract_rows(
-        jnp.concatenate([near[2], far[2]]), jnp.concatenate(sent)
-    ).astype(LOWER)
-    grad_w_in = jnp.stack(
-        [
-            contract_rows(rows, jnp.concatenate([near_back[k], far_back[k]])).astype(LOWER)
-            for k in range(2)
-        ]
-    )
+    ends = (place, near, far, near_back, far_back)
+    eout_g, came_back = sum_experts_out(*ends, came_back)
     dots = [jnp.sum(saved["outs"][k] * grad_third, -1, keepdims=True) for k in range(2)]
     hits = saved["hits"].astype(WIDE)
     grad_real = (dots[0] * hits[:, 0] + dots[1] * hits[:, 1])[:, :EXPERTS]
@@ -757,12 +954,13 @@
     )
     grad_first = grad_third + grad_first_norm
     grad_attn = grad_first.astype(LOWER)
-    grad_mixed = plain(grad_attn, dense_t[3 * D :]).astype(LOWER)
+    grad_mixed = plain(grad_attn, w_attn).astype(LOWER)
     grad_qkv = attend_back(saved["qkv"], grad_mixed, saved["segment"])
-    grad_normed = plain(grad_qkv, dense_t[: 3 * D])
+    grad_qkv, eout_g = lax.optimization_barrier((grad_qkv, eout_g))
+    grad_normed = plain(grad_qkv, w_qkv)
     unused, grad_gain_one = norm_back(hidden, saved["scale_one"], gains[0], grad_normed)
     left = (grad_qkv, grad_attn)
-    return (left, grad_gain_one, grad_gain_two, grad_cvec, grad_gates, grad_w_in, grad_w_out)
+    return (left, grad_gain_one, grad_gain_two, grad_cvec, grad_gates, ends, eout_g)
 
 
 def fold(value):
@@ -773,8 +971,8 @@
     return jnp.sum(squares.reshape(8, cols // LANES, LANES), (0, 1))
 
 
-def group_squares(arrays, device):
-    dense, small, ein, eout, tab = arrays
+def own_squares(arrays, device):
+    dense, small = arrays
     width = dense.shape[1]
     front = (device * width + jnp.arange(width, dtype=jnp.int32) < 3 * D).astype(WIDE)
     lanes = (0, LANES - width)
@@ -784,18 +982,24 @@
         jnp.pad(dense_sq * (1.0 - front), lanes),
         jnp.pad(jnp.sum(small[:5] * small[:5], 0), (0, LANES - small.shape[1])),
         jnp.pad(jnp.sum(small[5:] * small[5:], 0), (0, LANES - small.shape[1])),
-        fold(ein.reshape(-1, ein.shape[-1])),
-        fold(eout),
-        fold(tab),
     ]
+
+
+def update_of(weight, first, second):
+    corr = 1.0 - 0.5**STEP
+    return first / corr / (jnp.sqrt(second / corr) + EPS) + 0.01 * weight
 
 
 def moments(weight, first, second, grad):
     first = 0.5 * first + 0.5 * grad
     second = 0.5 * second + 0.5 * grad * grad
-    corr = 1.0 - 0.5**STEP
-    update = first / corr / (jnp.sqrt(second / corr) + EPS) + 0.01 * weight
-    return (first, second, update)
+    return (first, second, update_of(weight, first, second))
+
+
+def shared_update(weight, first, second, parts):
+    first, second, update = moments(weight, first, second, add_up(parts))
+    lanes = weight.shape[-1]
+    return (first, second, fold(weight.reshape(-1, lanes)), fold(update.reshape(-1, lanes)))
 
 
 def local(
@@ -828,40 +1032,60 @@
     width, thin = dense_w.shape[1], small_w.shape[1]
     place = jnp.stack([own, lax.axis_index("rep")]).astype(jnp.int32)
     flips = n_rep == 4 and width % 16 == 0 and thin % 8 == 0
+    shared = (expert_in, expert_out, table)
     if flips:
-        dense_t, small_all = gather_weights(dense_w, small_w, place, n_dp)
+        block, shared = lax.optimization_barrier((pack(dense_w, small_w), shared))
+        w_qkv, w_attn, small_all = gather_weights(block, place, n_dp, width, thin)
     else:
         dense_t = lax.all_gather(dense_w.T.astype(LOWER), BOTH, axis=0, tiled=True)
         small_t = jnp.pad(small_w.T.astype(LOWER), ((0, 0), (0, LANES - small_w.shape[0])))
         small_all = share(small_t, BOTH, devices).reshape(-1, LANES).T
+        w_qkv, w_attn = dense_t[: 3 * D], dense_t[3 * D :]
     w_in, w_out, table_all = (
-        lax.all_gather(expert_in.astype(LOWER), "rep", axis=1, tiled=True),
-        lax.all_gather(expert_out.astype(LOWER), "rep", axis=0, tiled=True),
-        lax.all_gather(table.astype(LOWER), "rep", axis=0, tiled=True),
+        lax.all_gather(value.astype(LOWER), "rep", axis=axis, tiled=True)
+        for value, axis in zip(shared, (1, 0, 0))
     )
     hidden = x_in.astype(WIDE)
     third, saved = layer_forward(
-        hidden, seq_lens[0], routes, dense_t, small_all, w_in, w_out, own, n_dp
+        hidden, seq_lens[0], routes, w_qkv, w_attn, small_all, w_in, w_out, own, n_dp
     )
     loss_part, grad_third, grad_gain_final, grad_table = head_step(
         third, positions, targets[0], table_all, saved["gains"][2], own, n_dp
     )
     table_g = lax.psum_scatter(grad_table, "rep", scatter_dimension=0, tiled=True)
-    left, gain_one, gain_two, grad_cvec, grad_gates, grad_w_in, grad_w_out = layer_backward(
-        hidden, grad_third, saved, dense_t, w_in, w_out, n_dp
-    )
-    ein_g, eout_g = (
-        lax.psum_scatter(grad_w_in, "rep", scatter_dimension=1, tiled=True),
-        lax.psum_scatter(grad_w_out, "rep", scatter_dimension=0, tiled=True),
+    left, gain_one, gain_two, grad_cvec, grad_gates, ends, eout_g = layer_backward(
+        hidden, grad_third, saved, w_qkv, w_attn, w_in, w_out, n_dp, place
     )
     small_grad = jnp.concatenate(
         [gain_one[None], gain_two[None], grad_gain_final[None], grad_cvec, grad_gates], 0
     )
+    loss_row = jnp.pad(loss_part[None], (0, LANES - 1))
+
+    def crossed(value):
+        return flip(value, "rep", 2, 4) if n_rep == 4 else value
+
+    def table_job(done):
+        return shared_update(table, table_m, table_v, [table_g]), crossed(eout_g[-1])
+
+    def out_job(done):
+        made = shared_update(expert_out, expout_m, expout_v, eout_g[:-1] + [done[0][1]])
+        if n_rep != 4:
+            return made, None
+        return made, crossed(ein_g[2][0])
+
+    def in_job(done):
+        parts = ein_g
+        if n_rep == 4:
+            parts = ein_g[:2] + [jnp.stack([done[1][1], crossed(ein_g[2][1])])]
+        return shared_update(expert_in, expin_m, expin_v, parts), None
+
+    jobs = (table_job, out_job, in_job)
     normed, mixed = saved["normed_low"], saved["mixed"]
     if flips:
         turned = jnp.pad(small_grad, ((0, LANES - small_grad.shape[0]), (0, 0))).T
         mine, other = dense_grads(place, *left, normed, mixed, turned, n_dp, width)
-        block = sum_weights(mine, other, n_dp)
+        ein_g, other = sum_experts_in(*ends, other)
+        block, done = sum_weights(mine, other, n_dp, jobs)
         small_g = block[width:].reshape(8, -1, LANES)[:, : thin // 8].swapaxes(0, 1)
         small_g = small_g.reshape(thin, LANES)[:, : small_w.shape[0]].T
     else:
@@ -876,18 +1100,26 @@
         )
         block = scatter_sum(blocks.reshape((n_dp, n_rep) + blocks.shape[1:]), n_dp, n_rep)
         small_g = block[width:].reshape(-1)[: small_w.size].reshape(small_w.shape)
+        ein_g, block = sum_experts_in(*ends, block)
+        done = []
+        for job in jobs:
+            done.append(job(done))
     dense_g = block[:width].T
-    grads = (dense_g, small_g, ein_g.astype(WIDE), eout_g.astype(WIDE), table_g.astype(WIDE))
-    firsts = (dense_m, small_m, expin_m, expout_m, table_m)
-    seconds = (dense_v, small_v, expin_v, expout_v, table_v)
-    results = [moments(w, m, v, g) for w, m, v, g in zip(masters, firsts, seconds, grads)]
-    update_parts = group_squares(tuple((r[2] for r in results)), device)
-    loss_row = jnp.pad(loss_part[None], (0, LANES - 1))
-    parts = jnp.stack(group_squares(masters, device) + update_parts + [loss_row, loss_row * 0.0])
-    sums = jnp.sum(share(parts, BOTH, devices), (0, 2))
+    own_results = [
+        moments(w, m, v, g)
+        for w, m, v, g in ((dense_w, dense_m, dense_v, dense_g), (small_w, small_m, small_v, small_g))
+    ]
+    made = [done[2][0], done[1][0], done[0][0]]
+    rows = own_squares((dense_w, small_w), device) + [one[2] for one in made]
+    rows = rows + own_squares([r[2] for r in own_results], device) + [one[3] for one in made]
+    rows = jnp.stack(rows + [loss_row, loss_row * 0.0])
+    sums = jnp.sum(share(rows, BOTH, devices), (0, 2))
+    shared_results = [(m, v, update_of(w, m, v)) for w, (m, v, *_) in zip(masters[2:], made)]
+    results = own_results + shared_results
     loss = sums[14]
-    weight_norm = jnp.sqrt(sums[:7])
-    update_norm = jnp.sqrt(sums[7:14])
+    weight_sq, update_sq = sums[:7], sums[7:14]
+    weight_norm = jnp.sqrt(weight_sq)
+    update_norm = jnp.sqrt(update_sq)
     trust = weight_norm / update_norm
     column = device * width + jnp.arange(width, dtype=jnp.int32)
     dense_scale = jnp.where(column < 3 * D, trust[0], trust[1])[None, :]

time: 641 us -> 569 us (0.89); the launches traced: 629 us -> 563 us
  waiting for transfers between devices: 152 us -> 90 us
  Pallas kernels: 99.9 us -> 157 us
  matrix products: 78.6 us -> 29.9 us
  local copies, waits for them, and re-layouts: 56.9 us -> 38.8 us
    pallas_call x0 -> x7, Pallas kernels: none -> 56.9 us  [the longest x2 20.1 us: experts_backward(): pl.pallas_call(experts_backward_body, grid=(hidden // tile,), in_specs=[p...]
    ppermute x67 -> x72, waiting for transfers between devices: 124 us -> 80.7 us  [flip(): return lax.ppermute(value, axis, [(i, i ^ mask) for i in range(size)])]
    dot_general x13 -> x7, matrix products: 29.5 us -> 9.97 us  [plain(): return jnp.dot(left, right, preferred_element_type=WIDE)]
    reduce_scatter x1, waiting for transfers between devices: 18.2 us -> 0.01 us  [local(): lax.psum_scatter(grad_table, 'rep', scatter_dimension=0, tiled=True)]
    dot_general x10 -> x4, matrix products: 22.9 us -> 7.44 us  [contract_cols(): lax.dot_general(left, right, (((1,), (1,)), ((), ())), preferred_element_...]
    dot_general x6 -> x3, matrix products: 16.8 us -> 3.05 us  [contract_rows(): lax.dot_general(left, right, (((0,), (0,)), ((), ())), preferred_element_...]
    unnamed x316 -> x293, local copies, waits for them, and re-layouts: 32.9 us -> 21 us
    convert_element_type x3 -> x6, other arithmetic: 8.98 us -> 16.1 us  [the longest x3 10.4 us: local(): value.astype(LOWER)]
  transfers between devices with their start and end apart: 74 -> 77, of which waited for: 31 -> 22; matrix products, arithmetic and copies ran while one was open for 24% -> 21% of each run, Pallas kernels for 8% -> 19%
where the time goes in v3:
time: 569 us; the launch traced here: 563 us
  Pallas kernels  157 us (28%)
  starting transfers between devices  110 us (19%)
  other arithmetic  107 us (19%)
  waiting for transfers between devices  90 us (16%)
  local copies, waits for them, and re-layouts  38.8 us (7%)
  matrix products  29.9 us (5%)
  between operations  18.7 us (3%)
  blocking collectives  12.5 us (2%)
    ppermute x72, starting transfers between devices, flip(): return lax.ppermute(value, axis, [(i, i ^ mask) for i in range(size)])  107 us
    ppermute x72, waiting for transfers between devices, flip(): return lax.ppermute(value, axis, [(i, i ^ mask) for i in range(size)])  80.7 us
    pallas_call x1, Pallas kernels, vocab_scores(): pl.pallas_call(functools.partial(scores_body, step_rows=ROWS), grid=(step...  27 us
    reduce_sum x9, other arithmetic, fold(): return jnp.sum(squares.reshape(8, cols // LANES, LANES), (0, 1))  23.2 us
    convert_element_type x5, other arithmetic, local(): outs += [r[0], r[1], fresh, fresh.astype(LOWER)]  21.7 us
    pallas_call x1, Pallas kernels, vocab_grad_rows(): pl.pallas_call(functools.partial(dlogits_body, step_rows=ROWS, unit=unit)...  21.2 us
    unnamed x293, local copies, waits for them, and re-layouts  21 us
    pallas_call x2, Pallas kernels, experts_backward(): pl.pallas_call(experts_backward_body, grid=(hidden // tile,), in_specs=[p...  20.1 us
  transfers between devices with their start and end apart: 77, of which 22 were waited for; matrix products, arithmetic and copies ran while one was open for 21% of the time, Pallas kernels for 19%

profile of v3, /device:TPU:0, one launch (start us, length us, event | category | flops | bytes accessed | tf_op | source)
XLA Modules:
  0.0 563.5 jit_solution(2275117504236652183)
XLA Ops:
  15.0 4.8 convert_element_type.331
  36.9 15.8 %collective-permute-done.4.refs_4_ = bf16[208,768]{1,0:T(8,128)(2,1)S(1)} collective-permute-done((bf16[208,768]{1,0:T(8,128)(2,1)S(1)}, bf16[208,768]{1,0:T(8,128)(2,1)S(1)}, u32[]{:S(2)}, u32[]{:S(2)}) %collective-permute-start.4) | collective-permute-done | bytes 319520 | tf_op jit(solution)/shard_map/ppermute | solution.py:64
  65.2 4.6 collective-permute-done.7.refs_7_
  77.4 4.0 convolution_convert_fusion.q_ref.k_ref.v_ref
  82.3 7.9 %attend.1.mixed_ref = bf16[512,768]{1,0:T(8,128)(2,1)S(1)} custom-call(s32[512,1]{1,0:T(8,128)S(1)} %convert_add_fusion.4.seg_col, s32[1,512]{1,0:T(1,128)S(1)} %fusion.78.seg_row, bf16[512,2304]{1,0:T(8,128)(2,1)S(1)} %convolution_convert_fusion.q_ref.k_ref.v_ref, bf16[512,2304]{1,0:T(8,128)(2,1)S(1)} %convolution_convert_fusion.q_ref.k_ref.v_ref, ...), custom_call_target="tpu_custom_call" | custom-call | flops 805306368 | bytes 3145728 | tf_op jit(solution)/shard_map/attend/pallas_call | solution.py:373
  123.5 9.4 %experts_forward.2 = (f32[384,2048]{1,0:T(8,128)}, f32[384,2048]{1,0:T(8,128)}, bf16[384,2048]{1,0:T(8,128)(2,1)S(1)}, bf16[384,768]{1,0:T(8,128)(2,1)S(1)}, bf1...) custom-call(bf16[96,768]{1,0:T(8,128)(2,1)S(1)} %get-tuple-element.3, ...), custom_call_target="tpu_custom_call" | custom-call | flops 3623878656 | bytes 17301504 | tf_op jit(solution)/shard_map/experts_forward/pallas_call | solution.py:489
  138.5 9.2 %experts_forward.3 = (f32[384,2048]{1,0:T(8,128)}, f32[384,2048]{1,0:T(8,128)}, bf16[384,2048]{1,0:T(8,128)(2,1)S(1)}, bf16[384,768]{1,0:T(8,128)(2,1)S(1)}, bf1...) custom-call(bf16[96,768]{1,0:T(8,128)(2,1)} %collective-permute-done, ...), custom_call_target="tpu_custom_call" | custom-call | flops 3623878656 | bytes 17301504 | tf_op jit(solution)/shard_map/experts_forward/pallas_call | solution.py:489
  155.6 9.7 %collective-permute-done.26 = bf16[96,768]{1,0:T(8,128)(2,1)S(1)} collective-permute-done((bf16[96,768]{1,0:T(8,128)(2,1)S(1)}, bf16[96,768]{1,0:T(8,128)(2,1)S(1)}, u32[]{:S(2)}, u32[]{:S(2)}) %collective-permute-start.26) | collective-permute-done | bytes 147488 | tf_op jit(solution)/shard_map/ppermute | solution.py:64
  175.3 5.6 collective-permute-start.31
  184.2 6.3 %collective-permute-done.33 = bf16[128,768]{1,0:T(8,128)(2,1)S(1)} collective-permute-done((bf16[128,768]{1,0:T(8,128)(2,1)S(1)}, bf16[128,768]{1,0:T(8,128)(2,1)S(1)}, u32[]{:S(2)}, u32[]{:S(2)}) %collective-permute-start.33) | collective-permute-done | bytes 196640 | tf_op jit(solution)/shard_map/ppermute | solution.py:64
  204.6 27.0 %vocab_scores.1 = (bf16[8192,1024]{1,0:T(8,128)(2,1)}, f32[8,1,1024]{2,1,0:T(1,128)S(1)}, f32[8,1024]{1,0:T(8,128)S(1)}) custom-call(s32[1,1024]{1,0:T(1,128)S(1)} %bitcast.264, bf16[1024,768]{1,0:T(8,128)(2,1)S(1)} %copy-done.14, bf16[8192,768]{1,0:T(8,128)(2,1)} %all-gather.8.cloned.1.call-done.table_ref), custom_call_target="tpu_custom_call" | custom-call | flops 12884901888 | bytes 29360128 | tf_op jit(solution)/shard_map/vocab_scores/pallas_call | solution.py:790
  231.8 12.5 %all_to_all.10 = f32[8,8,8,128]{3,1,2,0:T(8,128)S(1)} all-to-all(f32[8,8,8,128]{3,1,2,0:T(8,128)S(1)} %broadcast_in_dim.126), channel_id=1, replica_groups=mesh['dp'=8,'rep'=4] {'dp'}, dimensions={0} | all-to-all | bytes 524288 | tf_op jit(solution)/shard_map/all_to_all | solution.py:56
  247.3 21.2 %vocab_grad_rows.1 = (bf16[8192,1024]{1,0:T(8,128)(2,1)}, f32[1024,768]{1,0:T(8,128)S(1)}) custom-call(s32[1,1024]{1,0:T(1,128)S(1)} %bitcast.265, f32[8,1,1024]{2,1,0:T(1,128)S(1)} %exponential_multiply_fusion.scale_ref, bf16[8192,1024]{1,0:T(8,128)(2,1)} %get-tuple-element.117.expo_ref, bf16[8192,768]{1,0:T(8,128)(2,1)} %all-gather.8.cloned.1.call-done.table_ref), custom_call_target="tpu_custom_call" | custom-call | flops 12884901888 | bytes 46137344 | tf_op jit(solution)/shard_map/vocab_grad_rows/pallas_call | solution.py:835
  279.2 4.5 collective-permute-done.41
  284.5 18.0 %vocab_grad_table.1 = bf16[8192,768]{1,0:T(8,128)(2,1)} custom-call(bf16[8192,1024]{1,0:T(8,128)(2,1)} %get-tuple-element.119.grad_ref, bf16[1024,768]{1,0:T(8,128)(2,1)S(1)} %copy-done.15), custom_call_target="tpu_custom_call" | custom-call | flops 12884901888 | bytes 29360128 | tf_op jit(solution)/shard_map/vocab_grad_table/pallas_call | solution.py:863
  310.9 4.3 multiply_reduce_fusion.12
  341.8 9.9 %experts_backward.2 = (bf16[2,384,2048]{2,1,0:T(8,128)(2,1)S(1)}, bf16[384,768]{1,0:T(8,128)(2,1)S(1)}, bf16[96,768]{1,0:T(8,128)(2,1)S(1)}, bf16[96,768]{1,0:T(...) custom-call(bf16[96,768]{1,0:T(8,128)(2,1)S(1)} %get-tuple-element.333.refs_0_, ...), custom_call_target="tpu_custom_call" | custom-call | flops 3623878656 | bytes 18874368 | tf_op jit(solution)/shard_map/experts_backward/pallas_call | solution.py:543
  357.0 10.1 %experts_backward.3 = (bf16[2,384,2048]{2,1,0:T(8,128)(2,1)S(1)}, bf16[384,768]{1,0:T(8,128)(2,1)S(1)}, bf16[96,768]{1,0:T(8,128)(2,1)S(1)}, bf16[96,768]{1,0:T(...) custom-call(bf16[96,768]{1,0:T(8,128)(2,1)} %collective-permute-done.50.refs_0_, ...), custom_call_target="tpu_custom_call" | custom-call | flops 3623878656 | bytes 18874368 | tf_op jit(solution)/shard_map/experts_backward/pallas_call | solution.py:543
  395.0 14.2 %attend_back.1.qkv_ref = bf16[512,2304]{1,0:T(8,128)(2,1)S(1)} custom-call(s32[512,1]{1,0:T(8,128)S(1)} %convert_add_fusion.4.seg_col, s32[1,512]{1,0:T(1,128)S(1)} %copy-done.17, bf16[512,2304]{1,0:T(8,128)(2,1)S(1)} %convolution_convert_fusion.q_ref.k_ref.v_ref, bf16[512,2304]{1,0:T(8,128)(2,1)S(1)} %convolution_convert_fusion.q_ref.k_ref.v_ref, ...), custom_call_target="tpu_custom_call" | custom-call | flops 2013265920 | bytes 5505024 | tf_op jit(solution)/shard_map/attend_back/pallas_call | solution.py:435
  417.3 7.6 %dense_grads.1 = (f32[8,2,104,768]{3,2,1,0:T(8,128)}, bf16[8,2,104,768]{3,2,1,0:T(8,128)(2,1)}) custom-call(s32[2]{0:T(128)S(1)} %copy-done.19, bf16[512,2304]{1,0:T(8,128)(2,1)S(1)} %copy-done.5, bf16[512,768]{1,0:T(8,128)(2,1)S(1)} %copy-done.9, bf16[512,768]{1,0:T(8,128)(2,1)S(1)} %copy-done.7, bf16[512,768]{1,0:T(8,128)(2,1)S(1)} %attend.1.mixed_ref, ...), custom_call_target="tpu_custom_call" | custom-call | flops 2415919104 | bytes 18874368 | tf_op jit(solution)/shard_map/dense_grads/pallas_call | solution.py:260
  425.3 12.5 %grads_in.1 = (bf16[2,2,192,2048]{3,2,1,0:T(8,128)(2,1)S(1)}, bf16[2,2,192,2048]{3,2,1,0:T(8,128)(2,1)}) custom-call(s32[2]{0:T(128)S(1)} %copy-done.19, bf16[384,768]{1,0:T(8,128)(2,1)S(1)} %copy-done.23, bf16[384,768]{1,0:T(8,128)(2,1)S(1)} %copy-done.25, bf16[2,384,2048]{2,1,0:T(8,128)(2,1)} %copy-done.20, bf16[2,384,2048]{2,1,0:T(8,128)(2,1)} %copy-done.21), custom_call_target="tpu_custom_call" | custom-call | flops 4831838208 | bytes 12582912 | tf_op jit(solution)/shard_map/grads_in/pallas_call | solution.py:588
  440.3 6.4 %collective-permute-start.66 = (bf16[512,768]{1,0:T(8,128)(2,1)}, bf16[512,768]{1,0:T(8,128)(2,1)}, u32[]{:S(2)}, u32[]{:S(2)}) collective-permute-start(bf16[512,768]{1,0:T(8,128)(2,1)} %fusion.23), channel_id=1, source_target_pairs={{0,2},{1,3},{2,0},{3,1},{4,6},{5,7},{6,4},{7,5},{8,10},{9,11},{10,... | collective-permute-start | bytes 2359304 | tf_op jit(solution)/shard_map/ppermute | solution.py:64
  446.7 6.3 %fusion.105 = (bf16[8,2,104,768]{3,2,1,0:T(8,128)(2,1)S(1)}, f32[8,2,104,768]{3,2,1,0:T(8,128)}) fusion(f32[8,2,104,768]{3,2,1,0:T(8,128)} %get-tuple-element.144, bf16[8,2,104,768]{3,2,1,0:T(8,128)(2,1)} %collective-permute-done.59), kind=kLoop, calls=%fused_computation.299 | loop fusion | flops 3833856 | bytes 15335424 | tf_op jit(solution)/shard_map/convert.6
  454.8 5.4 collective-permute-start.64
  464.3 12.6 %multiply_reduce_fusion = (f32[768]{0:T(1024)S(1)}, f32[768]{0:T(1024)S(1)}, f32[2048,768]{1,0:T(8,128)}, f32[2048,768]{1,0:T(8,128)}) fusion(f32[2048,768]{1,0:T(8,128)} %param.29, bf16[2048,768]{1,0:T(8,128)(2,1)} %reduce-scatter.2.cloned.1.call-done, f32[2048,768]{1,0:T(8,128)} %param.39, f32[2048,768]{1,0:T(8,128)} %param.34), kind=kLoop, calls=%fused_computation.4 | loop fusion | flops 26737152 | bytes 34609152 | tf_op jit(solution)/shard_map/reduce_sum | solution.py:971
  488.1 4.4 multiply_reduce_fusion.5
  492.5 9.6 %collective-permute-done.67 = bf16[2,104,768]{2,1,0:T(8,128)(2,1)S(1)} collective-permute-done((bf16[2,104,768]{2,1,0:T(8,128)(2,1)S(1)}, bf16[2,104,768]{2,1,0:T(8,128)(2,1)S(1)}, u32[]{:S(2)}, u32[]{:S(2)}) %collective-permute-start.67) | collective-permute-done | bytes 319520 | tf_op jit(solution)/shard_map/ppermute | solution.py:64
  505.2 6.1 %multiply_reduce_fusion.2 = (f32[2048]{0:T(1024)S(1)}, f32[2048]{0:T(1024)S(1)}, f32[2,192,2048]{2,1,0:T(8,128)}, f32[2,192,2048]{2,1,0:T(8,128)}) fusion(f32[2,192,2048]{2,1,0:T(8,128)S(1)} %copy-done.32, bf16[1,192,2048]{2,1,0:T(8,128)(2,1)S(1)} %bitcast.270, bf16[1,192,2048]{2,1,0:T(8,128)(2,1)} %bitcast.61, ...), kind=kLoop, calls=%fused_computation.13 | loop fusion | flops 18870272 | bytes 20463616 | tf_op jit(solution)/shard_map/reduce_sum | solution.py:971
  517.9 9.2 %all-to-all-done.1 = f32[32,16,128]{2,1,0:T(8,128)S(1)} async-done(((f32[32,16,128]{2,1,0:T(8,128)}), f32[32,16,128]{2,1,0:T(8,128)S(1)}, u32[]{:S(2)}, u32[]{:S(2)}) %all-to-all-start.1) | async-done | bytes 262176 | tf_op jit(solution)/shard_map/all_to_all | solution.py:56
  537.3 7.8 %fusion.97 = (bf16[2,192,2048]{2,1,0:T(8,128)(2,1)}, f32[2,192,2048]{2,1,0:T(8,128)}) fusion(f32[2,192,2048]{2,1,0:T(8,128)S(1)} %copy-done.33, f32[2,192,2048]{2,1,0:T(8,128)} %get-tuple-element.255, f32[2,192,2048]{2,1,0:T(8,128)} %get-tuple-element.254, f32[]{:T(128)} %bitcast.98), kind=kLoop, calls=%fused_computation.296 | loop fusion | flops 7077888 | bytes 14155780 | tf_op jit(solution)/shard_map/convert_element_type | solution.py:1131
  545.1 4.1 fusion.96
  549.3 7.5 %fusion.95 = (bf16[2048,768]{1,0:T(8,128)(2,1)}, f32[2048,768]{1,0:T(8,128)}) fusion(f32[2048,768]{1,0:T(8,128)} %param.29, f32[2048,768]{1,0:T(8,128)S(1)} %bitcast.267, f32[2048,768]{1,0:T(8,128)S(1)} %bitcast.269, f32[]{:T(128)} %bitcast.100), kind=kLoop, calls=%fused_computation.294 | loop fusion | flops 14155776 | bytes 28311556 | tf_op jit(solution)/shard_map/convert_element_type | solution.py:1131
  (602 shorter events, 246.0 us)
Async XLA Ops:
  7.2 116.3 %all-gather.6.cloned.1.call-start = ((), (), s32[]{:S(2)}) async-start(), calls=%async_computation.4 | async-start | bytes 3932160 | tf_op jit(solution)/shard_map/all_gather | solution.py:1045
  11.6 111.9 %all-gather.4.cloned.1.call-start = ((), (), s32[]{:S(2)}) async-start(), calls=%async_computation.3 | async-start | bytes 7864320 | tf_op jit(solution)/shard_map/all_gather | solution.py:1045
  14.9 188.3 %all-gather.8.cloned.1.call-start = ((), (), s32[]{:S(2)}) async-start(), calls=%async_computation.5 | async-start | bytes 15728640 | tf_op jit(solution)/shard_map/all_gather | solution.py:1045
  19.8 444.5 %reduce-scatter.2.cloned.1.call-start = ((), (), s32[]{:S(2)}) async-start(), calls=%async_computation.6 | async-start | bytes 15728640 | tf_op jit(solution)/shard_map/reduce_scatter | solution.py:1055
  30.2 23.0 %collective-permute-start.1 = (bf16[208,768]{1,0:T(8,128)(2,1)S(1)}, bf16[208,768]{1,0:T(8,128)(2,1)S(1)}, u32[]{:S(2)}, u32[]{:S(2)}) collective-permute-start(bf16[208,768]{1,0:T(8,128)(2,1)S(1)} %constant_dynamic-update-slice_fusion.refs_0_), channel_id=1, source_target_pairs={{0,4},{4,0},{8,12},{12,8},{16,20},{20,16},{24,28},{28,24},{1,5},{5... | collective-permute-start | bytes 958472 | tf_op jit(solution)/shard_map/ppermute | solution.py:64
  32.3 24.6 %collective-permute-start.2 = (bf16[208,768]{1,0:T(8,128)(2,1)S(1)}, bf16[208,768]{1,0:T(8,128)(2,1)S(1)}, u32[]{:S(2)}, u32[]{:S(2)}) collective-permute-start(bf16[208,768]{1,0:T(8,128)(2,1)S(1)} %constant_dynamic-update-slice_fusion.refs_0_), channel_id=1, source_target_pairs={{0,8},{4,12},{8,0},{12,4},{16,24},{20,28},{24,16},{28,20},{1,9},{5... | collective-permute-start | bytes 958472 | tf_op jit(solution)/shard_map/ppermute | solution.py:64
  33.9 24.3 %collective-permute-start.3 = (bf16[208,768]{1,0:T(8,128)(2,1)S(1)}, bf16[208,768]{1,0:T(8,128)(2,1)S(1)}, u32[]{:S(2)}, u32[]{:S(2)}) collective-permute-start(bf16[208,768]{1,0:T(8,128)(2,1)S(1)} %constant_dynamic-update-slice_fusion.refs_0_), channel_id=1, source_target_pairs={{0,12},{4,8},{8,4},{12,0},{16,28},{20,24},{24,20},{28,16},{1,13},{... | collective-permute-start | bytes 958472 | tf_op jit(solution)/shard_map/ppermute | solution.py:64
  36.8 21.4 %collective-permute-start.8 = (bf16[208,768]{1,0:T(8,128)(2,1)S(1)}, bf16[208,768]{1,0:T(8,128)(2,1)S(1)}, u32[]{:S(2)}, u32[]{:S(2)}) collective-permute-start(bf16[208,768]{1,0:T(8,128)(2,1)S(1)} %constant_dynamic-update-slice_fusion.refs_0_), channel_id=1, source_target_pairs={{0,1},{1,0},{2,3},{3,2},{4,5},{5,4},{6,7},{7,6},{8,9},{9,8},{10,11... | collective-permute-start | bytes 958472 | tf_op jit(solution)/shard_map/ppermute | solution.py:64
  94.9 23.7 %collective-permute-start.16 = (bf16[96,768]{1,0:T(8,128)(2,1)}, bf16[96,768]{1,0:T(8,128)(2,1)}, u32[]{:S(2)}, u32[]{:S(2)}) collective-permute-start(bf16[96,768]{1,0:T(8,128)(2,1)} %get-tuple-element.340), channel_id=1, source_target_pairs={{0,4},{4,0},{8,12},{12,8},{16,20},{20,16},{24,28},{28,24},{1,5},{5... | collective-permute-start | bytes 442376 | tf_op jit(solution)/shard_map/ppermute | solution.py:64
  95.2 26.0 %collective-permute-start.17 = (bf16[96,768]{1,0:T(8,128)(2,1)}, bf16[96,768]{1,0:T(8,128)(2,1)}, u32[]{:S(2)}, u32[]{:S(2)}) collective-permute-start(bf16[96,768]{1,0:T(8,128)(2,1)} %get-tuple-element.339), channel_id=1, source_target_pairs={{0,8},{4,12},{8,0},{12,4},{16,24},{20,28},{24,16},{28,20},{1,9},{5... | collective-permute-start | bytes 442376 | tf_op jit(solution)/shard_map/ppermute | solution.py:64
  97.0 26.5 %collective-permute-start.18 = (bf16[96,768]{1,0:T(8,128)(2,1)}, bf16[96,768]{1,0:T(8,128)(2,1)}, u32[]{:S(2)}, u32[]{:S(2)}) collective-permute-start(bf16[96,768]{1,0:T(8,128)(2,1)} %get-tuple-element.338), channel_id=1, source_target_pairs={{0,12},{4,8},{8,4},{12,0},{16,28},{20,24},{24,20},{28,16},{1,13},{... | collective-permute-start | bytes 442376 | tf_op jit(solution)/shard_map/ppermute | solution.py:64
  98.4 36.8 %collective-permute-start.22 = (bf16[96,768]{1,0:T(8,128)(2,1)}, bf16[96,768]{1,0:T(8,128)(2,1)}, u32[]{:S(2)}, u32[]{:S(2)}) collective-permute-start(bf16[96,768]{1,0:T(8,128)(2,1)} %get-tuple-element.337), channel_id=1, source_target_pairs={{0,16},{4,20},{8,24},{12,28},{16,0},{20,4},{24,8},{28,12},{1,17},{... | collective-permute-start | bytes 442376 | tf_op jit(solution)/shard_map/ppermute | solution.py:64
  99.6 35.6 %collective-permute-start.23 = (bf16[96,768]{1,0:T(8,128)(2,1)}, bf16[96,768]{1,0:T(8,128)(2,1)}, u32[]{:S(2)}, u32[]{:S(2)}) collective-permute-start(bf16[96,768]{1,0:T(8,128)(2,1)} %get-tuple-element.336), channel_id=1, source_target_pairs={{0,20},{4,16},{8,28},{12,24},{16,4},{20,0},{24,12},{28,8},{1,21},{... | collective-permute-start | bytes 442376 | tf_op jit(solution)/shard_map/ppermute | solution.py:64
  173.4 21.4 %collective-permute-start.30 = (bf16[128,768]{1,0:T(8,128)(2,1)S(1)}, bf16[128,768]{1,0:T(8,128)(2,1)S(1)}, u32[]{:S(2)}, u32[]{:S(2)}) collective-permute-start(bf16[128,768]{1,0:T(8,128)(2,1)S(1)} %get-tuple-element.378), channel_id=1, source_target_pairs={{0,4},{4,0},{8,12},{12,8},{16,20},{20,16},{24,28},{28,24},{1,5},{5... | collective-permute-start | bytes 589832 | tf_op jit(solution)/shard_map/ppermute | solution.py:64
  273.0 29.5 %collective-permute-start.39 = (bf16[128,768]{1,0:T(8,128)(2,1)}, bf16[128,768]{1,0:T(8,128)(2,1)}, u32[]{:S(2)}, u32[]{:S(2)}) collective-permute-start(bf16[128,768]{1,0:T(8,128)(2,1)} %get-tuple-element.324), channel_id=1, source_target_pairs={{0,12},{4,8},{8,4},{12,0},{16,28},{20,24},{24,20},{28,16},{1,13},{... | collective-permute-start | bytes 589832 | tf_op jit(solution)/shard_map/ppermute | solution.py:64
  273.9 28.6 %collective-permute-start.38 = (bf16[128,768]{1,0:T(8,128)(2,1)}, bf16[128,768]{1,0:T(8,128)(2,1)}, u32[]{:S(2)}, u32[]{:S(2)}) collective-permute-start(bf16[128,768]{1,0:T(8,128)(2,1)} %get-tuple-element.325), channel_id=1, source_target_pairs={{0,8},{4,12},{8,0},{12,4},{16,24},{20,28},{24,16},{28,20},{1,9},{5... | collective-permute-start | bytes 589832 | tf_op jit(solution)/shard_map/ppermute | solution.py:64
  278.4 24.2 %collective-permute-start.37 = (bf16[128,768]{1,0:T(8,128)(2,1)}, bf16[128,768]{1,0:T(8,128)(2,1)}, u32[]{:S(2)}, u32[]{:S(2)}) collective-permute-start(bf16[128,768]{1,0:T(8,128)(2,1)} %get-tuple-element.320), channel_id=1, source_target_pairs={{0,4},{4,0},{8,12},{12,8},{16,20},{20,16},{24,28},{28,24},{1,5},{5... | collective-permute-start | bytes 589832 | tf_op jit(solution)/shard_map/ppermute | solution.py:64
  320.7 21.1 %collective-permute-start.46 = (bf16[96,768]{1,0:T(8,128)(2,1)}, bf16[96,768]{1,0:T(8,128)(2,1)}, u32[]{:S(2)}, u32[]{:S(2)}) collective-permute-start(bf16[96,768]{1,0:T(8,128)(2,1)} %get-tuple-element.330), channel_id=1, source_target_pairs={{0,12},{4,8},{8,4},{12,0},{16,28},{20,24},{24,20},{28,16},{1,13},{... | collective-permute-start | bytes 442376 | tf_op jit(solution)/shard_map/ppermute | solution.py:64
  322.2 32.4 %collective-permute-start.50 = (bf16[96,768]{1,0:T(8,128)(2,1)}, bf16[96,768]{1,0:T(8,128)(2,1)}, u32[]{:S(2)}, u32[]{:S(2)}) collective-permute-start(bf16[96,768]{1,0:T(8,128)(2,1)} %get-tuple-element.329), channel_id=1, source_target_pairs={{0,16},{4,20},{8,24},{12,28},{16,0},{20,4},{24,8},{28,12},{1,17},{... | collective-permute-start | bytes 442376 | tf_op jit(solution)/shard_map/ppermute | solution.py:64
  324.8 29.9 %collective-permute-start.51 = (bf16[96,768]{1,0:T(8,128)(2,1)}, bf16[96,768]{1,0:T(8,128)(2,1)}, u32[]{:S(2)}, u32[]{:S(2)}) collective-permute-start(bf16[96,768]{1,0:T(8,128)(2,1)} %get-tuple-element.328), channel_id=1, source_target_pairs={{0,20},{4,16},{8,28},{12,24},{16,4},{20,0},{24,12},{28,8},{1,21},{... | collective-permute-start | bytes 442376 | tf_op jit(solution)/shard_map/ppermute | solution.py:64
  354.7 21.9 %collective-permute-start.49 = (bf16[96,768]{1,0:T(8,128)(2,1)S(1)}, bf16[96,768]{1,0:T(8,128)(2,1)S(1)}, u32[]{:S(2)}, u32[]{:S(2)}) collective-permute-start(bf16[96,768]{1,0:T(8,128)(2,1)S(1)} %get-tuple-element.126), channel_id=1, source_target_pairs={{0,12},{4,8},{8,4},{12,0},{16,28},{20,24},{24,20},{28,16},{1,13},{... | collective-permute-start | bytes 442376 | tf_op jit(solution)/shard_map/ppermute | solution.py:64
  389.0 21.1 %collective-permute-start.58 = (bf16[2,512,768]{2,1,0:T(8,128)(2,1)S(1)}, bf16[2,512,768]{2,1,0:T(8,128)(2,1)S(1)}, u32[]{:S(2)}, u32[]{:S(2)}) collective-permute-start(bf16[2,512,768]{2,1,0:T(8,128)(2,1)S(1)} %grads_out.2), channel_id=1, source_target_pairs={{0,1},{1,0},{2,3},{3,2},{4,5},{5,4},{6,7},{7,6},{8,9},{9,8},{10,11... | collective-permute-start | bytes 4718600 | tf_op jit(solution)/shard_map/ppermute | solution.py:64
  424.9 21.8 %collective-permute-start.59 = (bf16[8,2,104,768]{3,2,1,0:T(8,128)(2,1)}, bf16[8,2,104,768]{3,2,1,0:T(8,128)(2,1)}, u32[]{:S(2)}, u32[]{:S(2)}) collective-permute-start(bf16[8,2,104,768]{3,2,1,0:T(8,128)(2,1)} %get-tuple-element.148), channel_id=1, source_target_pairs={{0,1},{1,0},{2,3},{3,2},{4,5},{5,4},{6,7},{7,6},{8,9},{9,8},{10,11... | collective-permute-start | bytes 7667720 | tf_op jit(solution)/shard_map/ppermute | solution.py:64
  437.8 23.3 %collective-permute-start.68 = (bf16[2,2,192,2048]{3,2,1,0:T(8,128)(2,1)}, bf16[2,2,192,2048]{3,2,1,0:T(8,128)(2,1)}, u32[]{:S(2)}, u32[]{:S(2)}) collective-permute-start(bf16[2,2,192,2048]{3,2,1,0:T(8,128)(2,1)} %get-tuple-element.162), channel_id=1, source_target_pairs={{0,1},{1,0},{2,3},{3,2},{4,5},{5,4},{6,7},{7,6},{8,9},{9,8},{10,11... | collective-permute-start | bytes 9437192 | tf_op jit(solution)/shard_map/ppermute | solution.py:64
  440.3 36.7 %collective-permute-start.66 = (bf16[512,768]{1,0:T(8,128)(2,1)}, bf16[512,768]{1,0:T(8,128)(2,1)}, u32[]{:S(2)}, u32[]{:S(2)}) collective-permute-start(bf16[512,768]{1,0:T(8,128)(2,1)} %fusion.23), channel_id=1, source_target_pairs={{0,2},{1,3},{2,0},{3,1},{4,6},{5,7},{6,4},{7,5},{8,10},{9,11},{10,... | collective-permute-start | bytes 2359304 | tf_op jit(solution)/shard_map/ppermute | solution.py:64
  454.3 24.9 %collective-permute-start.63 = (bf16[2,104,768]{2,1,0:T(8,128)(2,1)}, bf16[2,104,768]{2,1,0:T(8,128)(2,1)}, u32[]{:S(2)}, u32[]{:S(2)}) collective-permute-start(bf16[2,104,768]{2,1,0:T(8,128)(2,1)} %get-tuple-element.315), channel_id=1, source_target_pairs={{0,4},{4,0},{8,12},{12,8},{16,20},{20,16},{24,28},{28,24},{1,5},{5... | collective-permute-start | bytes 958472 | tf_op jit(solution)/shard_map/ppermute | solution.py:64
  454.8 24.3 %collective-permute-start.64 = (bf16[2,104,768]{2,1,0:T(8,128)(2,1)}, bf16[2,104,768]{2,1,0:T(8,128)(2,1)}, u32[]{:S(2)}, u32[]{:S(2)}) collective-permute-start(bf16[2,104,768]{2,1,0:T(8,128)(2,1)} %get-tuple-element.314), channel_id=1, source_target_pairs={{0,8},{4,12},{8,0},{12,4},{16,24},{20,28},{24,16},{28,20},{1,9},{5... | collective-permute-start | bytes 958472 | tf_op jit(solution)/shard_map/ppermute | solution.py:64
  464.3 20.8 %collective-permute-start.69 = (bf16[192,2048]{1,0:T(8,128)(2,1)}, bf16[192,2048]{1,0:T(8,128)(2,1)}, u32[]{:S(2)}, u32[]{:S(2)}) collective-permute-start(bf16[192,2048]{1,0:T(8,128)(2,1)} %get-tuple-element.311), channel_id=1, source_target_pairs={{0,2},{1,3},{2,0},{3,1},{4,6},{5,7},{6,4},{7,5},{8,10},{9,11},{10,... | collective-permute-start | bytes 2359304 | tf_op jit(solution)/shard_map/ppermute | solution.py:64
  477.0 25.1 %collective-permute-start.62 = (bf16[2,104,768]{2,1,0:T(8,128)(2,1)}, bf16[2,104,768]{2,1,0:T(8,128)(2,1)S(1)}, u32[]{:S(2)}, u32[]{:S(2)}) collective-permute-start(bf16[2,104,768]{2,1,0:T(8,128)(2,1)} %get-tuple-element.316), channel_id=1, source_target_pairs={{0,12},{4,8},{8,4},{12,0},{16,28},{20,24},{24,20},{28,16},{1,13},{... | collective-permute-start | bytes 958472 | tf_op jit(solution)/shard_map/ppermute | solution.py:64
  479.2 23.0 %collective-permute-start.61 = (bf16[2,104,768]{2,1,0:T(8,128)(2,1)}, bf16[2,104,768]{2,1,0:T(8,128)(2,1)S(1)}, u32[]{:S(2)}, u32[]{:S(2)}) collective-permute-start(bf16[2,104,768]{2,1,0:T(8,128)(2,1)} %get-tuple-element.317), channel_id=1, source_target_pairs={{0,8},{4,12},{8,0},{12,4},{16,24},{20,28},{24,16},{28,20},{1,9},{5... | collective-permute-start | bytes 958472 | tf_op jit(solution)/shard_map/ppermute | solution.py:64
  479.2 23.0 %collective-permute-start.60 = (bf16[2,104,768]{2,1,0:T(8,128)(2,1)}, bf16[2,104,768]{2,1,0:T(8,128)(2,1)S(1)}, u32[]{:S(2)}, u32[]{:S(2)}) collective-permute-start(bf16[2,104,768]{2,1,0:T(8,128)(2,1)} %get-tuple-element.312), channel_id=1, source_target_pairs={{0,4},{4,0},{8,12},{12,8},{16,20},{20,16},{24,28},{28,24},{1,5},{5... | collective-permute-start | bytes 958472 | tf_op jit(solution)/shard_map/ppermute | solution.py:64
  480.6 24.5 %collective-permute-start.71 = (bf16[192,2048]{1,0:T(8,128)(2,1)S(1)}, bf16[192,2048]{1,0:T(8,128)(2,1)S(1)}, u32[]{:S(2)}, u32[]{:S(2)}) collective-permute-start(bf16[192,2048]{1,0:T(8,128)(2,1)S(1)} %copy-done.55), channel_id=1, source_target_pairs={{0,2},{1,3},{2,0},{3,1},{4,6},{5,7},{6,4},{7,5},{8,10},{9,11},{10,... | collective-permute-start | bytes 2359304 | tf_op jit(solution)/shard_map/ppermute | solution.py:64
  (177 other events, 1675.8 us)
Sparse Core Ops, SparseCore 0:
  11.7 33.6 all-gather.5
  47.5 47.3 all-gather.3
  97.1 82.1 all-gather.7
  304.9 100.9 reduce-scatter.1

commit v4 on v3

--- a/solution.py
+++ b/solution.py
@@ -23,12 +23,13 @@
 LANES = 128
 MOST_FLIPS = 8
 ROWS = 256
+BAND = 256
 VMEM_BYTES = 48 << 20
 
 
-def params(name, products=0, moved=0, exps=0):
+def params(name, products=0, moved=0, exps=0, room=None):
     return dict(
-        compiler_params=pltpu.CompilerParams(vmem_limit_bytes=VMEM_BYTES),
+        compiler_params=pltpu.CompilerParams(vmem_limit_bytes=room or VMEM_BYTES),
         cost_estimate=pl.CostEstimate(
             flops=2 * products, bytes_accessed=moved, transcendentals=exps
         ),
@@ -98,13 +99,12 @@
     half = n_dp // 2
     if n_dp > MOST_FLIPS:
         pieces = by_distance(jnp.stack(parts).astype(LOWER), lax.axis_index("dp"))
-        return jnp.sum(swap(pieces, "dp").astype(WIDE), 0)
+        return [jnp.sum(swap(pieces, "dp").astype(WIDE), 0)]
     aims = [flip(parts[half + m].astype(LOWER), "dp", m, n_dp) for m in range(1, half)]
     across = sum([a.astype(WIDE) for a in aims], parts[half].astype(WIDE)).astype(LOWER)
     cross = flip(across, "dp", half, n_dp)
     near = [flip(parts[m].astype(LOWER), "dp", m, n_dp) for m in range(1, half)]
-    total = sum([a.astype(WIDE) for a in near], parts[0].astype(WIDE))
-    return total + cross.astype(WIDE)
+    return [parts[0]] + near + [cross]
 
 
 def halve(buffer, axis, mask, size):
@@ -209,7 +209,7 @@
             pltpu.SemaphoreType.DMA((4 * n_dp,)),
             pltpu.SemaphoreType.DMA((4 * n_dp,)),
         ],
-        **params("assemble", 0, 32 * n_dp * width * D),
+        **params("assemble", 0, 32 * n_dp * width * D, room=48 << 20),
     )(place, *pieces)
 
 
@@ -272,17 +272,14 @@
             out_specs=[out_spec, out_spec],
             scratch_shapes=[pltpu.VMEM((wide, D), WIDE)],
         ),
-        out_shape=[
-            jax.ShapeDtypeStruct((n_dp,) + block[1:], WIDE),
-            jax.ShapeDtypeStruct((n_dp,) + block[1:], LOWER),
-        ],
+        out_shape=[jax.ShapeDtypeStruct((n_dp,) + block[1:], LOWER)] * 2,
         **params("dense_grads", tokens * 4 * D * D, 12 * tokens * D + 24 * D * D),
     )(place, grad_qkv, grad_attn, normed, mixed, small_turned)
 
 
 def sum_weights(mine, other, n_dp, jobs):
-    both = mine + flip(other, "rep", 1, 4).astype(WIDE)
-    parts = [both[m] for m in range(n_dp)]
+    both = flip(other, "rep", 1, 4)
+    parts = [mine[m].astype(WIDE) + both[m].astype(WIDE) for m in range(n_dp)]
     done = []
 
     def beside(value, job):
@@ -291,12 +288,12 @@
         return value
 
     if n_dp > MOST_FLIPS:
-        pair = beside(beside(sum_flips(parts, n_dp), jobs[0]), jobs[1])
+        pair = beside(beside(add_up(sum_flips(parts, n_dp)), jobs[0]), jobs[1])
     else:
         half = n_dp // 2
         aims = [flip(parts[half + m].astype(LOWER), "dp", m, n_dp) for m in range(1, half)]
         near = [flip(parts[m].astype(LOWER), "dp", m, n_dp) for m in range(1, half)]
-        aims = beside(aims, jobs[0])
+        aims, near = beside((aims, near), jobs[0])
         cross = flip(add_up([parts[half]] + aims).astype(LOWER), "dp", half, n_dp)
         cross = beside(cross, jobs[1])
         pair = add_up([parts[0]] + near + [cross])
@@ -345,20 +342,20 @@
         bias_ref[...] = jnp.where(counts, 0.0, -1e30)
 
     masks = lane_masks()
-    for start in range(0, tokens, ROWS):
-        keys = start + ROWS
+    for start in range(0, tokens, BAND):
+        keys = start + BAND
         k = k_ref[:keys, :]
         v = v_ref[:keys, :]
-        q = q_ref[start : start + ROWS, :]
-        acc = jnp.zeros((ROWS, 2 * HDIM), WIDE)
+        q = q_ref[start : start + BAND, :]
+        acc = jnp.zeros((BAND, 2 * HDIM), WIDE)
         for mine in masks:
             scores = contract_cols(q * mine, k) * HDIM ** (-0.5)
-            scores = scores + bias_ref[start : start + ROWS, :keys]
+            scores = scores + bias_ref[start : start + BAND, :keys]
             expo = jnp.exp(scores - jnp.max(scores, -1, keepdims=True))
             total = jnp.sum(expo, -1, keepdims=True)
             probs = (expo * (1.0 / total)).astype(LOWER)
             acc = acc + plain(probs, v * mine)
-        out_ref[start : start + ROWS, :] = acc.astype(LOWER)
+        out_ref[start : start + BAND, :] = acc.astype(LOWER)
 
 
 def head_specs(tokens, first):
@@ -396,20 +393,20 @@
 
     masks = lane_masks()
     scale = HDIM ** (-0.5)
-    grad_k = [jnp.zeros((ROWS, 2 * HDIM), WIDE) for _ in range(tokens // ROWS)]
-    grad_v = [jnp.zeros((ROWS, 2 * HDIM), WIDE) for _ in range(tokens // ROWS)]
+    grad_k = [jnp.zeros((BAND, 2 * HDIM), WIDE) for _ in range(tokens // BAND)]
+    grad_v = [jnp.zeros((BAND, 2 * HDIM), WIDE) for _ in range(tokens // BAND)]
     col = pl.multiple_of(step * 2 * HDIM, 2 * HDIM)
-    for block, start in enumerate(range(0, tokens, ROWS)):
-        keys = start + ROWS
+    for block, start in enumerate(range(0, tokens, BAND)):
+        keys = start + BAND
         k = k_ref[:keys, :]
         v = v_ref[:keys, :]
-        q = q_ref[start : start + ROWS, :]
-        do = do_ref[start : start + ROWS, :]
-        grad_q = jnp.zeros((ROWS, 2 * HDIM), WIDE)
+        q = q_ref[start : start + BAND, :]
+        do = do_ref[start : start + BAND, :]
+        grad_q = jnp.zeros((BAND, 2 * HDIM), WIDE)
         for mine in masks:
             q_own = q * mine
             do_own = do * mine
-            scores = contract_cols(k, q_own) * scale + bias_ref[:keys, start : start + ROWS]
+            scores = contract_cols(k, q_own) * scale + bias_ref[:keys, start : start + BAND]
             expo = jnp.exp(scores - jnp.max(scores, 0, keepdims=True))
             total = jnp.sum(expo, 0, keepdims=True)
             probs = expo * (1.0 / total)
@@ -420,11 +417,11 @@
             into_v = plain(probs.astype(LOWER), do_own)
             into_k = plain(grad_s, q_own)
             for b in range(block + 1):
-                grad_v[b] = grad_v[b] + into_v[b * ROWS : (b + 1) * ROWS]
-                grad_k[b] = grad_k[b] + into_k[b * ROWS : (b + 1) * ROWS]
-        out_ref[start : start + ROWS, pl.ds(col, 2 * HDIM)] = (grad_q * scale).astype(LOWER)
-    for b in range(tokens // ROWS):
-        rows = slice(b * ROWS, (b + 1) * ROWS)
+                grad_v[b] = grad_v[b] + into_v[b * BAND : (b + 1) * BAND]
+                grad_k[b] = grad_k[b] + into_k[b * BAND : (b + 1) * BAND]
+        out_ref[start : start + BAND, pl.ds(col, 2 * HDIM)] = (grad_q * scale).astype(LOWER)
+    for b in range(tokens // BAND):
+        rows = slice(b * BAND, (b + 1) * BAND)
         out_ref[rows, pl.ds(D + col, 2 * HDIM)] = (grad_k[b] * scale).astype(LOWER)
         out_ref[rows, pl.ds(2 * D + col, 2 * HDIM)] = grad_v[b].astype(LOWER)
 
@@ -564,14 +561,18 @@
 
 
 def grads_in_body(
-    place_ref, rows_a, rows_b, back_a, back_b, keep_ref, give_ref, sum_ref, turned_a, turned_b
+    place_ref, rows_a, rows_b, back_a, back_b, keep_ref, give_ref, sum_ref, turned_ref, back_ref
 ):
+    rows = rows_a.shape[0]
+
     @pl.when((pl.program_id(0) == 0) & (pl.program_id(1) == 0))
     def _():
-        turned_a[...] = rows_a[...].T
-        turned_b[...] = rows_b[...].T
-
-    sum_ref[...] = plain(turned_a[...], back_a[0]) + plain(turned_b[...], back_b[0])
+        turned_ref[:, :rows] = rows_a[...].T
+        turned_ref[:, rows:] = rows_b[...].T
+
+    back_ref[:rows, :] = back_a[0]
+    back_ref[rows:, :] = back_b[0]
+    sum_ref[...] = plain(turned_ref[...], back_ref[...])
     size = keep_ref.shape[2]
     for pair in range(2):
         for core, out_ref in enumerate((keep_ref, give_ref)):
@@ -592,7 +593,11 @@
             grid=(2, hidden // tile),
             in_specs=[full((rows, D)), full((rows, D)), back, back],
             out_specs=[out, out],
-            scratch_shapes=[pltpu.VMEM((D, tile), WIDE)] + [pltpu.VMEM((D, rows), LOWER)] * 2,
+            scratch_shapes=[
+                pltpu.VMEM((D, tile), WIDE),
+                pltpu.VMEM((D, 2 * rows), LOWER),
+                pltpu.VMEM((2 * rows, tile), LOWER),
+            ],
         ),
         out_shape=[jax.ShapeDtypeStruct((2, 2, size, hidden), LOWER)] * 2,
         **params("grads_in", 4 * rows * hidden * D, 4 * hidden * D + 8 * rows * hidden),
@@ -627,7 +632,9 @@
             jnp.concatenate([near[2], far[2]]), jnp.concatenate([near_back[1], far_back[1]])
         ).astype(LOWER)
         return [lax.psum_scatter(grad, "rep", scatter_dimension=0, tiled=True)], came_back
-    came_back, rows = lax.optimization_barrier((came_back, (near_back[1], far_back[1])))
+    half = len(came_back) // 2
+    arrived, rows = lax.optimization_barrier((came_back[:half], (near_back[1], far_back[1])))
+    came_back = arrived + came_back[half:]
     ends = (near[2], far[2]) + rows
     give, keep = grads_out(place, 1, *ends), grads_out(place, 0, *ends)
     came_back, give, keep = lax.optimization_barrier((came_back, give, keep))
@@ -635,17 +642,19 @@
     return [keep[0], take[0], (keep[1].astype(WIDE) + take[1].astype(WIDE)).astype(LOWER)], came_back
 
 
-def sum_experts_in(place, near, far, near_back, far_back, after):
+def sum_experts_in(place, near, far, near_back, far_back, after, eout_g):
     if lax.axis_size("rep") != 4:
         rows = jnp.concatenate([near[3], far[3]])
         backs = jnp.concatenate([near_back[0], far_back[0]], 1)
         grad = jnp.stack([contract_rows(rows, back).astype(LOWER) for back in backs])
-        return [lax.psum_scatter(grad, "rep", scatter_dimension=1, tiled=True)], after
+        return [lax.psum_scatter(grad, "rep", scatter_dimension=1, tiled=True)], after, eout_g
     after, backs = lax.optimization_barrier((after, (near_back[0], far_back[0])))
     keep, give = grads_in(place, near[3], far[3], *backs)
+    crossed = flip(eout_g[2], "rep", 2, 4)
+    give, crossed = lax.optimization_barrier((give, crossed))
     take = flip(give, "rep", 1, 4)
     far = [(keep[k, 1].astype(WIDE) + take[k, 1].astype(WIDE)).astype(LOWER) for k in range(2)]
-    return [keep[:, 0], take[:, 0], far], after
+    return [keep[:, 0], take[:, 0], far], after, eout_g[:2] + [crossed]
 
 
 def add_up(parts):
@@ -659,7 +668,7 @@
 
 def send_slots(buffer, n_dp, shards):
     half = n_dp // 2
-    blocks = trade([b for b in cut(buffer, EXPERTS) for _ in range(shards)], n_dp)
+    blocks = trade([b for b in buffer for _ in range(shards)], n_dp)
     return blocks[:half], blocks[half:]
 
 
@@ -705,7 +714,7 @@
     picks = [(slot[:, k : k + 1] == all_slots[None]).astype(LOWER) for k in range(2)]
     both = picks[0] + picks[1]
     buffer = contract_rows(both, second_low).astype(LOWER)
-    sent = send_slots(buffer, n_dp, shards)
+    sent = send_slots(cut(buffer, EXPERTS), n_dp, shards)
     near, far = (experts_forward(rows, w_in, w_out) for rows in sent)
     returned = return_slots(near[4], far[4], n_dp, shards)
     outs = [pick_slots(picks[k], returned) for k in range(2)]
@@ -738,6 +747,7 @@
         used=used,
         weight=weight,
         w_slot=w_slot,
+        slot=slot,
         picks=picks,
         both=both,
         near=near,
@@ -874,7 +884,7 @@
 
 
 def head_step(third, positions, targets, table_all, gain, own, n_dp):
-    final, scale_three = norm_fwd(third, gain)
+    final, unused = norm_fwd(third, gain)
     tokens = third.shape[0]
     count = positions.shape[0]
     pick = positions[:, None] == jnp.arange(tokens, dtype=jnp.int32)[None, :]
@@ -897,12 +907,54 @@
     grad_chosen = sum_flips(cut(grad_rows, n_dp), n_dp)
     grad_table = vocab_grad_table(grad_logits, gathered)
     grad_chosen, grad_table = lax.optimization_barrier((grad_chosen, grad_table))
-    grad_final = rows_high(pick.astype(WIDE), grad_chosen)
-    grad_third, grad_gain = norm_back(third, scale_three, gain, grad_final)
-    return (loss_part, grad_third, grad_gain, grad_table)
-
-
-def layer_backward(hidden, grad_third, saved, w_qkv, w_attn, w_in, w_out, n_dp, place):
+    return (loss_part, grad_chosen, grad_table)
+
+
+def head_back_body(*refs, count):
+    terms, refs = refs[:count], refs[count:]
+    spot_ref, slot_ref, third_ref, gain_ref, w_ref, grad_ref, gain_grad_ref, *blocks = refs
+    tokens = third_ref.shape[0]
+    total = terms[0][...].astype(WIDE)
+    for term in terms[1:]:
+        total = total + term[...].astype(WIDE)
+    spots = spot_ref[...] == lax.broadcasted_iota(jnp.int32, (tokens, total.shape[0]), 0)
+    spots = spots.astype(WIDE).astype(LOWER)
+    grad = jnp.zeros(third_ref.shape, WIDE)
+    for _ in range(3):
+        piece = total.astype(LOWER)
+        total = total - piece.astype(WIDE)
+        grad = grad + plain(spots, piece)
+    third = third_ref[...]
+    scale = lax.rsqrt(jnp.mean(third * third, -1, keepdims=True) + EPS)
+    normed = third * scale
+    gain_grad_ref[...] = jnp.sum(grad * normed, 0, keepdims=True)
+    inner = grad * gain_ref[...]
+    grad = scale * (inner - normed * jnp.mean(inner * normed, -1, keepdims=True))
+    grad_ref[...] = grad
+    out = jnp.zeros((EXPERTS * CAP, D), WIDE)
+    places = lax.broadcasted_iota(jnp.int32, (EXPERTS * CAP, tokens), 0)
+    for k in range(2):
+        picks = (slot_ref[k : k + 1, :] == places).astype(WIDE).astype(LOWER)
+        out = out + plain(picks, (w_ref[:, k : k + 1] * grad).astype(LOWER))
+    for e, block in enumerate(blocks):
+        block[...] = out[e * CAP : (e + 1) * CAP, :].astype(LOWER)
+
+
+def head_back(terms, positions, slot, third, gain, w_slot):
+    tokens = third.shape[0]
+    grad_third, grad_gain, *blocks = pl.pallas_call(
+        functools.partial(head_back_body, count=len(terms)),
+        out_shape=[
+            jax.ShapeDtypeStruct((tokens, D), WIDE),
+            jax.ShapeDtypeStruct((1, D), WIDE),
+        ]
+        + [jax.ShapeDtypeStruct((CAP, D), LOWER)] * EXPERTS,
+        **params("head_back", 2 * tokens * EXPERTS * CAP * D, 12 * tokens * D),
+    )(*terms, positions[None, :], slot.T, third, gain[None, :], w_slot)
+    return grad_third, grad_gain[0], blocks
+
+
+def layer_backward(hidden, grad_third, saved, w_qkv, w_attn, w_in, w_out, n_dp, place, blocks):
     shards = n_dp // EXPERTS
     gains, const_vec = saved["gains"], saved["const_vec"]
     router, const_gate = saved["router"], saved["const_gate"]
@@ -910,16 +962,14 @@
     weight = saved["weight"]
     route_p = saved["route_p"]
     second_wide = saved["second_low"].astype(WIDE)
-    w_slot, picks = saved["w_slot"], saved["picks"]
-    grad_out = contract_rows(picks[0], (w_slot[:, 0:1] * grad_third).astype(LOWER))
-    grad_out = grad_out + contract_rows(picks[1], (w_slot[:, 1:2] * grad_third).astype(LOWER))
-    sent = send_slots(grad_out.astype(LOWER), n_dp, shards)
+    sent = send_slots(blocks, n_dp, shards)
     near, far = saved["near"], saved["far"]
     near_back = experts_backward(sent[0], near[0], near[1], w_in, w_out)
     far_back = experts_backward(sent[1], far[0], far[1], w_in, w_out)
-    came_back = return_slots(near_back[2], far_back[2], n_dp, shards)
+    blocks = trade(list(near_back[2]) + list(far_back[2]), n_dp)
     ends = (place, near, far, near_back, far_back)
-    eout_g, came_back = sum_experts_out(*ends, came_back)
+    eout_g, blocks = sum_experts_out(*ends, blocks)
+    came_back = [jnp.concatenate(blocks[s::shards]) for s in range(shards)]
     dots = [jnp.sum(saved["outs"][k] * grad_third, -1, keepdims=True) for k in range(2)]
     hits = saved["hits"].astype(WIDE)
     grad_real = (dots[0] * hits[:, 0] + dots[1] * hits[:, 1])[:, :EXPERTS]
@@ -1049,12 +1099,15 @@
     third, saved = layer_forward(
         hidden, seq_lens[0], routes, w_qkv, w_attn, small_all, w_in, w_out, own, n_dp
     )
-    loss_part, grad_third, grad_gain_final, grad_table = head_step(
+    loss_part, terms, grad_table = head_step(
         third, positions, targets[0], table_all, saved["gains"][2], own, n_dp
+    )
+    grad_third, grad_gain_final, blocks = head_back(
+        terms, positions, saved["slot"], third, saved["gains"][2], saved["w_slot"]
     )
     table_g = lax.psum_scatter(grad_table, "rep", scatter_dimension=0, tiled=True)
     left, gain_one, gain_two, grad_cvec, grad_gates, ends, eout_g = layer_backward(
-        hidden, grad_third, saved, w_qkv, w_attn, w_in, w_out, n_dp, place
+        hidden, grad_third, saved, w_qkv, w_attn, w_in, w_out, n_dp, place, blocks
     )
     small_grad = jnp.concatenate(
         [gain_one[None], gain_two[None], grad_gain_final[None], grad_cvec, grad_gates], 0
@@ -1065,18 +1118,17 @@
         return flip(value, "rep", 2, 4) if n_rep == 4 else value
 
     def table_job(done):
-        return shared_update(table, table_m, table_v, [table_g]), crossed(eout_g[-1])
+        made = shared_update(table, table_m, table_v, [table_g])
+        return made, (crossed(ein_g[2][0]) if n_rep == 4 else None)
 
     def out_job(done):
-        made = shared_update(expert_out, expout_m, expout_v, eout_g[:-1] + [done[0][1]])
-        if n_rep != 4:
-            return made, None
-        return made, crossed(ein_g[2][0])
+        made = shared_update(expert_out, expout_m, expout_v, eout_g)
+        return made, (crossed(ein_g[2][1]) if n_rep == 4 else None)
 
     def in_job(done):
         parts = ein_g
         if n_rep == 4:
-            parts = ein_g[:2] + [jnp.stack([done[1][1], crossed(ein_g[2][1])])]
+            parts = ein_g[:2] + [jnp.stack([done[0][1], done[1][1]])]
         return shared_update(expert_in, expin_m, expin_v, parts), None
 
     jobs = (table_job, out_job, in_job)
@@ -1084,7 +1136,7 @@
     if flips:
         turned = jnp.pad(small_grad, ((0, LANES - small_grad.shape[0]), (0, 0))).T
         mine, other = dense_grads(place, *left, normed, mixed, turned, n_dp, width)
-        ein_g, other = sum_experts_in(*ends, other)
+        ein_g, other, eout_g = sum_experts_in(*ends, other, eout_g)
         block, done = sum_weights(mine, other, n_dp, jobs)
         small_g = block[width:].reshape(8, -1, LANES)[:, : thin // 8].swapaxes(0, 1)
         small_g = small_g.reshape(thin, LANES)[:, : small_w.shape[0]].T
@@ -1100,7 +1152,7 @@
         )
         block = scatter_sum(blocks.reshape((n_dp, n_rep) + blocks.shape[1:]), n_dp, n_rep)
         small_g = block[width:].reshape(-1)[: small_w.size].reshape(small_w.shape)
-        ein_g, block = sum_experts_in(*ends, block)
+        ein_g, block, eout_g = sum_experts_in(*ends, block, eout_g)
         done = []
         for job in jobs:
             done.append(job(done))

time: 569 us -> 537 us (0.944)
  other arithmetic: 107 us -> 88.1 us
  matrix products: 29.9 us -> 19.3 us
    ppermute x72, starting transfers between devices: 107 us -> 101 us  [flip(): return lax.ppermute(value, axis, [(i, i ^ mask) for i in range(size)])]
    another operation x2 -> x1, other arithmetic: 6.29 us -> 0.01 us
    unnamed x293 -> x299, local copies, waits for them, and re-layouts: 21 us -> 25.4 us
  transfers between devices with their start and end apart: 77 -> 77, of which waited for: 22 -> 27; matrix products, arithmetic and copies ran while one was open for 21% -> 17% of each run, Pallas kernels for 19% -> 21%
where the time goes in v4:
time: 537 us; the launch traced here: 533 us
  Pallas kernels  159 us (30%)
  starting transfers between devices  106 us (20%)
  waiting for transfers between devices  92.8 us (17%)
  other arithmetic  88.1 us (16%)
  local copies, waits for them, and re-layouts  37.7 us (7%)
  matrix products  19.3 us (4%)
  between operations  18.7 us (3%)
  blocking collectives  11.3 us (2%)
    ppermute x72, starting transfers between devices, flip(): return lax.ppermute(value, axis, [(i, i ^ mask) for i in range(size)])  101 us
    ppermute x72, waiting for transfers between devices, flip(): return lax.ppermute(value, axis, [(i, i ^ mask) for i in range(size)])  83.5 us
    pallas_call x1, Pallas kernels, vocab_scores(): pl.pallas_call(functools.partial(scores_body, step_rows=ROWS), grid=(step...  27.1 us
    unnamed x299, local copies, waits for them, and re-layouts  25.4 us
    reduce_sum x9, other arithmetic, fold(): return jnp.sum(squares.reshape(8, cols // LANES, LANES), (0, 1))  23.3 us
    pallas_call x1, Pallas kernels, vocab_grad_rows(): pl.pallas_call(functools.partial(dlogits_body, step_rows=ROWS, unit=unit)...  21.6 us
    pallas_call x2, Pallas kernels, experts_backward(): pl.pallas_call(experts_backward_body, grid=(hidden // tile,), in_specs=[p...  19.3 us
    pallas_call x2, Pallas kernels, experts_forward(): pl.pallas_call(experts_forward_body, grid=(hidden // tile,), in_specs=[pi...  18.1 us
  transfers between devices with their start and end apart: 77, of which 27 were waited for; matrix products, arithmetic and copies ran while one was open for 17% of the time, Pallas kernels for 21%

profile of v4, /device:TPU:0, one launch (start us, length us, event | category | flops | bytes accessed | tf_op | source)
XLA Modules:
  0.0 532.8 jit_solution(12359506014624103901)
XLA Ops:
  15.0 4.8 convert_element_type.379
  36.9 9.6 %collective-permute-done.4.refs_4_ = bf16[208,768]{1,0:T(8,128)(2,1)S(1)} collective-permute-done((bf16[208,768]{1,0:T(8,128)(2,1)S(1)}, bf16[208,768]{1,0:T(8,128)(2,1)S(1)}, u32[]{:S(2)}, u32[]{:S(2)}) %collective-permute-start.4) | collective-permute-done | bytes 319520 | tf_op jit(solution)/shard_map/ppermute | solution.py:65
  50.7 6.4 %collective-permute-done.3.refs_3_ = bf16[208,768]{1,0:T(8,128)(2,1)S(1)} collective-permute-done((bf16[208,768]{1,0:T(8,128)(2,1)S(1)}, bf16[208,768]{1,0:T(8,128)(2,1)S(1)}, u32[]{:S(2)}, u32[]{:S(2)}) %collective-permute-start.3) | collective-permute-done | bytes 319520 | tf_op jit(solution)/shard_map/ppermute | solution.py:65
  63.0 5.2 collective-permute-done.7.refs_7_
  75.9 4.0 convolution_convert_fusion.q_ref.k_ref.v_ref
  80.8 7.9 %attend.1.mixed_ref = bf16[512,768]{1,0:T(8,128)(2,1)S(1)} custom-call(s32[512,1]{1,0:T(8,128)S(1)} %convert_add_fusion.2.seg_col, s32[1,512]{1,0:T(1,128)S(1)} %fusion.75.seg_row, bf16[512,2304]{1,0:T(8,128)(2,1)S(1)} %convolution_convert_fusion.q_ref.k_ref.v_ref, bf16[512,2304]{1,0:T(8,128)(2,1)S(1)} %convolution_convert_fusion.q_ref.k_ref.v_ref, ...), custom_call_target="tpu_custom_call" | custom-call | flops 805306368 | bytes 3145728 | tf_op jit(solution)/shard_map/attend/pallas_call | solution.py:370
  115.5 9.0 %experts_forward.2 = (f32[384,2048]{1,0:T(8,128)}, f32[384,2048]{1,0:T(8,128)}, bf16[384,2048]{1,0:T(8,128)(2,1)S(1)}, bf16[384,768]{1,0:T(8,128)(2,1)S(1)}, bf1...) custom-call(bf16[96,768]{1,0:T(8,128)(2,1)S(1)} %get-tuple-element.3, ...), custom_call_target="tpu_custom_call" | custom-call | flops 3623878656 | bytes 17301504 | tf_op jit(solution)/shard_map/experts_forward/pallas_call | solution.py:486
  128.1 9.1 %experts_forward.3 = (f32[384,2048]{1,0:T(8,128)}, f32[384,2048]{1,0:T(8,128)}, bf16[384,2048]{1,0:T(8,128)(2,1)S(1)}, bf16[384,768]{1,0:T(8,128)(2,1)S(1)}, bf1...) custom-call(bf16[96,768]{1,0:T(8,128)(2,1)S(1)} %collective-permute-, ...), custom_call_target="tpu_custom_call" | custom-call | flops 3623878656 | bytes 17301504 | tf_op jit(solution)/shard_map/experts_forward/pallas_call | solution.py:486
  146.9 4.4 collective-permute-start.29
  153.6 5.4 %collective-permute-done.27 = bf16[96,768]{1,0:T(8,128)(2,1)S(1)} collective-permute-done((bf16[96,768]{1,0:T(8,128)(2,1)S(1)}, bf16[96,768]{1,0:T(8,128)(2,1)S(1)}, u32[]{:S(2)}, u32[]{:S(2)}) %collective-permute-start.27) | collective-permute-done | bytes 147488 | tf_op jit(solution)/shard_map/ppermute | solution.py:65
  165.7 5.4 %collective-permute-start.31 = (bf16[128,768]{1,0:T(8,128)(2,1)S(1)}, bf16[128,768]{1,0:T(8,128)(2,1)S(1)}, u32[]{:S(2)}, u32[]{:S(2)}) collective-permute-start(bf16[128,768]{1,0:T(8,128)(2,1)S(1)} %get-tuple-element.425), channel_id=1, source_target_pairs={{0,8},{4,12},{8,0},{12,4},{16,24},{20,28},{24,16},{28,20},{1,9},{5... | collective-permute-start | bytes 589832 | tf_op jit(solution)/shard_map/ppermute | solution.py:65
  173.6 6.9 %collective-permute-done.33 = bf16[128,768]{1,0:T(8,128)(2,1)S(1)} collective-permute-done((bf16[128,768]{1,0:T(8,128)(2,1)S(1)}, bf16[128,768]{1,0:T(8,128)(2,1)S(1)}, u32[]{:S(2)}, u32[]{:S(2)}) %collective-permute-start.33) | collective-permute-done | bytes 196640 | tf_op jit(solution)/shard_map/ppermute | solution.py:65
  185.2 4.0 collective-permute-done.34
  194.7 27.1 %vocab_scores.1 = (bf16[8192,1024]{1,0:T(8,128)(2,1)}, f32[8,1,1024]{2,1,0:T(1,128)S(1)}, f32[8,1024]{1,0:T(8,128)S(1)}) custom-call(s32[1,1024]{1,0:T(1,128)S(1)} %bitcast.254, bf16[1024,768]{1,0:T(8,128)(2,1)S(1)} %copy-done.19, bf16[8192,768]{1,0:T(8,128)(2,1)} %all-gather.8.cloned.1.call-done.table_ref), custom_call_target="tpu_custom_call" | custom-call | flops 12884901888 | bytes 29360128 | tf_op jit(solution)/shard_map/vocab_scores/pallas_call | solution.py:800
  221.8 11.3 %all_to_all.10 = f32[8,8,8,128]{3,1,2,0:T(8,128)S(1)} all-to-all(f32[8,8,8,128]{3,1,2,0:T(8,128)S(1)} %broadcast_in_dim.125), channel_id=1, replica_groups=mesh['dp'=8,'rep'=4] {'dp'}, dimensions={0} | all-to-all | bytes 524288 | tf_op jit(solution)/shard_map/all_to_all | solution.py:57
  233.9 21.6 %vocab_grad_rows.1 = (bf16[8192,1024]{1,0:T(8,128)(2,1)}, f32[1024,768]{1,0:T(8,128)S(1)}) custom-call(s32[1,1024]{1,0:T(1,128)S(1)} %bitcast.255, f32[8,1,1024]{2,1,0:T(1,128)S(1)} %exponential_multiply_fusion.scale_ref, bf16[8192,1024]{1,0:T(8,128)(2,1)} %get-tuple-element.146.expo_ref, bf16[8192,768]{1,0:T(8,128)(2,1)} %all-gather.8.cloned.1.call-done.table_ref), custom_call_target="tpu_custom_call" | custom-call | flops 12884901888 | bytes 46137344 | tf_op jit(solution)/shard_map/vocab_grad_rows/pallas_call | solution.py:845
  265.8 5.6 %collective-permute-done.42 = bf16[128,768]{1,0:T(8,128)(2,1)S(1)} collective-permute-done((bf16[128,768]{1,0:T(8,128)(2,1)S(1)}, bf16[128,768]{1,0:T(8,128)(2,1)S(1)}, u32[]{:S(2)}, u32[]{:S(2)}) %collective-permute-start.42) | collective-permute-done | bytes 196640 | tf_op jit(solution)/shard_map/ppermute | solution.py:65
  272.3 18.1 %vocab_grad_table.1 = bf16[8192,768]{1,0:T(8,128)(2,1)} custom-call(bf16[8192,1024]{1,0:T(8,128)(2,1)} %get-tuple-element.148.grad_ref, bf16[1024,768]{1,0:T(8,128)(2,1)S(1)} %copy-done.20), custom_call_target="tpu_custom_call" | custom-call | flops 12884901888 | bytes 29360128 | tf_op jit(solution)/shard_map/vocab_grad_table/pallas_call | solution.py:873
  296.0 4.7 head_back.1
  320.3 9.5 %experts_backward.2 = (bf16[2,384,2048]{2,1,0:T(8,128)(2,1)S(1)}, bf16[384,768]{1,0:T(8,128)(2,1)S(1)}, bf16[96,768]{1,0:T(8,128)(2,1)S(1)}, bf16[96,768]{1,0:T(...) custom-call(bf16[96,768]{1,0:T(8,128)(2,1)S(1)} %get-tuple-element.155.refs_0_, ...), custom_call_target="tpu_custom_call" | custom-call | flops 3623878656 | bytes 18874368 | tf_op jit(solution)/shard_map/experts_backward/pallas_call | solution.py:540
  335.0 9.8 %experts_backward.3 = (bf16[2,384,2048]{2,1,0:T(8,128)(2,1)S(1)}, bf16[384,768]{1,0:T(8,128)(2,1)S(1)}, bf16[96,768]{1,0:T(8,128)(2,1)S(1)}, bf16[96,768]{1,0:T(...) custom-call(bf16[96,768]{1,0:T(8,128)(2,1)S(1)} %collective-permute-done.50.refs_0_, ...), custom_call_target="tpu_custom_call" | custom-call | flops 3623878656 | bytes 18874368 | tf_op jit(solution)/shard_map/experts_backward/pallas_call | solution.py:540
  365.6 14.2 %attend_back.1.qkv_ref = bf16[512,2304]{1,0:T(8,128)(2,1)S(1)} custom-call(s32[512,1]{1,0:T(8,128)S(1)} %convert_add_fusion.2.seg_col, s32[1,512]{1,0:T(1,128)S(1)} %fusion.75.seg_row, bf16[512,2304]{1,0:T(8,128)(2,1)S(1)} %convolution_convert_fusion.q_ref.k_ref.v_ref, bf16[512,2304]{1,0:T(8,128)(2,1)S(1)} %convolution_convert_fusion.q_ref.k_ref.v_ref, ...), custom_call_target="tpu_custom_call" | custom-call | flops 2013265920 | bytes 5505024 | tf_op jit(solution)/shard_map/attend_back/pallas_call | solution.py:432
  389.7 7.1 %dense_grads.1 = (bf16[8,2,104,768]{3,2,1,0:T(8,128)(2,1)}, bf16[8,2,104,768]{3,2,1,0:T(8,128)(2,1)}) custom-call(s32[2]{0:T(128)S(1)} %pad_add_fusion.place_ref, bf16[512,2304]{1,0:T(8,128)(2,1)S(1)} %copy-done.9, bf16[512,768]{1,0:T(8,128)(2,1)S(1)} %copy-done.15, bf16[512,768]{1,0:T(8,128)(2,1)S(1)} %copy-done.13, bf16[512,768]{1,0:T(8,128)(2,1)S(1)} %copy-done.11, ...), custom_call_target="tpu_custom_call" | custom-call | flops 2415919104 | bytes 18874368 | tf_op jit(solution)/shard_map/dense_grads/pallas_call | solution.py:260
  396.9 11.6 %grads_in.1 = (bf16[2,2,192,2048]{3,2,1,0:T(8,128)(2,1)S(1)}, bf16[2,2,192,2048]{3,2,1,0:T(8,128)(2,1)}) custom-call(s32[2]{0:T(128)S(1)} %pad_add_fusion.place_ref, bf16[384,768]{1,0:T(8,128)(2,1)S(1)} %copy-done.36, bf16[384,768]{1,0:T(8,128)(2,1)S(1)} %copy-done.38, bf16[2,384,2048]{2,1,0:T(8,128)(2,1)} %copy-done.22, bf16[2,384,2048]{2,1,0:T(8,128)(2,1)} %copy-done.23), custom_call_target="tpu_custom_call" | custom-call | flops 4831838208 | bytes 12582912 | tf_op jit(solution)/shard_map/grads_in/pallas_call | solution.py:589
  411.3 6.8 %collective-permute-done.59 = bf16[8,2,104,768]{3,2,1,0:T(8,128)(2,1)} collective-permute-done((bf16[8,2,104,768]{3,2,1,0:T(8,128)(2,1)}, bf16[8,2,104,768]{3,2,1,0:T(8,128)(2,1)}, u32[]{:S(2)}, u32[]{:S(2)}) %collective-permute-start.59) | collective-permute-done | bytes 2555936 | tf_op jit(solution)/shard_map/ppermute | solution.py:65
  437.6 12.6 %multiply_reduce_fusion = (f32[768]{0:T(1024)S(1)}, f32[768]{0:T(1024)S(1)}, f32[2048,768]{1,0:T(8,128)}, f32[2048,768]{1,0:T(8,128)}) fusion(f32[2048,768]{1,0:T(8,128)} %param.29, bf16[2048,768]{1,0:T(8,128)(2,1)} %reduce-scatter.2.cloned.1.call-done, f32[2048,768]{1,0:T(8,128)} %param.39, f32[2048,768]{1,0:T(8,128)} %param.34), kind=kLoop, calls=%fused_computation.4 | loop fusion | flops 26737152 | bytes 34609152 | tf_op jit(solution)/shard_map/reduce_sum | solution.py:1021
  461.4 4.4 multiply_reduce_fusion.5
  465.9 6.0 %collective-permute-done.70 = bf16[192,2048]{1,0:T(8,128)(2,1)S(1)} collective-permute-done((bf16[192,2048]{1,0:T(8,128)(2,1)S(1)}, bf16[192,2048]{1,0:T(8,128)(2,1)S(1)}, u32[]{:S(2)}, u32[]{:S(2)}) %collective-permute-start.70) | collective-permute-done | bytes 786464 | tf_op jit(solution)/shard_map/ppermute | solution.py:65
  475.4 6.1 %multiply_reduce_fusion.2 = (f32[2048]{0:T(1024)S(1)}, f32[2048]{0:T(1024)S(1)}, f32[2,192,2048]{2,1,0:T(8,128)}, f32[2,192,2048]{2,1,0:T(8,128)}) fusion(f32[2,192,2048]{2,1,0:T(8,128)S(1)} %copy-done.43, bf16[1,192,2048]{2,1,0:T(8,128)(2,1)S(1)} %bitcast.257, bf16[1,192,2048]{2,1,0:T(8,128)(2,1)} %bitcast.64, ...), kind=kLoop, calls=%fused_computation.12 | loop fusion | flops 17297408 | bytes 20463616 | tf_op jit(solution)/shard_map/reduce_sum | solution.py:1021
  483.2 4.6 all-to-all-start.1
  489.2 9.2 %all-to-all-done.1 = f32[32,16,128]{2,1,0:T(8,128)S(1)} async-done(((f32[32,16,128]{2,1,0:T(8,128)}), f32[32,16,128]{2,1,0:T(8,128)S(1)}, u32[]{:S(2)}, u32[]{:S(2)}) %all-to-all-start.1) | async-done | bytes 262176 | tf_op jit(solution)/shard_map/all_to_all | solution.py:57
  505.8 10.7 %fusion.92 = (bf16[2048,768]{1,0:T(8,128)(2,1)}, f32[2048,768]{1,0:T(8,128)}) fusion(f32[2048,768]{1,0:T(8,128)} %param.29, f32[2048,768]{1,0:T(8,128)} %get-tuple-element.321, f32[2048,768]{1,0:T(8,128)} %get-tuple-element.320, f32[]{:T(128)} %bitcast.102), kind=kLoop, calls=%fused_computation.281 | loop fusion | flops 14155776 | bytes 28311556 | tf_op jit(solution)/shard_map/convert_element_type | solution.py:1183
  (600 shorter events, 230.6 us)
Async XLA Ops:
  7.2 107.4 %all-gather.6.cloned.1.call-start = ((), (), s32[]{:S(2)}) async-start(), calls=%async_computation.4 | async-start | bytes 3932160 | tf_op jit(solution)/shard_map/all_gather | solution.py:1095
  11.6 103.0 %all-gather.4.cloned.1.call-start = ((), (), s32[]{:S(2)}) async-start(), calls=%async_computation.3 | async-start | bytes 7864320 | tf_op jit(solution)/shard_map/all_gather | solution.py:1095
  14.9 178.3 %all-gather.8.cloned.1.call-start = ((), (), s32[]{:S(2)}) async-start(), calls=%async_computation.5 | async-start | bytes 15728640 | tf_op jit(solution)/shard_map/all_gather | solution.py:1095
  19.8 417.7 %reduce-scatter.2.cloned.1.call-start = ((), (), s32[]{:S(2)}) async-start(), calls=%async_computation.6 | async-start | bytes 15728640 | tf_op jit(solution)/shard_map/reduce_scatter | solution.py:1108
  34.9 22.2 %collective-permute-start.3 = (bf16[208,768]{1,0:T(8,128)(2,1)S(1)}, bf16[208,768]{1,0:T(8,128)(2,1)S(1)}, u32[]{:S(2)}, u32[]{:S(2)}) collective-permute-start(bf16[208,768]{1,0:T(8,128)(2,1)S(1)} %constant_dynamic-update-slice_fusion.refs_0_), channel_id=1, source_target_pairs={{0,12},{4,8},{8,4},{12,0},{16,28},{20,24},{24,20},{28,16},{1,13},{... | collective-permute-start | bytes 958472 | tf_op jit(solution)/shard_map/ppermute | solution.py:65
  36.3 22.1 %collective-permute-start.1 = (bf16[208,768]{1,0:T(8,128)(2,1)S(1)}, bf16[208,768]{1,0:T(8,128)(2,1)S(1)}, u32[]{:S(2)}, u32[]{:S(2)}) collective-permute-start(bf16[208,768]{1,0:T(8,128)(2,1)S(1)} %constant_dynamic-update-slice_fusion.refs_0_), channel_id=1, source_target_pairs={{0,4},{4,0},{8,12},{12,8},{16,20},{20,16},{24,28},{28,24},{1,5},{5... | collective-permute-start | bytes 958472 | tf_op jit(solution)/shard_map/ppermute | solution.py:65
  36.9 21.6 %collective-permute-start.8 = (bf16[208,768]{1,0:T(8,128)(2,1)S(1)}, bf16[208,768]{1,0:T(8,128)(2,1)S(1)}, u32[]{:S(2)}, u32[]{:S(2)}) collective-permute-start(bf16[208,768]{1,0:T(8,128)(2,1)S(1)} %constant_dynamic-update-slice_fusion.refs_0_), channel_id=1, source_target_pairs={{0,1},{1,0},{2,3},{3,2},{4,5},{5,4},{6,7},{7,6},{8,9},{9,8},{10,11... | collective-permute-start | bytes 958472 | tf_op jit(solution)/shard_map/ppermute | solution.py:65
  93.3 34.8 %collective-permute-start.22 = (bf16[96,768]{1,0:T(8,128)(2,1)}, bf16[96,768]{1,0:T(8,128)(2,1)S(1)}, u32[]{:S(2)}, u32[]{:S(2)}) collective-permute-start(bf16[96,768]{1,0:T(8,128)(2,1)} %get-tuple-element.383), channel_id=1, source_target_pairs={{0,16},{4,20},{8,24},{12,28},{16,0},{20,4},{24,8},{28,12},{1,17},{... | collective-permute-start | bytes 442376 | tf_op jit(solution)/shard_map/ppermute | solution.py:65
  95.3 32.8 %collective-permute-start.23 = (bf16[96,768]{1,0:T(8,128)(2,1)}, bf16[96,768]{1,0:T(8,128)(2,1)S(1)}, u32[]{:S(2)}, u32[]{:S(2)}) collective-permute-start(bf16[96,768]{1,0:T(8,128)(2,1)} %get-tuple-element.382), channel_id=1, source_target_pairs={{0,20},{4,16},{8,28},{12,24},{16,4},{20,0},{24,12},{28,8},{1,21},{... | collective-permute-start | bytes 442376 | tf_op jit(solution)/shard_map/ppermute | solution.py:65
  109.3 18.8 %collective-permute-start.24 = (bf16[96,768]{1,0:T(8,128)(2,1)}, bf16[96,768]{1,0:T(8,128)(2,1)}, u32[]{:S(2)}, u32[]{:S(2)}) collective-permute-start(bf16[96,768]{1,0:T(8,128)(2,1)} %get-tuple-element.381), channel_id=1, source_target_pairs={{0,24},{4,28},{8,16},{12,20},{16,8},{20,12},{24,0},{28,4},{1,25},{... | collective-permute-start | bytes 442376 | tf_op jit(solution)/shard_map/ppermute | solution.py:65
  141.3 17.7 %collective-permute-start.27 = (bf16[96,768]{1,0:T(8,128)(2,1)S(1)}, bf16[96,768]{1,0:T(8,128)(2,1)S(1)}, u32[]{:S(2)}, u32[]{:S(2)}) collective-permute-start(bf16[96,768]{1,0:T(8,128)(2,1)S(1)} %get-tuple-element.140), channel_id=1, source_target_pairs={{0,20},{4,16},{8,28},{12,24},{16,4},{20,0},{24,12},{28,8},{1,21},{... | collective-permute-start | bytes 442376 | tf_op jit(solution)/shard_map/ppermute | solution.py:65
  164.3 18.7 %collective-permute-start.30 = (bf16[128,768]{1,0:T(8,128)(2,1)S(1)}, bf16[128,768]{1,0:T(8,128)(2,1)S(1)}, u32[]{:S(2)}, u32[]{:S(2)}) collective-permute-start(bf16[128,768]{1,0:T(8,128)(2,1)S(1)} %get-tuple-element.425), channel_id=1, source_target_pairs={{0,4},{4,0},{8,12},{12,8},{16,20},{20,16},{24,28},{28,24},{1,5},{5... | collective-permute-start | bytes 589832 | tf_op jit(solution)/shard_map/ppermute | solution.py:65
  165.7 18.3 %collective-permute-start.31 = (bf16[128,768]{1,0:T(8,128)(2,1)S(1)}, bf16[128,768]{1,0:T(8,128)(2,1)S(1)}, u32[]{:S(2)}, u32[]{:S(2)}) collective-permute-start(bf16[128,768]{1,0:T(8,128)(2,1)S(1)} %get-tuple-element.425), channel_id=1, source_target_pairs={{0,8},{4,12},{8,0},{12,4},{16,24},{20,28},{24,16},{28,20},{1,9},{5... | collective-permute-start | bytes 589832 | tf_op jit(solution)/shard_map/ppermute | solution.py:65
  260.0 30.3 %collective-permute-start.37 = (bf16[128,768]{1,0:T(8,128)(2,1)}, bf16[128,768]{1,0:T(8,128)(2,1)S(1)}, u32[]{:S(2)}, u32[]{:S(2)}) collective-permute-start(bf16[128,768]{1,0:T(8,128)(2,1)} %get-tuple-element.378), channel_id=1, source_target_pairs={{0,4},{4,0},{8,12},{12,8},{16,20},{20,16},{24,28},{28,24},{1,5},{5... | collective-permute-start | bytes 589832 | tf_op jit(solution)/shard_map/ppermute | solution.py:65
  260.1 30.3 %collective-permute-start.38 = (bf16[128,768]{1,0:T(8,128)(2,1)}, bf16[128,768]{1,0:T(8,128)(2,1)}, u32[]{:S(2)}, u32[]{:S(2)}) collective-permute-start(bf16[128,768]{1,0:T(8,128)(2,1)} %get-tuple-element.377), channel_id=1, source_target_pairs={{0,8},{4,12},{8,0},{12,4},{16,24},{20,28},{24,16},{28,20},{1,9},{5... | collective-permute-start | bytes 589832 | tf_op jit(solution)/shard_map/ppermute | solution.py:65
  264.9 25.5 %collective-permute-start.39 = (bf16[128,768]{1,0:T(8,128)(2,1)}, bf16[128,768]{1,0:T(8,128)(2,1)}, u32[]{:S(2)}, u32[]{:S(2)}) collective-permute-start(bf16[128,768]{1,0:T(8,128)(2,1)} %get-tuple-element.376), channel_id=1, source_target_pairs={{0,12},{4,8},{8,4},{12,0},{16,28},{20,24},{24,20},{28,16},{1,13},{... | collective-permute-start | bytes 589832 | tf_op jit(solution)/shard_map/ppermute | solution.py:65
  272.2 18.2 %collective-permute-start.43 = (bf16[128,768]{1,0:T(8,128)(2,1)}, bf16[128,768]{1,0:T(8,128)(2,1)}, u32[]{:S(2)}, u32[]{:S(2)}) collective-permute-start(bf16[128,768]{1,0:T(8,128)(2,1)} %add_convert_fusion.10), channel_id=1, source_target_pairs={{0,16},{4,20},{8,24},{12,28},{16,0},{20,4},{24,8},{28,12},{1,17},{... | collective-permute-start | bytes 589832 | tf_op jit(solution)/shard_map/ppermute | solution.py:65
  304.3 28.4 %collective-permute-start.50 = (bf16[96,768]{1,0:T(8,128)(2,1)}, bf16[96,768]{1,0:T(8,128)(2,1)S(1)}, u32[]{:S(2)}, u32[]{:S(2)}) collective-permute-start(bf16[96,768]{1,0:T(8,128)(2,1)} %copy-done.29), channel_id=1, source_target_pairs={{0,16},{4,20},{8,24},{12,28},{16,0},{20,4},{24,8},{28,12},{1,17},{... | collective-permute-start | bytes 442376 | tf_op jit(solution)/shard_map/ppermute | solution.py:65
  307.3 26.8 %collective-permute-start.51 = (bf16[96,768]{1,0:T(8,128)(2,1)}, bf16[96,768]{1,0:T(8,128)(2,1)S(1)}, u32[]{:S(2)}, u32[]{:S(2)}) collective-permute-start(bf16[96,768]{1,0:T(8,128)(2,1)} %copy-done.28), channel_id=1, source_target_pairs={{0,20},{4,16},{8,28},{12,24},{16,4},{20,0},{24,12},{28,8},{1,21},{... | collective-permute-start | bytes 442376 | tf_op jit(solution)/shard_map/ppermute | solution.py:65
  315.7 19.3 %collective-permute-start.52 = (bf16[96,768]{1,0:T(8,128)(2,1)S(1)}, bf16[96,768]{1,0:T(8,128)(2,1)S(1)}, u32[]{:S(2)}, u32[]{:S(2)}) collective-permute-start(bf16[96,768]{1,0:T(8,128)(2,1)S(1)} %copy-done.27), channel_id=1, source_target_pairs={{0,24},{4,28},{8,16},{12,20},{16,8},{20,12},{24,0},{28,4},{1,25},{... | collective-permute-start | bytes 442376 | tf_op jit(solution)/shard_map/ppermute | solution.py:65
  317.9 17.1 %collective-permute-start.53 = (bf16[96,768]{1,0:T(8,128)(2,1)S(1)}, bf16[96,768]{1,0:T(8,128)(2,1)S(1)}, u32[]{:S(2)}, u32[]{:S(2)}) collective-permute-start(bf16[96,768]{1,0:T(8,128)(2,1)S(1)} %get-tuple-element.169), channel_id=1, source_target_pairs={{0,28},{4,24},{8,20},{12,16},{16,12},{20,8},{24,4},{28,0},{1,29},{... | collective-permute-start | bytes 442376 | tf_op jit(solution)/shard_map/ppermute | solution.py:65
  332.7 18.2 %collective-permute-start.48 = (bf16[96,768]{1,0:T(8,128)(2,1)S(1)}, bf16[96,768]{1,0:T(8,128)(2,1)S(1)}, u32[]{:S(2)}, u32[]{:S(2)}) collective-permute-start(bf16[96,768]{1,0:T(8,128)(2,1)S(1)} %get-tuple-element.163), channel_id=1, source_target_pairs={{0,8},{4,12},{8,0},{12,4},{16,24},{20,28},{24,16},{28,20},{1,9},{5... | collective-permute-start | bytes 442376 | tf_op jit(solution)/shard_map/ppermute | solution.py:65
  334.1 18.5 %collective-permute-start.49 = (bf16[96,768]{1,0:T(8,128)(2,1)S(1)}, bf16[96,768]{1,0:T(8,128)(2,1)S(1)}, u32[]{:S(2)}, u32[]{:S(2)}) collective-permute-start(bf16[96,768]{1,0:T(8,128)(2,1)S(1)} %get-tuple-element.164), channel_id=1, source_target_pairs={{0,12},{4,8},{8,4},{12,0},{16,28},{20,24},{24,20},{28,16},{1,13},{... | collective-permute-start | bytes 442376 | tf_op jit(solution)/shard_map/ppermute | solution.py:65
  359.5 21.3 %collective-permute-start.58 = (bf16[2,512,768]{2,1,0:T(8,128)(2,1)S(1)}, bf16[2,512,768]{2,1,0:T(8,128)(2,1)S(1)}, u32[]{:S(2)}, u32[]{:S(2)}) collective-permute-start(bf16[2,512,768]{2,1,0:T(8,128)(2,1)S(1)} %grads_out.2), channel_id=1, source_target_pairs={{0,1},{1,0},{2,3},{3,2},{4,5},{5,4},{6,7},{7,6},{8,9},{9,8},{10,11... | collective-permute-start | bytes 4718600 | tf_op jit(solution)/shard_map/ppermute | solution.py:65
  386.2 22.3 %collective-permute-start.66 = (bf16[512,768]{1,0:T(8,128)(2,1)}, bf16[512,768]{1,0:T(8,128)(2,1)}, u32[]{:S(2)}, u32[]{:S(2)}) collective-permute-start(bf16[512,768]{1,0:T(8,128)(2,1)} %fusion.22), channel_id=1, source_target_pairs={{0,2},{1,3},{2,0},{3,1},{4,6},{5,7},{6,4},{7,5},{8,10},{9,11},{10,... | collective-permute-start | bytes 2359304 | tf_op jit(solution)/shard_map/ppermute | solution.py:65
  408.5 19.4 %collective-permute-start.67 = (bf16[2,2,192,2048]{3,2,1,0:T(8,128)(2,1)}, bf16[2,2,192,2048]{3,2,1,0:T(8,128)(2,1)}, u32[]{:S(2)}, u32[]{:S(2)}) collective-permute-start(bf16[2,2,192,2048]{3,2,1,0:T(8,128)(2,1)} %get-tuple-element.210), channel_id=1, source_target_pairs={{0,1},{1,0},{2,3},{3,2},{4,5},{5,4},{6,7},{7,6},{8,9},{9,8},{10,11... | collective-permute-start | bytes 9437192 | tf_op jit(solution)/shard_map/ppermute | solution.py:65
  426.4 23.9 %collective-permute-start.62 = (bf16[2,104,768]{2,1,0:T(8,128)(2,1)}, bf16[2,104,768]{2,1,0:T(8,128)(2,1)}, u32[]{:S(2)}, u32[]{:S(2)}) collective-permute-start(bf16[2,104,768]{2,1,0:T(8,128)(2,1)} %get-tuple-element.368), channel_id=1, source_target_pairs={{0,12},{4,8},{8,4},{12,0},{16,28},{20,24},{24,20},{28,16},{1,13},{... | collective-permute-start | bytes 958472 | tf_op jit(solution)/shard_map/ppermute | solution.py:65
  426.9 25.3 %collective-permute-start.63 = (bf16[2,104,768]{2,1,0:T(8,128)(2,1)}, bf16[2,104,768]{2,1,0:T(8,128)(2,1)}, u32[]{:S(2)}, u32[]{:S(2)}) collective-permute-start(bf16[2,104,768]{2,1,0:T(8,128)(2,1)} %get-tuple-element.367), channel_id=1, source_target_pairs={{0,4},{4,0},{8,12},{12,8},{16,20},{20,16},{24,28},{28,24},{1,5},{5... | collective-permute-start | bytes 958472 | tf_op jit(solution)/shard_map/ppermute | solution.py:65
  427.8 24.4 %collective-permute-start.64 = (bf16[2,104,768]{2,1,0:T(8,128)(2,1)}, bf16[2,104,768]{2,1,0:T(8,128)(2,1)}, u32[]{:S(2)}, u32[]{:S(2)}) collective-permute-start(bf16[2,104,768]{2,1,0:T(8,128)(2,1)} %get-tuple-element.366), channel_id=1, source_target_pairs={{0,8},{4,12},{8,0},{12,4},{16,24},{20,28},{24,16},{28,20},{1,9},{5... | collective-permute-start | bytes 958472 | tf_op jit(solution)/shard_map/ppermute | solution.py:65
  433.0 22.2 %collective-permute-start.65 = (bf16[2,104,768]{2,1,0:T(8,128)(2,1)}, bf16[2,104,768]{2,1,0:T(8,128)(2,1)}, u32[]{:S(2)}, u32[]{:S(2)}) collective-permute-start(bf16[2,104,768]{2,1,0:T(8,128)(2,1)} %get-tuple-element.365), channel_id=1, source_target_pairs={{0,12},{4,8},{8,4},{12,0},{16,28},{20,24},{24,20},{28,16},{1,13},{... | collective-permute-start | bytes 958472 | tf_op jit(solution)/shard_map/ppermute | solution.py:65
  437.4 20.8 %collective-permute-start.68 = (bf16[192,2048]{1,0:T(8,128)(2,1)}, bf16[192,2048]{1,0:T(8,128)(2,1)}, u32[]{:S(2)}, u32[]{:S(2)}) collective-permute-start(bf16[192,2048]{1,0:T(8,128)(2,1)} %get-tuple-element.364), channel_id=1, source_target_pairs={{0,2},{1,3},{2,0},{3,1},{4,6},{5,7},{6,4},{7,5},{8,10},{9,11},{10,... | collective-permute-start | bytes 2359304 | tf_op jit(solution)/shard_map/ppermute | solution.py:65
  450.3 21.6 %collective-permute-start.70 = (bf16[192,2048]{1,0:T(8,128)(2,1)S(1)}, bf16[192,2048]{1,0:T(8,128)(2,1)S(1)}, u32[]{:S(2)}, u32[]{:S(2)}) collective-permute-start(bf16[192,2048]{1,0:T(8,128)(2,1)S(1)} %copy-done.69), channel_id=1, source_target_pairs={{0,2},{1,3},{2,0},{3,1},{4,6},{5,7},{6,4},{7,5},{8,10},{9,11},{10,... | collective-permute-start | bytes 2359304 | tf_op jit(solution)/shard_map/ppermute | solution.py:65
  (180 other events, 1695.1 us)
Sparse Core Ops, SparseCore 0:
  11.7 33.6 all-gather.5
  47.5 47.3 all-gather.3
  97.1 82.0 all-gather.7
  290.6 99.7 reduce-scatter.1

commit v5 on v4

--- a/solution.py
+++ b/solution.py
@@ -480,7 +480,7 @@
 
 def experts_forward(pieces, w_in, w_out):
     rows, hidden = len(pieces) * CAP, w_out.shape[0]
-    tile = min(hidden, 512)
+    tile = min(hidden, 1024)
     piece = full((CAP, D))
     band = pl.BlockSpec((rows, tile), lambda j: (0, j))
     gate, up, inner, joined, *parts = pl.pallas_call(
@@ -534,7 +534,7 @@
 
 def experts_backward(pieces, gate, up, w_in, w_out):
     rows, hidden = gate.shape
-    tile = min(hidden, 512)
+    tile = min(hidden, 1024)
     piece = full((CAP, D))
     band = pl.BlockSpec((rows, tile), lambda j: (0, j))
     backs, joined, *parts = pl.pallas_call(
@@ -582,7 +582,7 @@
 
 def grads_in(place, rows_a, rows_b, back_a, back_b):
     rows, hidden = back_a.shape[1:]
-    tile = 512
+    tile = 1024
     size = D // 4
     back = pl.BlockSpec((1, rows, tile), lambda k, j, place: (k, 0, j))
     out = pl.BlockSpec((1, 2, size, tile), lambda k, j, place: (k, 0, 0, j))

time: 537 us -> 534 us (level)
  transfers between devices with their start and end apart: 77 -> 77, of which waited for: 27 -> 27; matrix products, arithmetic and copies ran while one was open for 17% -> 17% of each run, Pallas kernels for 21% -> 20%
where the time goes in v5:
time: 534 us; the launch traced here: 530 us
  Pallas kernels  156 us (29%)
  starting transfers between devices  106 us (20%)
  waiting for transfers between devices  93 us (17%)
  other arithmetic  88 us (16%)
  local copies, waits for them, and re-layouts  38.1 us (7%)
  matrix products  18.8 us (4%)
  between operations  18.7 us (4%)
  blocking collectives  11.3 us (2%)
    ppermute x72, starting transfers between devices, flip(): return lax.ppermute(value, axis, [(i, i ^ mask) for i in range(size)])  102 us
    ppermute x72, waiting for transfers between devices, flip(): return lax.ppermute(value, axis, [(i, i ^ mask) for i in range(size)])  83.7 us
    pallas_call x1, Pallas kernels, vocab_scores(): pl.pallas_call(functools.partial(scores_body, step_rows=ROWS), grid=(step...  27.1 us
    unnamed x299, local copies, waits for them, and re-layouts  25.4 us
    reduce_sum x9, other arithmetic, fold(): return jnp.sum(squares.reshape(8, cols // LANES, LANES), (0, 1))  23.3 us
    pallas_call x1, Pallas kernels, vocab_grad_rows(): pl.pallas_call(functools.partial(dlogits_body, step_rows=ROWS, unit=unit)...  21.6 us
    pallas_call x2, Pallas kernels, experts_backward(): pl.pallas_call(experts_backward_body, grid=(hidden // tile,), in_specs=[p...  19.1 us
    pallas_call x1, Pallas kernels, vocab_grad_table(): pl.pallas_call(vocab_grad_table_body, grid=(vocab // tile,), in_specs=[pl...  18.1 us
  transfers between devices with their start and end apart: 77, of which 27 were waited for; matrix products, arithmetic and copies ran while one was open for 17% of the time, Pallas kernels for 20%

profile of v5, /device:TPU:0, one launch (start us, length us, event | category | flops | bytes accessed | tf_op | source)
XLA Modules:
  0.0 529.8 jit_solution(10139727429901448044)
XLA Ops:
  15.0 4.8 convert_element_type.379
  36.9 9.6 %collective-permute-done.4.refs_4_ = bf16[208,768]{1,0:T(8,128)(2,1)S(1)} collective-permute-done((bf16[208,768]{1,0:T(8,128)(2,1)S(1)}, bf16[208,768]{1,0:T(8,128)(2,1)S(1)}, u32[]{:S(2)}, u32[]{:S(2)}) %collective-permute-start.4) | collective-permute-done | bytes 319520 | tf_op jit(solution)/shard_map/ppermute | solution.py:65
  50.7 6.4 %collective-permute-done.3.refs_3_ = bf16[208,768]{1,0:T(8,128)(2,1)S(1)} collective-permute-done((bf16[208,768]{1,0:T(8,128)(2,1)S(1)}, bf16[208,768]{1,0:T(8,128)(2,1)S(1)}, u32[]{:S(2)}, u32[]{:S(2)}) %collective-permute-start.3) | collective-permute-done | bytes 319520 | tf_op jit(solution)/shard_map/ppermute | solution.py:65
  63.0 5.2 collective-permute-done.7.refs_7_
  75.9 4.0 convolution_convert_fusion.q_ref.k_ref.v_ref
  80.8 7.9 %attend.1.mixed_ref = bf16[512,768]{1,0:T(8,128)(2,1)S(1)} custom-call(s32[512,1]{1,0:T(8,128)S(1)} %convert_add_fusion.2.seg_col, s32[1,512]{1,0:T(1,128)S(1)} %fusion.75.seg_row, bf16[512,2304]{1,0:T(8,128)(2,1)S(1)} %convolution_convert_fusion.q_ref.k_ref.v_ref, bf16[512,2304]{1,0:T(8,128)(2,1)S(1)} %convolution_convert_fusion.q_ref.k_ref.v_ref, ...), custom_call_target="tpu_custom_call" | custom-call | flops 805306368 | bytes 3145728 | tf_op jit(solution)/shard_map/attend/pallas_call | solution.py:370
  115.5 8.7 %experts_forward.2 = (f32[384,2048]{1,0:T(8,128)}, f32[384,2048]{1,0:T(8,128)}, bf16[384,2048]{1,0:T(8,128)(2,1)S(1)}, bf16[384,768]{1,0:T(8,128)(2,1)S(1)}, bf1...) custom-call(bf16[96,768]{1,0:T(8,128)(2,1)S(1)} %get-tuple-element.3, ...), custom_call_target="tpu_custom_call" | custom-call | flops 3623878656 | bytes 17301504 | tf_op jit(solution)/shard_map/experts_forward/pallas_call | solution.py:486
  127.8 9.2 %experts_forward.3 = (f32[384,2048]{1,0:T(8,128)}, f32[384,2048]{1,0:T(8,128)}, bf16[384,2048]{1,0:T(8,128)(2,1)S(1)}, bf16[384,768]{1,0:T(8,128)(2,1)S(1)}, bf1...) custom-call(bf16[96,768]{1,0:T(8,128)(2,1)S(1)} %collective-permute-, ...), custom_call_target="tpu_custom_call" | custom-call | flops 3623878656 | bytes 17301504 | tf_op jit(solution)/shard_map/experts_forward/pallas_call | solution.py:486
  146.7 4.3 collective-permute-start.29
  153.3 5.5 %collective-permute-done.27 = bf16[96,768]{1,0:T(8,128)(2,1)S(1)} collective-permute-done((bf16[96,768]{1,0:T(8,128)(2,1)S(1)}, bf16[96,768]{1,0:T(8,128)(2,1)S(1)}, u32[]{:S(2)}, u32[]{:S(2)}) %collective-permute-start.27) | collective-permute-done | bytes 147488 | tf_op jit(solution)/shard_map/ppermute | solution.py:65
  165.1 5.4 %collective-permute-start.31 = (bf16[128,768]{1,0:T(8,128)(2,1)S(1)}, bf16[128,768]{1,0:T(8,128)(2,1)S(1)}, u32[]{:S(2)}, u32[]{:S(2)}) collective-permute-start(bf16[128,768]{1,0:T(8,128)(2,1)S(1)} %get-tuple-element.425), channel_id=1, source_target_pairs={{0,8},{4,12},{8,0},{12,4},{16,24},{20,28},{24,16},{28,20},{1,9},{5... | collective-permute-start | bytes 589832 | tf_op jit(solution)/shard_map/ppermute | solution.py:65
  172.8 6.8 %collective-permute-done.33 = bf16[128,768]{1,0:T(8,128)(2,1)S(1)} collective-permute-done((bf16[128,768]{1,0:T(8,128)(2,1)S(1)}, bf16[128,768]{1,0:T(8,128)(2,1)S(1)}, u32[]{:S(2)}, u32[]{:S(2)}) %collective-permute-start.33) | collective-permute-done | bytes 196640 | tf_op jit(solution)/shard_map/ppermute | solution.py:65
  193.9 27.1 %vocab_scores.1 = (bf16[8192,1024]{1,0:T(8,128)(2,1)}, f32[8,1,1024]{2,1,0:T(1,128)S(1)}, f32[8,1024]{1,0:T(8,128)S(1)}) custom-call(s32[1,1024]{1,0:T(1,128)S(1)} %bitcast.254, bf16[1024,768]{1,0:T(8,128)(2,1)S(1)} %copy-done.19, bf16[8192,768]{1,0:T(8,128)(2,1)} %all-gather.8.cloned.1.call-done.table_ref), custom_call_target="tpu_custom_call" | custom-call | flops 12884901888 | bytes 29360128 | tf_op jit(solution)/shard_map/vocab_scores/pallas_call | solution.py:800
  221.0 11.3 %all_to_all.10 = f32[8,8,8,128]{3,1,2,0:T(8,128)S(1)} all-to-all(f32[8,8,8,128]{3,1,2,0:T(8,128)S(1)} %broadcast_in_dim.125), channel_id=1, replica_groups=mesh['dp'=8,'rep'=4] {'dp'}, dimensions={0} | all-to-all | bytes 524288 | tf_op jit(solution)/shard_map/all_to_all | solution.py:57
  233.1 21.6 %vocab_grad_rows.1 = (bf16[8192,1024]{1,0:T(8,128)(2,1)}, f32[1024,768]{1,0:T(8,128)S(1)}) custom-call(s32[1,1024]{1,0:T(1,128)S(1)} %bitcast.255, f32[8,1,1024]{2,1,0:T(1,128)S(1)} %exponential_multiply_fusion.scale_ref, bf16[8192,1024]{1,0:T(8,128)(2,1)} %get-tuple-element.146.expo_ref, bf16[8192,768]{1,0:T(8,128)(2,1)} %all-gather.8.cloned.1.call-done.table_ref), custom_call_target="tpu_custom_call" | custom-call | flops 12884901888 | bytes 46137344 | tf_op jit(solution)/shard_map/vocab_grad_rows/pallas_call | solution.py:845
  265.0 5.7 %collective-permute-done.42 = bf16[128,768]{1,0:T(8,128)(2,1)S(1)} collective-permute-done((bf16[128,768]{1,0:T(8,128)(2,1)S(1)}, bf16[128,768]{1,0:T(8,128)(2,1)S(1)}, u32[]{:S(2)}, u32[]{:S(2)}) %collective-permute-start.42) | collective-permute-done | bytes 196640 | tf_op jit(solution)/shard_map/ppermute | solution.py:65
  271.5 18.1 %vocab_grad_table.1 = bf16[8192,768]{1,0:T(8,128)(2,1)} custom-call(bf16[8192,1024]{1,0:T(8,128)(2,1)} %get-tuple-element.148.grad_ref, bf16[1024,768]{1,0:T(8,128)(2,1)S(1)} %copy-done.20), custom_call_target="tpu_custom_call" | custom-call | flops 12884901888 | bytes 29360128 | tf_op jit(solution)/shard_map/vocab_grad_table/pallas_call | solution.py:873
  295.4 4.4 head_back.1
  319.3 9.4 %experts_backward.2 = (bf16[2,384,2048]{2,1,0:T(8,128)(2,1)S(1)}, bf16[384,768]{1,0:T(8,128)(2,1)S(1)}, bf16[96,768]{1,0:T(8,128)(2,1)S(1)}, bf16[96,768]{1,0:T(...) custom-call(bf16[96,768]{1,0:T(8,128)(2,1)S(1)} %get-tuple-element.155.refs_0_, ...), custom_call_target="tpu_custom_call" | custom-call | flops 3623878656 | bytes 18874368 | tf_op jit(solution)/shard_map/experts_backward/pallas_call | solution.py:540
  333.9 9.7 %experts_backward.3 = (bf16[2,384,2048]{2,1,0:T(8,128)(2,1)S(1)}, bf16[384,768]{1,0:T(8,128)(2,1)S(1)}, bf16[96,768]{1,0:T(8,128)(2,1)S(1)}, bf16[96,768]{1,0:T(...) custom-call(bf16[96,768]{1,0:T(8,128)(2,1)S(1)} %collective-permute-done.50.refs_0_, ...), custom_call_target="tpu_custom_call" | custom-call | flops 3623878656 | bytes 18874368 | tf_op jit(solution)/shard_map/experts_backward/pallas_call | solution.py:540
  364.2 14.2 %attend_back.1.qkv_ref = bf16[512,2304]{1,0:T(8,128)(2,1)S(1)} custom-call(s32[512,1]{1,0:T(8,128)S(1)} %convert_add_fusion.2.seg_col, s32[1,512]{1,0:T(1,128)S(1)} %fusion.75.seg_row, bf16[512,2304]{1,0:T(8,128)(2,1)S(1)} %convolution_convert_fusion.q_ref.k_ref.v_ref, bf16[512,2304]{1,0:T(8,128)(2,1)S(1)} %convolution_convert_fusion.q_ref.k_ref.v_ref, ...), custom_call_target="tpu_custom_call" | custom-call | flops 2013265920 | bytes 5505024 | tf_op jit(solution)/shard_map/attend_back/pallas_call | solution.py:432
  388.7 7.1 %dense_grads.1 = (bf16[8,2,104,768]{3,2,1,0:T(8,128)(2,1)}, bf16[8,2,104,768]{3,2,1,0:T(8,128)(2,1)}) custom-call(s32[2]{0:T(128)S(1)} %pad_add_fusion.place_ref, bf16[512,2304]{1,0:T(8,128)(2,1)S(1)} %copy-done.9, bf16[512,768]{1,0:T(8,128)(2,1)S(1)} %copy-done.15, bf16[512,768]{1,0:T(8,128)(2,1)S(1)} %copy-done.13, bf16[512,768]{1,0:T(8,128)(2,1)S(1)} %copy-done.11, ...), custom_call_target="tpu_custom_call" | custom-call | flops 2415919104 | bytes 18874368 | tf_op jit(solution)/shard_map/dense_grads/pallas_call | solution.py:260
  395.9 9.6 %grads_in.1 = (bf16[2,2,192,2048]{3,2,1,0:T(8,128)(2,1)S(1)}, bf16[2,2,192,2048]{3,2,1,0:T(8,128)(2,1)}) custom-call(s32[2]{0:T(128)S(1)} %pad_add_fusion.place_ref, bf16[384,768]{1,0:T(8,128)(2,1)S(1)} %copy-done.36, bf16[384,768]{1,0:T(8,128)(2,1)S(1)} %copy-done.38, bf16[2,384,2048]{2,1,0:T(8,128)(2,1)} %copy-done.22, bf16[2,384,2048]{2,1,0:T(8,128)(2,1)} %copy-done.23), custom_call_target="tpu_custom_call" | custom-call | flops 4831838208 | bytes 12582912 | tf_op jit(solution)/shard_map/grads_in/pallas_call | solution.py:589
  408.4 6.8 %collective-permute-done.59 = bf16[8,2,104,768]{3,2,1,0:T(8,128)(2,1)} collective-permute-done((bf16[8,2,104,768]{3,2,1,0:T(8,128)(2,1)}, bf16[8,2,104,768]{3,2,1,0:T(8,128)(2,1)}, u32[]{:S(2)}, u32[]{:S(2)}) %collective-permute-start.59) | collective-permute-done | bytes 2555936 | tf_op jit(solution)/shard_map/ppermute | solution.py:65
  430.0 3.9 collective-permute-start.65
  436.3 12.6 %multiply_reduce_fusion = (f32[768]{0:T(1024)S(1)}, f32[768]{0:T(1024)S(1)}, f32[2048,768]{1,0:T(8,128)}, f32[2048,768]{1,0:T(8,128)}) fusion(f32[2048,768]{1,0:T(8,128)} %param.29, bf16[2048,768]{1,0:T(8,128)(2,1)} %reduce-scatter.2.cloned.1.call-done, f32[2048,768]{1,0:T(8,128)} %param.39, f32[2048,768]{1,0:T(8,128)} %param.34), kind=kLoop, calls=%fused_computation.4 | loop fusion | flops 26737152 | bytes 34609152 | tf_op jit(solution)/shard_map/reduce_sum | solution.py:1021
  458.0 4.4 multiply_reduce_fusion.5
  462.4 6.2 %collective-permute-done.70 = bf16[192,2048]{1,0:T(8,128)(2,1)S(1)} collective-permute-done((bf16[192,2048]{1,0:T(8,128)(2,1)S(1)}, bf16[192,2048]{1,0:T(8,128)(2,1)S(1)}, u32[]{:S(2)}, u32[]{:S(2)}) %collective-permute-start.70) | collective-permute-done | bytes 786464 | tf_op jit(solution)/shard_map/ppermute | solution.py:65
  473.6 6.1 %multiply_reduce_fusion.2 = (f32[2048]{0:T(1024)S(1)}, f32[2048]{0:T(1024)S(1)}, f32[2,192,2048]{2,1,0:T(8,128)}, f32[2,192,2048]{2,1,0:T(8,128)}) fusion(f32[2,192,2048]{2,1,0:T(8,128)S(1)} %copy-done.43, bf16[1,192,2048]{2,1,0:T(8,128)(2,1)S(1)} %bitcast.257, bf16[1,192,2048]{2,1,0:T(8,128)(2,1)} %bitcast.64, ...), kind=kLoop, calls=%fused_computation.12 | loop fusion | flops 17297408 | bytes 20463616 | tf_op jit(solution)/shard_map/reduce_sum | solution.py:1021
  486.2 9.2 %all-to-all-done.1 = f32[32,16,128]{2,1,0:T(8,128)S(1)} async-done(((f32[32,16,128]{2,1,0:T(8,128)}), f32[32,16,128]{2,1,0:T(8,128)S(1)}, u32[]{:S(2)}, u32[]{:S(2)}) %all-to-all-start.1) | async-done | bytes 262176 | tf_op jit(solution)/shard_map/all_to_all | solution.py:57
  502.8 10.7 %fusion.92 = (bf16[2048,768]{1,0:T(8,128)(2,1)}, f32[2048,768]{1,0:T(8,128)}) fusion(f32[2048,768]{1,0:T(8,128)} %param.29, f32[2048,768]{1,0:T(8,128)} %get-tuple-element.321, f32[2048,768]{1,0:T(8,128)} %get-tuple-element.320, f32[]{:T(128)} %bitcast.102), kind=kLoop, calls=%fused_computation.281 | loop fusion | flops 14155776 | bytes 28311556 | tf_op jit(solution)/shard_map/convert_element_type | solution.py:1183
  517.7 3.9 fusion.94
  (600 shorter events, 230.9 us)
Async XLA Ops:
  7.2 107.4 %all-gather.6.cloned.1.call-start = ((), (), s32[]{:S(2)}) async-start(), calls=%async_computation.4 | async-start | bytes 3932160 | tf_op jit(solution)/shard_map/all_gather | solution.py:1095
  11.6 103.0 %all-gather.4.cloned.1.call-start = ((), (), s32[]{:S(2)}) async-start(), calls=%async_computation.3 | async-start | bytes 7864320 | tf_op jit(solution)/shard_map/all_gather | solution.py:1095
  14.9 177.5 %all-gather.8.cloned.1.call-start = ((), (), s32[]{:S(2)}) async-start(), calls=%async_computation.5 | async-start | bytes 15728640 | tf_op jit(solution)/shard_map/all_gather | solution.py:1095
  19.8 416.5 %reduce-scatter.2.cloned.1.call-start = ((), (), s32[]{:S(2)}) async-start(), calls=%async_computation.6 | async-start | bytes 15728640 | tf_op jit(solution)/shard_map/reduce_scatter | solution.py:1108
  34.9 22.2 %collective-permute-start.3 = (bf16[208,768]{1,0:T(8,128)(2,1)S(1)}, bf16[208,768]{1,0:T(8,128)(2,1)S(1)}, u32[]{:S(2)}, u32[]{:S(2)}) collective-permute-start(bf16[208,768]{1,0:T(8,128)(2,1)S(1)} %constant_dynamic-update-slice_fusion.refs_0_), channel_id=1, source_target_pairs={{0,12},{4,8},{8,4},{12,0},{16,28},{20,24},{24,20},{28,16},{1,13},{... | collective-permute-start | bytes 958472 | tf_op jit(solution)/shard_map/ppermute | solution.py:65
  36.3 22.1 %collective-permute-start.1 = (bf16[208,768]{1,0:T(8,128)(2,1)S(1)}, bf16[208,768]{1,0:T(8,128)(2,1)S(1)}, u32[]{:S(2)}, u32[]{:S(2)}) collective-permute-start(bf16[208,768]{1,0:T(8,128)(2,1)S(1)} %constant_dynamic-update-slice_fusion.refs_0_), channel_id=1, source_target_pairs={{0,4},{4,0},{8,12},{12,8},{16,20},{20,16},{24,28},{28,24},{1,5},{5... | collective-permute-start | bytes 958472 | tf_op jit(solution)/shard_map/ppermute | solution.py:65
  36.9 21.6 %collective-permute-start.8 = (bf16[208,768]{1,0:T(8,128)(2,1)S(1)}, bf16[208,768]{1,0:T(8,128)(2,1)S(1)}, u32[]{:S(2)}, u32[]{:S(2)}) collective-permute-start(bf16[208,768]{1,0:T(8,128)(2,1)S(1)} %constant_dynamic-update-slice_fusion.refs_0_), channel_id=1, source_target_pairs={{0,1},{1,0},{2,3},{3,2},{4,5},{5,4},{6,7},{7,6},{8,9},{9,8},{10,11... | collective-permute-start | bytes 958472 | tf_op jit(solution)/shard_map/ppermute | solution.py:65
  93.3 34.4 %collective-permute-start.22 = (bf16[96,768]{1,0:T(8,128)(2,1)}, bf16[96,768]{1,0:T(8,128)(2,1)S(1)}, u32[]{:S(2)}, u32[]{:S(2)}) collective-permute-start(bf16[96,768]{1,0:T(8,128)(2,1)} %get-tuple-element.383), channel_id=1, source_target_pairs={{0,16},{4,20},{8,24},{12,28},{16,0},{20,4},{24,8},{28,12},{1,17},{... | collective-permute-start | bytes 442376 | tf_op jit(solution)/shard_map/ppermute | solution.py:65
  95.3 32.4 %collective-permute-start.23 = (bf16[96,768]{1,0:T(8,128)(2,1)}, bf16[96,768]{1,0:T(8,128)(2,1)S(1)}, u32[]{:S(2)}, u32[]{:S(2)}) collective-permute-start(bf16[96,768]{1,0:T(8,128)(2,1)} %get-tuple-element.382), channel_id=1, source_target_pairs={{0,20},{4,16},{8,28},{12,24},{16,4},{20,0},{24,12},{28,8},{1,21},{... | collective-permute-start | bytes 442376 | tf_op jit(solution)/shard_map/ppermute | solution.py:65
  109.3 18.5 %collective-permute-start.24 = (bf16[96,768]{1,0:T(8,128)(2,1)}, bf16[96,768]{1,0:T(8,128)(2,1)}, u32[]{:S(2)}, u32[]{:S(2)}) collective-permute-start(bf16[96,768]{1,0:T(8,128)(2,1)} %get-tuple-element.381), channel_id=1, source_target_pairs={{0,24},{4,28},{8,16},{12,20},{16,8},{20,12},{24,0},{28,4},{1,25},{... | collective-permute-start | bytes 442376 | tf_op jit(solution)/shard_map/ppermute | solution.py:65
  140.9 17.8 %collective-permute-start.27 = (bf16[96,768]{1,0:T(8,128)(2,1)S(1)}, bf16[96,768]{1,0:T(8,128)(2,1)S(1)}, u32[]{:S(2)}, u32[]{:S(2)}) collective-permute-start(bf16[96,768]{1,0:T(8,128)(2,1)S(1)} %get-tuple-element.140), channel_id=1, source_target_pairs={{0,20},{4,16},{8,28},{12,24},{16,4},{20,0},{24,12},{28,8},{1,21},{... | collective-permute-start | bytes 442376 | tf_op jit(solution)/shard_map/ppermute | solution.py:65
  163.5 18.7 %collective-permute-start.30 = (bf16[128,768]{1,0:T(8,128)(2,1)S(1)}, bf16[128,768]{1,0:T(8,128)(2,1)S(1)}, u32[]{:S(2)}, u32[]{:S(2)}) collective-permute-start(bf16[128,768]{1,0:T(8,128)(2,1)S(1)} %get-tuple-element.425), channel_id=1, source_target_pairs={{0,4},{4,0},{8,12},{12,8},{16,20},{20,16},{24,28},{28,24},{1,5},{5... | collective-permute-start | bytes 589832 | tf_op jit(solution)/shard_map/ppermute | solution.py:65
  165.1 18.1 %collective-permute-start.31 = (bf16[128,768]{1,0:T(8,128)(2,1)S(1)}, bf16[128,768]{1,0:T(8,128)(2,1)S(1)}, u32[]{:S(2)}, u32[]{:S(2)}) collective-permute-start(bf16[128,768]{1,0:T(8,128)(2,1)S(1)} %get-tuple-element.425), channel_id=1, source_target_pairs={{0,8},{4,12},{8,0},{12,4},{16,24},{20,28},{24,16},{28,20},{1,9},{5... | collective-permute-start | bytes 589832 | tf_op jit(solution)/shard_map/ppermute | solution.py:65
  259.3 30.4 %collective-permute-start.37 = (bf16[128,768]{1,0:T(8,128)(2,1)}, bf16[128,768]{1,0:T(8,128)(2,1)S(1)}, u32[]{:S(2)}, u32[]{:S(2)}) collective-permute-start(bf16[128,768]{1,0:T(8,128)(2,1)} %get-tuple-element.378), channel_id=1, source_target_pairs={{0,4},{4,0},{8,12},{12,8},{16,20},{20,16},{24,28},{28,24},{1,5},{5... | collective-permute-start | bytes 589832 | tf_op jit(solution)/shard_map/ppermute | solution.py:65
  259.3 30.4 %collective-permute-start.38 = (bf16[128,768]{1,0:T(8,128)(2,1)}, bf16[128,768]{1,0:T(8,128)(2,1)}, u32[]{:S(2)}, u32[]{:S(2)}) collective-permute-start(bf16[128,768]{1,0:T(8,128)(2,1)} %get-tuple-element.377), channel_id=1, source_target_pairs={{0,8},{4,12},{8,0},{12,4},{16,24},{20,28},{24,16},{28,20},{1,9},{5... | collective-permute-start | bytes 589832 | tf_op jit(solution)/shard_map/ppermute | solution.py:65
  264.1 25.6 %collective-permute-start.39 = (bf16[128,768]{1,0:T(8,128)(2,1)}, bf16[128,768]{1,0:T(8,128)(2,1)}, u32[]{:S(2)}, u32[]{:S(2)}) collective-permute-start(bf16[128,768]{1,0:T(8,128)(2,1)} %get-tuple-element.376), channel_id=1, source_target_pairs={{0,12},{4,8},{8,4},{12,0},{16,28},{20,24},{24,20},{28,16},{1,13},{... | collective-permute-start | bytes 589832 | tf_op jit(solution)/shard_map/ppermute | solution.py:65
  271.5 18.1 %collective-permute-start.43 = (bf16[128,768]{1,0:T(8,128)(2,1)}, bf16[128,768]{1,0:T(8,128)(2,1)}, u32[]{:S(2)}, u32[]{:S(2)}) collective-permute-start(bf16[128,768]{1,0:T(8,128)(2,1)} %add_convert_fusion.10), channel_id=1, source_target_pairs={{0,16},{4,20},{8,24},{12,28},{16,0},{20,4},{24,8},{28,12},{1,17},{... | collective-permute-start | bytes 589832 | tf_op jit(solution)/shard_map/ppermute | solution.py:65
  303.4 28.1 %collective-permute-start.50 = (bf16[96,768]{1,0:T(8,128)(2,1)}, bf16[96,768]{1,0:T(8,128)(2,1)S(1)}, u32[]{:S(2)}, u32[]{:S(2)}) collective-permute-start(bf16[96,768]{1,0:T(8,128)(2,1)} %copy-done.29), channel_id=1, source_target_pairs={{0,16},{4,20},{8,24},{12,28},{16,0},{20,4},{24,8},{28,12},{1,17},{... | collective-permute-start | bytes 442376 | tf_op jit(solution)/shard_map/ppermute | solution.py:65
  306.4 26.1 %collective-permute-start.51 = (bf16[96,768]{1,0:T(8,128)(2,1)}, bf16[96,768]{1,0:T(8,128)(2,1)S(1)}, u32[]{:S(2)}, u32[]{:S(2)}) collective-permute-start(bf16[96,768]{1,0:T(8,128)(2,1)} %copy-done.28), channel_id=1, source_target_pairs={{0,20},{4,16},{8,28},{12,24},{16,4},{20,0},{24,12},{28,8},{1,21},{... | collective-permute-start | bytes 442376 | tf_op jit(solution)/shard_map/ppermute | solution.py:65
  314.8 19.1 %collective-permute-start.52 = (bf16[96,768]{1,0:T(8,128)(2,1)S(1)}, bf16[96,768]{1,0:T(8,128)(2,1)S(1)}, u32[]{:S(2)}, u32[]{:S(2)}) collective-permute-start(bf16[96,768]{1,0:T(8,128)(2,1)S(1)} %copy-done.27), channel_id=1, source_target_pairs={{0,24},{4,28},{8,16},{12,20},{16,8},{20,12},{24,0},{28,4},{1,25},{... | collective-permute-start | bytes 442376 | tf_op jit(solution)/shard_map/ppermute | solution.py:65
  317.0 16.8 %collective-permute-start.53 = (bf16[96,768]{1,0:T(8,128)(2,1)S(1)}, bf16[96,768]{1,0:T(8,128)(2,1)S(1)}, u32[]{:S(2)}, u32[]{:S(2)}) collective-permute-start(bf16[96,768]{1,0:T(8,128)(2,1)S(1)} %get-tuple-element.169), channel_id=1, source_target_pairs={{0,28},{4,24},{8,20},{12,16},{16,12},{20,8},{24,4},{28,0},{1,29},{... | collective-permute-start | bytes 442376 | tf_op jit(solution)/shard_map/ppermute | solution.py:65
  331.5 18.5 %collective-permute-start.48 = (bf16[96,768]{1,0:T(8,128)(2,1)S(1)}, bf16[96,768]{1,0:T(8,128)(2,1)S(1)}, u32[]{:S(2)}, u32[]{:S(2)}) collective-permute-start(bf16[96,768]{1,0:T(8,128)(2,1)S(1)} %get-tuple-element.163), channel_id=1, source_target_pairs={{0,8},{4,12},{8,0},{12,4},{16,24},{20,28},{24,16},{28,20},{1,9},{5... | collective-permute-start | bytes 442376 | tf_op jit(solution)/shard_map/ppermute | solution.py:65
  332.5 18.9 %collective-permute-start.49 = (bf16[96,768]{1,0:T(8,128)(2,1)S(1)}, bf16[96,768]{1,0:T(8,128)(2,1)S(1)}, u32[]{:S(2)}, u32[]{:S(2)}) collective-permute-start(bf16[96,768]{1,0:T(8,128)(2,1)S(1)} %get-tuple-element.164), channel_id=1, source_target_pairs={{0,12},{4,8},{8,4},{12,0},{16,28},{20,24},{24,20},{28,16},{1,13},{... | collective-permute-start | bytes 442376 | tf_op jit(solution)/shard_map/ppermute | solution.py:65
  358.2 21.3 %collective-permute-start.58 = (bf16[2,512,768]{2,1,0:T(8,128)(2,1)S(1)}, bf16[2,512,768]{2,1,0:T(8,128)(2,1)S(1)}, u32[]{:S(2)}, u32[]{:S(2)}) collective-permute-start(bf16[2,512,768]{2,1,0:T(8,128)(2,1)S(1)} %grads_out.2), channel_id=1, source_target_pairs={{0,1},{1,0},{2,3},{3,2},{4,5},{5,4},{6,7},{7,6},{8,9},{9,8},{10,11... | collective-permute-start | bytes 4718600 | tf_op jit(solution)/shard_map/ppermute | solution.py:65
  385.2 20.4 %collective-permute-start.66 = (bf16[512,768]{1,0:T(8,128)(2,1)}, bf16[512,768]{1,0:T(8,128)(2,1)}, u32[]{:S(2)}, u32[]{:S(2)}) collective-permute-start(bf16[512,768]{1,0:T(8,128)(2,1)} %fusion.22), channel_id=1, source_target_pairs={{0,2},{1,3},{2,0},{3,1},{4,6},{5,7},{6,4},{7,5},{8,10},{9,11},{10,... | collective-permute-start | bytes 2359304 | tf_op jit(solution)/shard_map/ppermute | solution.py:65
  405.6 19.2 %collective-permute-start.67 = (bf16[2,2,192,2048]{3,2,1,0:T(8,128)(2,1)}, bf16[2,2,192,2048]{3,2,1,0:T(8,128)(2,1)}, u32[]{:S(2)}, u32[]{:S(2)}) collective-permute-start(bf16[2,2,192,2048]{3,2,1,0:T(8,128)(2,1)} %get-tuple-element.210), channel_id=1, source_target_pairs={{0,1},{1,0},{2,3},{3,2},{4,5},{5,4},{6,7},{7,6},{8,9},{9,8},{10,11... | collective-permute-start | bytes 9437192 | tf_op jit(solution)/shard_map/ppermute | solution.py:65
  423.4 25.6 %collective-permute-start.62 = (bf16[2,104,768]{2,1,0:T(8,128)(2,1)}, bf16[2,104,768]{2,1,0:T(8,128)(2,1)}, u32[]{:S(2)}, u32[]{:S(2)}) collective-permute-start(bf16[2,104,768]{2,1,0:T(8,128)(2,1)} %get-tuple-element.368), channel_id=1, source_target_pairs={{0,12},{4,8},{8,4},{12,0},{16,28},{20,24},{24,20},{28,16},{1,13},{... | collective-permute-start | bytes 958472 | tf_op jit(solution)/shard_map/ppermute | solution.py:65
  424.0 25.5 %collective-permute-start.63 = (bf16[2,104,768]{2,1,0:T(8,128)(2,1)}, bf16[2,104,768]{2,1,0:T(8,128)(2,1)}, u32[]{:S(2)}, u32[]{:S(2)}) collective-permute-start(bf16[2,104,768]{2,1,0:T(8,128)(2,1)} %get-tuple-element.367), channel_id=1, source_target_pairs={{0,4},{4,0},{8,12},{12,8},{16,20},{20,16},{24,28},{28,24},{1,5},{5... | collective-permute-start | bytes 958472 | tf_op jit(solution)/shard_map/ppermute | solution.py:65
  424.8 24.6 %collective-permute-start.64 = (bf16[2,104,768]{2,1,0:T(8,128)(2,1)}, bf16[2,104,768]{2,1,0:T(8,128)(2,1)}, u32[]{:S(2)}, u32[]{:S(2)}) collective-permute-start(bf16[2,104,768]{2,1,0:T(8,128)(2,1)} %get-tuple-element.366), channel_id=1, source_target_pairs={{0,8},{4,12},{8,0},{12,4},{16,24},{20,28},{24,16},{28,20},{1,9},{5... | collective-permute-start | bytes 958472 | tf_op jit(solution)/shard_map/ppermute | solution.py:65
  430.0 22.3 %collective-permute-start.65 = (bf16[2,104,768]{2,1,0:T(8,128)(2,1)}, bf16[2,104,768]{2,1,0:T(8,128)(2,1)}, u32[]{:S(2)}, u32[]{:S(2)}) collective-permute-start(bf16[2,104,768]{2,1,0:T(8,128)(2,1)} %get-tuple-element.365), channel_id=1, source_target_pairs={{0,12},{4,8},{8,4},{12,0},{16,28},{20,24},{24,20},{28,16},{1,13},{... | collective-permute-start | bytes 958472 | tf_op jit(solution)/shard_map/ppermute | solution.py:65
  434.6 20.2 %collective-permute-start.68 = (bf16[192,2048]{1,0:T(8,128)(2,1)}, bf16[192,2048]{1,0:T(8,128)(2,1)}, u32[]{:S(2)}, u32[]{:S(2)}) collective-permute-start(bf16[192,2048]{1,0:T(8,128)(2,1)} %get-tuple-element.364), channel_id=1, source_target_pairs={{0,2},{1,3},{2,0},{3,1},{4,6},{5,7},{6,4},{7,5},{8,10},{9,11},{10,... | collective-permute-start | bytes 2359304 | tf_op jit(solution)/shard_map/ppermute | solution.py:65
  449.0 19.7 %collective-permute-start.70 = (bf16[192,2048]{1,0:T(8,128)(2,1)S(1)}, bf16[192,2048]{1,0:T(8,128)(2,1)S(1)}, u32[]{:S(2)}, u32[]{:S(2)}) collective-permute-start(bf16[192,2048]{1,0:T(8,128)(2,1)S(1)} %copy-done.69), channel_id=1, source_target_pairs={{0,2},{1,3},{2,0},{3,1},{4,6},{5,7},{6,4},{7,5},{8,10},{9,11},{10,... | collective-permute-start | bytes 2359304 | tf_op jit(solution)/shard_map/ppermute | solution.py:65
  (180 other events, 1672.1 us)
Sparse Core Ops, SparseCore 0:
  11.7 33.6 all-gather.5
  47.5 47.3 all-gather.3
  97.1 82.0 all-gather.7
  289.9 99.0 reduce-scatter.1
